TPU v7x, 32 devices: a whole 2x2x4 slice. The times are simulated.
32 devices in a mesh: rep: 16 (over z, y, core), shard: 2 (over x).
Axes of the slice: x: 2, y: 2, z: 4, core: 2. Of those that a mesh axis runs over, the one named last changes fastest.
Arguments:
- tokens: bfloat16 [2, 4096, 768], P('shard', 'rep'), may hold values from -6 to 6
- doc_ids: int32 [2, 4096], P('shard'), may hold values from 0 to 1, never falling along the last dimension, each value on 1 to 4095 neighbouring positions
- qkv_weight: bfloat16 [768, 2304], P('shard'), may hold values from -0.21875 to 0.21875
- qv_bias: bfloat16 [1536], P('shard'), may hold values from -1.796875 to 1.796875
- out_weight: bfloat16 [768, 768], P('shard'), may hold values from -2.5 to 2.5
- out_bias: bfloat16 [768], P('shard'), may hold values from -1.796875 to 1.796875
- mid_gain: bfloat16 [768], P('shard'), may hold values from 0.5 to 1.5
- mid_shift: bfloat16 [768], P('shard'), may hold values from -1.796875 to 1.796875
- up_weight: bfloat16 [768, 3072], P('shard'), may hold values from -0.21875 to 0.21875
- up_bias: bfloat16 [3072], P('shard'), may hold values from -3 to 3
- down_weight: bfloat16 [3072, 768], P('shard'), may hold values from -0.109375 to 0.109375
- down_bias: bfloat16 [768], P('shard'), may hold values from -1.796875 to 1.796875
- end_gain: bfloat16 [768], P('shard'), may hold values from 0.5 to 1.5
- end_shift: bfloat16 [768], P('shard'), may hold values from -1.796875 to 1.796875
- out_grad: bfloat16 [2, 4096, 768], P('shard', 'rep'), may hold values from -6 to 6
Outputs:
- layer_out: bfloat16 [2, 4096, 768], P('shard', 'rep')
- input_grad: bfloat16 [2, 4096, 768], P('shard', 'rep')
- grad_qkv_weight: float32 [768, 2304], P('shard')
- grad_qv_bias: float32 [1536], P('shard')
- grad_out_weight: float32 [768, 768], P('shard')
- grad_out_bias: float32 [768], P('shard')
- grad_mid_gain: float32 [768], P('shard')
- grad_mid_shift: float32 [768], P('shard')
- grad_up_weight: float32 [768, 3072], P('shard')
- grad_up_bias: float32 [3072], P('shard')
- grad_down_weight: float32 [3072, 768], P('shard')
- grad_down_bias: float32 [768], P('shard')
- grad_end_gain: float32 [768], P('shard')
- grad_end_shift: float32 [768], P('shard')
Inputs may be any that keep to these rules, and one draw needn't show every extreme that they name: `doc_ids`: within a stream the document numbers never fall; each document has 1 to 4095 positions.
All inputs are finite; a program needn't handle non-finite values.
Results may differ from a plain program's by a relative error of at most 0.02.
Values may be sent and summed in bfloat16 or wider, within the bound.
A program may use at most 128 MiB of HBM per device.

v0:
```python
import math

import jax
import jax.numpy as jnp
from jax import lax
from jax.sharding import PartitionSpec as P

HEADS = 12
HEAD_DIM = 64
BLOCK = 256


EPSILON = 1e-05
NEGATIVE = -1e30
SCORE_ROWS = 512


def shifted(value, axis, by):
    length = lax.axis_size(axis)
    pairs = [(i, i + by) for i in range(length) if 0 <= i + by < length]
    return lax.ppermute(value, axis, pairs)


def visible(query_pos, query_docs, key_pos, key_docs):
    causal = key_pos[None, :] // BLOCK <= query_pos[:, None] // BLOCK
    return jnp.logical_and(causal[None], query_docs[:, :, None] == key_docs[:, None, :])


def layer_norm(hidden, gain, shift):
    centre = hidden - jnp.mean(hidden, axis=-1, keepdims=True)
    inverse = lax.rsqrt(jnp.mean(centre * centre, axis=-1, keepdims=True) + EPSILON)
    normed = centre * inverse
    return (normed * gain + shift, normed, inverse)


def norm_back(grad_output, normed, inverse, gain):
    grad_normed = grad_output * gain
    centred = grad_normed - jnp.mean(grad_normed, axis=-1, keepdims=True)
    return inverse * (centred - normed * jnp.mean(grad_normed * normed, axis=-1, keepdims=True))


def gelu_slope(value):
    return (
        0.5 * (1.0 + lax.erf(value * 0.7071067811865476))
        + value * jnp.exp(-0.5 * value * value) * 0.3989422804014327
    )


def unpack(weight_set):
    return tuple(
        (member.astype(jnp.float32) if member.ndim == 1 else member for member in weight_set)
    )


def token_sum(values_in):
    return jnp.sum(values_in.astype(jnp.float32), axis=(0, 1))


def flat_product(left, right):
    rows_all = left.shape[0] * left.shape[1]
    return jnp.dot(
        left.reshape(rows_all, left.shape[2]).T,
        right.reshape(rows_all, right.shape[2]),
        preferred_element_type=jnp.float32,
    )


def on_device(
    tokens,
    doc_ids,
    qkv_weight,
    qv_bias,
    out_weight,
    out_bias,
    mid_gain,
    mid_shift,
    up_weight,
    up_bias,
    down_weight,
    down_bias,
    end_gain,
    end_shift,
    out_grad,
):
    streams, local_rows, width = tokens.shape
    total_length = doc_ids.shape[1]
    scale = HEAD_DIM ** (-0.5)
    first = lax.axis_index("rep") * local_rows
    query_pos = first + jnp.arange(local_rows, dtype=jnp.int32)
    own_docs = lax.dynamic_slice_in_dim(doc_ids, first, local_rows, 1)
    shape_heads = (streams, local_rows, HEADS, HEAD_DIM)
    params = (
        qkv_weight,
        qv_bias,
        out_weight,
        out_bias,
        mid_gain,
        mid_shift,
        up_weight,
        up_bias,
        down_weight,
        down_bias,
        end_gain,
        end_shift,
    )
    forward_set = (
        lax.all_gather(params[0], "shard", axis=0, tiled=True),
        lax.all_gather(params[1], "shard", axis=0, tiled=True),
        lax.all_gather(params[2], "shard", axis=0, tiled=True),
        lax.all_gather(params[3], "shard", axis=0, tiled=True),
        lax.all_gather(params[4], "shard", axis=0, tiled=True),
        lax.all_gather(params[5], "shard", axis=0, tiled=True),
        lax.all_gather(params[6], "shard", axis=0, tiled=True),
        lax.all_gather(params[7], "shard", axis=0, tiled=True),
        lax.all_gather(params[8], "shard", axis=0, tiled=True),
        lax.all_gather(params[9], "shard", axis=0, tiled=True),
        lax.all_gather(params[10], "shard", axis=0, tiled=True),
        lax.all_gather(params[11], "shard", axis=0, tiled=True),
    )
    (
        full_qkv,
        vec_qv,
        full_out,
        vec_out,
        gain_mid,
        shift_mid,
        full_up,
        vec_up,
        full_down,
        vec_down,
        gain_end,
        shift_end,
    ) = unpack(forward_set)
    projected = jnp.dot(tokens, full_qkv, preferred_element_type=jnp.float32)
    queries = (projected[..., :width] + vec_qv[:width]).astype(jnp.bfloat16)
    keys = projected[..., width : 2 * width].astype(jnp.bfloat16)
    values = (projected[..., 2 * width :] + vec_qv[width:]).astype(jnp.bfloat16)
    query_heads = queries.reshape(shape_heads)
    key_heads = keys.reshape(shape_heads)
    value_heads = values.reshape(shape_heads)
    last_block = (first + local_rows - 1) // BLOCK
    key_limit = (last_block + 1) * BLOCK

    def visible_steps(count, size):
        needed = (key_limit + size - 1) // size
        return jnp.clip(needed, 0, count // size)

    row_zeros = jnp.zeros((streams, local_rows, HEADS), jnp.float32)
    head_zeros = jnp.zeros(shape_heads, jnp.float32)
    initial = (jnp.full((streams, local_rows, HEADS), NEGATIVE, jnp.float32), row_zeros, head_zeros)
    key_piece = lax.all_gather(keys, "rep", axis=1, tiled=True)
    value_piece = lax.all_gather(values, "rep", axis=1, tiled=True)
    count = key_piece.shape[1]
    size = math.gcd(count, SCORE_ROWS)

    def attend_step(block_no, state):
        top, total, sums = state
        offset = block_no * size
        key_block = lax.dynamic_slice_in_dim(key_piece, offset, size, 1).reshape(
            streams, size, HEADS, HEAD_DIM
        )
        value_block = lax.dynamic_slice_in_dim(value_piece, offset, size, 1).reshape(
            streams, size, HEADS, HEAD_DIM
        )
        key_pos = offset + jnp.arange(size, dtype=jnp.int32)
        key_docs = lax.dynamic_slice_in_dim(doc_ids, offset, size, 1)
        allow = visible(query_pos, own_docs, key_pos, key_docs)[:, :, None, :]
        score = (
            jnp.einsum(
                "sqhd,skhd->sqhk", query_heads, key_block, preferred_element_type=jnp.float32
            )
            * scale
        )
        score = jnp.where(allow, score, NEGATIVE)
        peak = jnp.maximum(top, jnp.max(score, axis=-1))
        probs = jnp.where(allow, jnp.exp(score - peak[..., None]), 0.0)
        shrink = jnp.exp(top - peak)
        total = total * shrink + jnp.sum(probs, axis=-1)
        sums = sums * shrink[..., None] + jnp.einsum(
            "sqhk,skhd->sqhd",
            probs.astype(jnp.bfloat16),
            value_block,
            preferred_element_type=jnp.float32,
        )
        return (peak, total, sums)

    top, total, sums = lax.fori_loop(0, visible_steps(count, size), attend_step, initial)
    attended = sums / total[..., None]
    log_total = top + jnp.log(total)
    attended_low = attended.reshape(streams, local_rows, width).astype(jnp.bfloat16)
    branch = jnp.dot(attended_low, full_out, preferred_element_type=jnp.float32) + vec_out
    mid_out, mid_norm, mid_inv = layer_norm(
        tokens.astype(jnp.float32) + branch, gain_mid, shift_mid
    )
    mid_low = mid_out.astype(jnp.bfloat16)
    pre_act = jnp.dot(mid_low, full_up, preferred_element_type=jnp.float32) + vec_up
    activated = jax.nn.gelu(pre_act, approximate=False).astype(jnp.bfloat16)
    ffn_out = jnp.dot(activated, full_down, preferred_element_type=jnp.float32) + vec_down
    end_out, end_norm, end_inv = layer_norm(mid_out + ffn_out, gain_end, shift_end)
    layer_out = end_out.astype(jnp.bfloat16)
    backward_set = unpack(
        (
            lax.all_gather(params[0], "shard", axis=0, tiled=True),
            lax.all_gather(params[1], "shard", axis=0, tiled=True),
            lax.all_gather(params[2], "shard", axis=0, tiled=True),
            lax.all_gather(params[3], "shard", axis=0, tiled=True),
            lax.all_gather(params[4], "shard", axis=0, tiled=True),
            lax.all_gather(params[5], "shard", axis=0, tiled=True),
            lax.all_gather(params[6], "shard", axis=0, tiled=True),
            lax.all_gather(params[7], "shard", axis=0, tiled=True),
            lax.all_gather(params[8], "shard", axis=0, tiled=True),
            lax.all_gather(params[9], "shard", axis=0, tiled=True),
            lax.all_gather(params[10], "shard", axis=0, tiled=True),
            lax.all_gather(params[11], "shard", axis=0, tiled=True),
        )
    )
    back_qkv = backward_set[0]
    back_out = backward_set[2]
    back_gain_mid = backward_set[4]
    back_up = backward_set[6]
    back_down = backward_set[8]
    back_gain_end = backward_set[10]
    grad_top = out_grad.astype(jnp.float32)
    grad_end_gain = jnp.sum(grad_top * end_norm, axis=(0, 1))
    grad_end_shift = jnp.sum(grad_top, axis=(0, 1))
    grad_end_in = norm_back(grad_top, end_norm, end_inv, back_gain_end)
    grad_ffn = grad_end_in.astype(jnp.bfloat16)
    grad_down_bias = token_sum(grad_ffn)
    grad_down_weight = flat_product(activated, grad_ffn)
    grad_act = jnp.einsum("scd,fd->scf", grad_ffn, back_down, preferred_element_type=jnp.float32)
    grad_pre = (grad_act * gelu_slope(pre_act)).astype(jnp.bfloat16)
    grad_up_bias = token_sum(grad_pre)
    grad_up_weight = flat_product(mid_low, grad_pre)
    grad_mid_out = (
        jnp.einsum("scf,df->scd", grad_pre, back_up, preferred_element_type=jnp.float32)
        + grad_end_in
    )
    grad_mid_gain = jnp.sum(grad_mid_out * mid_norm, axis=(0, 1))
    grad_mid_shift = jnp.sum(grad_mid_out, axis=(0, 1))
    grad_mid_in = norm_back(grad_mid_out, mid_norm, mid_inv, back_gain_mid)
    grad_branch = grad_mid_in.astype(jnp.bfloat16)
    grad_out_bias = token_sum(grad_branch)
    grad_out_weight = flat_product(attended_low, grad_branch)
    grad_attended = jnp.einsum(
        "scd,ed->sce", grad_branch, back_out, preferred_element_type=jnp.float32
    ).astype(jnp.bfloat16)
    grad_heads = grad_attended.reshape(shape_heads)
    delta = jnp.sum(grad_heads.astype(jnp.float32) * attended, axis=-1)
    query_key_piece = lax.all_gather(keys, "rep", axis=1, tiled=True)
    query_value_piece = lax.all_gather(values, "rep", axis=1, tiled=True)
    count = query_key_piece.shape[1]
    query_size = math.gcd(count, SCORE_ROWS)

    def query_step(block_no, state):
        offset = block_no * query_size
        key_block = lax.dynamic_slice_in_dim(query_key_piece, offset, query_size, 1).reshape(
            streams, query_size, HEADS, HEAD_DIM
        )
        value_block = lax.dynamic_slice_in_dim(query_value_piece, offset, query_size, 1).reshape(
            streams, query_size, HEADS, HEAD_DIM
        )
        key_pos = offset + jnp.arange(query_size, dtype=jnp.int32)
        key_docs = lax.dynamic_slice_in_dim(doc_ids, offset, query_size, 1)
        allow = visible(query_pos, own_docs, key_pos, key_docs)[:, :, None, :]
        score = (
            jnp.einsum(
                "sqhd,skhd->sqhk", query_heads, key_block, preferred_element_type=jnp.float32
            )
            * scale
        )
        probs = jnp.where(
            allow, jnp.exp(jnp.where(allow, score, NEGATIVE) - log_total[..., None]), 0.0
        )
        grad_prob = jnp.einsum(
            "sqhd,skhd->sqhk", grad_heads, value_block, preferred_element_type=jnp.float32
        )
        grad_score = (probs * (grad_prob - delta[..., None])).astype(jnp.bfloat16)
        return state + jnp.einsum(
            "sqhk,skhd->sqhd", grad_score, key_block, preferred_element_type=jnp.float32
        )

    grad_query_sum = lax.fori_loop(0, visible_steps(count, query_size), query_step, head_zeros)

    def keys_back(carry, piece, stats, start):
        query_piece, grad_piece = piece
        lse_piece, delta_piece = stats
        count = query_piece.shape[1]
        size = math.gcd(count, SCORE_ROWS)

        def keys_step(block_no, state):
            grad_key, grad_value = state
            offset = block_no * size
            query_block = query_piece.reshape(streams, size, HEADS, HEAD_DIM)
            grad_block = grad_piece.reshape(streams, size, HEADS, HEAD_DIM)
            block_pos = start + offset + jnp.arange(size, dtype=jnp.int32)
            block_docs = lax.dynamic_slice_in_dim(doc_ids, start + offset, size, 1)
            allow = visible(block_pos, block_docs, query_pos, own_docs)[:, :, None, :]
            score = (
                jnp.einsum(
                    "sqhd,skhd->sqhk", query_block, key_heads, preferred_element_type=jnp.float32
                )
                * scale
            )
            probs = jnp.where(
                allow, jnp.exp(jnp.where(allow, score, NEGATIVE) - lse_piece[..., None]), 0.0
            )
            grad_value = grad_value + jnp.einsum(
                "sqhk,sqhd->skhd",
                probs.astype(jnp.bfloat16),
                grad_block,
                preferred_element_type=jnp.float32,
            )
            grad_prob = jnp.einsum(
                "sqhd,skhd->sqhk", grad_block, value_heads, preferred_element_type=jnp.float32
            )
            grad_score = (probs * (grad_prob - delta_piece[..., None])).astype(jnp.bfloat16)
            grad_key = grad_key + jnp.einsum(
                "sqhk,sqhd->skhd", grad_score, query_block, preferred_element_type=jnp.float32
            )
            return (grad_key, grad_value)

        return lax.fori_loop(0, count // size, keys_step, carry)

    own_piece = (queries, grad_attended)
    own_stats = (log_total, delta)
    start_carry = keys_back((head_zeros, head_zeros), own_piece, own_stats, first)

    def pass_step(distance, state):
        carry, moving, moving_stats = state
        moving = shifted((moving[0], moving[1]), "rep", -1)
        moving_stats = shifted((moving_stats[0], moving_stats[1]), "rep", -1)
        start = first + distance * local_rows

        def use_piece(inner):
            return keys_back(inner, moving, moving_stats, start)

        carry = lax.cond(start < total_length, use_piece, lambda inner: inner, carry)
        return (carry, moving, moving_stats)

    (grad_key_sum, grad_value_sum), moved_last, stats_last = lax.fori_loop(
        1, lax.axis_size("rep"), pass_step, (start_carry, own_piece, own_stats)
    )
    grad_queries = (grad_query_sum * scale).reshape(streams, local_rows, width).astype(jnp.bfloat16)
    grad_keys = (grad_key_sum * scale).reshape(streams, local_rows, width).astype(jnp.bfloat16)
    grad_values = grad_value_sum.reshape(streams, local_rows, width).astype(jnp.bfloat16)
    grad_proj = jnp.concatenate([grad_queries, grad_keys, grad_values], axis=-1)
    grad_qv_bias = jnp.concatenate([token_sum(grad_queries), token_sum(grad_values)], axis=0)
    grad_qkv_weight = flat_product(tokens, grad_proj)
    input_grad = (
        jnp.einsum("sce,de->scd", grad_proj, back_qkv, preferred_element_type=jnp.float32)
        + grad_mid_in
    ).astype(jnp.bfloat16)
    local_grads = (
        grad_qkv_weight,
        grad_qv_bias,
        grad_out_weight,
        grad_out_bias,
        grad_mid_gain,
        grad_mid_shift,
        grad_up_weight,
        grad_up_bias,
        grad_down_weight,
        grad_down_bias,
        grad_end_gain,
        grad_end_shift,
    )
    group_parts = (
        lax.psum_scatter(
            local_grads[0].astype(jnp.bfloat16), "shard", scatter_dimension=0, tiled=True
        ).astype(jnp.float32),
        lax.psum_scatter(
            local_grads[1].astype(jnp.bfloat16), "shard", scatter_dimension=0, tiled=True
        ).astype(jnp.float32),
        lax.psum_scatter(
            local_grads[2].astype(jnp.bfloat16), "shard", scatter_dimension=0, tiled=True
        ).astype(jnp.float32),
        lax.psum_scatter(
            local_grads[3].astype(jnp.bfloat16), "shard", scatter_dimension=0, tiled=True
        ).astype(jnp.float32),
        lax.psum_scatter(
            local_grads[4].astype(jnp.bfloat16), "shard", scatter_dimension=0, tiled=True
        ).astype(jnp.float32),
        lax.psum_scatter(
            local_grads[5].astype(jnp.bfloat16), "shard", scatter_dimension=0, tiled=True
        ).astype(jnp.float32),
        lax.psum_scatter(
            local_grads[6].astype(jnp.bfloat16), "shard", scatter_dimension=0, tiled=True
        ).astype(jnp.float32),
        lax.psum_scatter(
            local_grads[7].astype(jnp.bfloat16), "shard", scatter_dimension=0, tiled=True
        ).astype(jnp.float32),
        lax.psum_scatter(
            local_grads[8].astype(jnp.bfloat16), "shard", scatter_dimension=0, tiled=True
        ).astype(jnp.float32),
        lax.psum_scatter(
            local_grads[9].astype(jnp.bfloat16), "shard", scatter_dimension=0, tiled=True
        ).astype(jnp.float32),
        lax.psum_scatter(
            local_grads[10].astype(jnp.bfloat16), "shard", scatter_dimension=0, tiled=True
        ).astype(jnp.float32),
        lax.psum_scatter(
            local_grads[11].astype(jnp.bfloat16), "shard", scatter_dimension=0, tiled=True
        ).astype(jnp.float32),
    )
    totals = (
        lax.psum(group_parts[0].astype(jnp.bfloat16), "rep").astype(jnp.float32),
        lax.psum(group_parts[1].astype(jnp.bfloat16), "rep").astype(jnp.float32),
        lax.psum(group_parts[2].astype(jnp.bfloat16), "rep").astype(jnp.float32),
        lax.psum(group_parts[3].astype(jnp.bfloat16), "rep").astype(jnp.float32),
        lax.psum(group_parts[4].astype(jnp.bfloat16), "rep").astype(jnp.float32),
        lax.psum(group_parts[5].astype(jnp.bfloat16), "rep").astype(jnp.float32),
        lax.psum(group_parts[6].astype(jnp.bfloat16), "rep").astype(jnp.float32),
        lax.psum(group_parts[7].astype(jnp.bfloat16), "rep").astype(jnp.float32),
        lax.psum(group_parts[8].astype(jnp.bfloat16), "rep").astype(jnp.float32),
        lax.psum(group_parts[9].astype(jnp.bfloat16), "rep").astype(jnp.float32),
        lax.psum(group_parts[10].astype(jnp.bfloat16), "rep").astype(jnp.float32),
        lax.psum(group_parts[11].astype(jnp.bfloat16), "rep").astype(jnp.float32),
    )
    return (
        layer_out,
        input_grad,
        totals[0],
        totals[1],
        totals[2],
        totals[3],
        totals[4],
        totals[5],
        totals[6],
        totals[7],
        totals[8],
        totals[9],
        totals[10],
        totals[11],
    )


def solution(mesh):
    in_specs = (
        P("shard", "rep", None),
        P("shard", None),
        P("shard", None),
        P("shard"),
        P("shard", None),
        P("shard"),
        P("shard"),
        P("shard"),
        P("shard", None),
        P("shard"),
        P("shard", None),
        P("shard"),
        P("shard"),
        P("shard"),
        P("shard", "rep", None),
    )
    out_specs = (
        P("shard", "rep", None),
        P("shard", "rep", None),
        P("shard", None),
        P("shard"),
        P("shard", None),
        P("shard"),
        P("shard"),
        P("shard"),
        P("shard", None),
        P("shard"),
        P("shard", None),
        P("shard"),
        P("shard"),
        P("shard"),
    )
    return jax.shard_map(
        on_device, mesh=mesh, in_specs=in_specs, out_specs=out_specs, check_vma=False
    )
```

profile of v0, /device:TPU:1, one launch (start us, length us, event | category | flops | bytes accessed | tf_op | source)
XLA Modules:
  0.0 1234.0 jit_solution(6617288034165262786)
XLA Ops:
  12.4 48.6 %all-gather.15.cloned.1.call-done = bf16[768,2304]{1,0:T(8,128)(2,1)} async-done(((bf16[384,2304]{1,0:T(8,128)(2,1)}), bf16[768,2304]{1,0:T(8,128)(2,1)}) %all-gather.15.cloned.1.call-update) | async-done | bytes 3538960 | tf_op jit(solution)/shard_map/all_gather | solution.py:107
  97.6 30.0 %all-gather.19.cloned.1.call-done = bf16[1,4096,768]{2,1,0:T(8,128)(2,1)} async-done(((bf16[1,256,768]{2,1,0:T(8,128)(2,1)}), bf16[1,4096,768]{2,1,0:T(8,128)(2,1)}) %all-gather.19.cloned.1.call-update) | async-done | bytes 6291472 | tf_op jit(solution)/shard_map/all_gather | solution.py:152
  127.6 8.7 copy.81
  136.3 54.6 %all-gather.17.cloned.1.call-done = bf16[1,4096,768]{2,1,0:T(8,128)(2,1)} async-done(((bf16[1,256,768]{2,1,0:T(8,128)(2,1)}), bf16[1,4096,768]{2,1,0:T(8,128)(2,1)}) %all-gather.17.cloned.1.call-update) | async-done | bytes 6291472 | tf_op jit(solution)/shard_map/all_gather | solution.py:151
  190.9 8.6 copy.80
  199.7 7.7 while.71
  207.5 5.8 all-gather.21.cloned.1.call-done
  215.4 61.9 %all-gather.23.cloned.1.call-done = bf16[768,3072]{1,0:T(8,128)(2,1)} async-done(((bf16[384,3072]{1,0:T(8,128)(2,1)}), bf16[768,3072]{1,0:T(8,128)(2,1)}) %all-gather.23.cloned.1.call-update) | async-done | bytes 4718608 | tf_op jit(solution)/shard_map/all_gather | solution.py:113
  277.4 22.1 %fusion.103 = (bf16[256,3072]{1,0:T(8,128)(2,1)}, f32[256,3072]{1,0:T(8,128)}) fusion(f32[3072]{0:T(1024)S(1)} %bitcast.452, bf16[768,3072]{1,0:T(8,128)(2,1)} %all-gather.23.cloned.1.call-done, f32[1,256,768]{2,1,0:T(8,128)S(1)} %get-tuple-element.1222, f32[768]{0:T(1024)S(1)} %reshape.1218, f32[768]{0:T(1024)S(1)} %reshape.1217, ...), kind=kOutput, calls=%fused_computation.135 | convolution fusion | flops 1260847104 | bytes 10244096 | tf_op jit(solution)/shard_map/dot_general | solution.py:196
  299.5 42.0 %all-gather.25.cloned.1.call-done = bf16[3072,768]{1,0:T(8,128)(2,1)} async-done(((bf16[1536,768]{1,0:T(8,128)(2,1)}), bf16[3072,768]{1,0:T(8,128)(2,1)}) %all-gather.25.cloned.1.call-update) | async-done | bytes 4718608 | tf_op jit(solution)/shard_map/all_gather | solution.py:115
  341.5 4.5 fusion.176
  362.7 4.5 fusion.127
  368.2 12.4 %while.72 = (s32[]{:T(128)}, f32[1,256,12,64]{1,3,2,0:T(8,128)S(1)}, s32[]{:T(128)}, bf16[1,4096,768]{1,2,0:T(8,128)(2,1)}, s32[1,256]{1,0:T(1,128)}, /*index=5*...) while((s32[]{:T(128)}, ...), condition=%wide.region_14.15_spmd.clone.clone, body=%wide.region_13.14_spmd.clone.clone.sunk | while | flops 615592448 | bytes 20750044 | solution.py:282
  374.9 5.5 fusion.241
  381.5 468.2 %while.73 = (s32[]{:T(128)}, f32[1,256,12,64]{1,3,2,0:T(8,128)}, f32[1,256,12,64]{1,3,2,0:T(8,128)}, bf16[1,256,768]{1,2,0:T(8,128)(2,1)S(1)}, bf16[1,256,768]{1...) while((s32[]{:T(128)}, f32[1,256,12,64]{1,3,2,0:T(8,128)}, ...), condition=%wide.region_18.19_spmd.clone.clone, body=%wide.region_15.18_spmd.clone.clone.sunk | while | flops 412688384 | bytes 20101676 | solution.py:340
  389.8 17.4 %collective-permute-done.1 = f32[1,256,12]{1,2,0:T(8,128)S(1)} collective-permute-done((f32[1,256,12]{1,2,0:T(8,128)}, f32[1,256,12]{1,2,0:T(8,128)S(1)}, u32[]{:S(2)}, u32[]{:S(2)}) %collective-permute-start.1) | collective-permute-done | bytes 12320 | tf_op jit(solution)/shard_map/while/body/eval_jaxpr/ppermute | solution.py:21
  408.4 11.0 conditional.4
  429.9 5.8 collective-permute-done.1
  436.9 11.0 conditional.4
  458.3 12.3 collective-permute-done.1
  471.9 11.0 conditional.4
  475.7 4.0 fusion.35
  493.3 6.7 collective-permute-done.1
  501.2 11.0 conditional.4
  505.1 4.0 fusion.35
  522.7 11.5 collective-permute-done.1
  535.3 11.0 conditional.4
  539.2 4.0 fusion.35
  556.8 6.7 collective-permute-done.1
  564.7 11.0 conditional.4
  568.5 4.0 fusion.35
  586.1 11.4 collective-permute-done.1
  598.8 11.0 conditional.4
  602.6 4.0 fusion.35
  620.2 6.7 collective-permute-done.1
  628.1 11.0 conditional.4
  632.0 4.0 fusion.35
  649.6 11.5 collective-permute-done.1
  662.2 11.0 conditional.4
  666.1 4.0 fusion.35
  683.7 6.7 collective-permute-done.1
  691.6 11.0 conditional.4
  695.4 4.0 fusion.35
  713.0 11.4 collective-permute-done.1
  725.7 11.0 conditional.4
  729.6 4.0 fusion.35
  747.1 6.7 collective-permute-done.1
  755.0 11.0 conditional.4
  758.9 4.0 fusion.35
  776.5 11.4 collective-permute-done.1
  789.1 11.0 conditional.4
  793.0 4.0 fusion.35
  810.6 6.6 collective-permute-done.1
  818.5 11.0 conditional.4
  839.9 5.8 collective-permute-done.1
  862.0 4.4 convolution_convert_fusion.1
  872.4 36.2 %reduce-scatter.13.cloned.1.call-done = bf16[384,2304]{1,0:T(8,128)(2,1)} async-done(((bf16[768,2304]{1,0:T(8,128)(2,1)}), bf16[384,2304]{1,0:T(8,128)(2,1)}) %reduce-scatter.13.cloned.1.call-update) | async-done | bytes 1769488
  912.5 20.9 %reduce-scatter.7.cloned.1.call-done = bf16[384,768]{1,0:T(8,128)(2,1)} async-done(((bf16[768,768]{1,0:T(8,128)(2,1)}), bf16[384,768]{1,0:T(8,128)(2,1)}) %reduce-scatter.7.cloned.1.call-update) | async-done | bytes 589840 | tf_op jit(solution)/shard_map/reduce_scatter | solution.py:374
  933.3 62.9 %reduce-scatter.9.cloned.1.call-done = bf16[384,3072]{1,0:T(8,128)(2,1)} async-done(((bf16[768,3072]{1,0:T(8,128)(2,1)}), bf16[384,3072]{1,0:T(8,128)(2,1)}) %reduce-scatter.9.cloned.1.call-update) | async-done | bytes 2359312 | tf_op jit(solution)/shard_map/reduce_scatter | solution.py:386
  996.2 62.9 %reduce-scatter.11.cloned.1.call-done = bf16[1536,768]{1,0:T(8,128)(2,1)} async-done(((bf16[3072,768]{1,0:T(8,128)(2,1)}), bf16[1536,768]{1,0:T(8,128)(2,1)}) %reduce-scatter.11.cloned.1.call-update) | async-done | bytes 2359312 | tf_op jit(solution)/shard_map/reduce_scatter | solution.py:392
  1062.5 5.4 all-reduce.10
  1068.5 60.2 %all-reduce.8 = (bf16[768]{0:T(1024)(128)(2,1)S(1)}, bf16[384]{0:T(512)(128)(2,1)S(1)}, bf16[384]{0:T(512)(128)(2,1)S(1)}, bf16[384]{0:T(512)(128)(2,1)S(1)}, bf...) all-reduce(bf16[768]{0:T(1024)(128)(2,1)S(1)} %dynamic-slice.1, ...), channel_id=1, replica_groups=mesh['rep'=16,'shard'=2] {'rep'}, use_global_device_ids=true, to_apply=%region_24.25 | all-reduce | flops 4608 | bytes 18432 | tf_op jit(solution)/shard_map/psum | solution.py:407
  1137.3 78.7 %all-reduce.13.cloned.1.call-done = (bf16[384,2304]{0,1:T(8,128)(2,1)}, bf16[384,768]{1,0:T(8,128)(2,1)}, bf16[384,3072]{1,0:T(8,128)(2,1)}, bf16[1536,768]{1,0:T(8,128)(2,1)}) async-done(((bf16[384,2304]{0,1:T(8,128)(2,1)}, bf16[384,768]{1,0:T(8,128)(2,1)}, bf16[384,3072]{1,0:T(8,128)(2,1)}, bf16[1536,768]{1,0:T(8,128)(2,1)}), (bf16[384,2304]{0,1:T(8,128)(2,1)}, bf16[384,768]{1,0:T(8,128)(2,1)}, ...) | async-done | bytes 7077904 | tf_op jit(solution)/shard_map/psum | solution.py:406
  1216.1 4.6 convert_element_type.323
  (538 shorter events, 399.8 us)
Async XLA Ops:
  7.2 53.9 %all-gather.15.cloned.1.call-start = ((), (), s32[]{:S(2)}) async-start(), calls=%async_computation.4 | async-start | bytes 5308416 | tf_op jit(solution)/shard_map/all_gather | solution.py:107
  7.9 119.7 %all-gather.19.cloned.1.call-start = ((), (), s32[]{:S(2)}) async-start(), calls=%async_computation.6 | async-start | bytes 6684672 | tf_op jit(solution)/shard_map/all_gather | solution.py:152
  65.2 125.7 %all-gather.17.cloned.1.call-start = ((), (), s32[]{:S(2)}) async-start(), calls=%async_computation.5 | async-start | bytes 6684672 | tf_op jit(solution)/shard_map/all_gather | solution.py:151
  66.1 147.2 %all-gather.21.cloned.1.call-start = ((), (), s32[]{:S(2)}) async-start(), calls=%async_computation.7 | async-start | bytes 1769472 | tf_op jit(solution)/shard_map/all_gather | solution.py:109
  66.7 210.7 %all-gather.23.cloned.1.call-start = ((), (), s32[]{:S(2)}) async-start(), calls=%async_computation.8 | async-start | bytes 7077888 | tf_op jit(solution)/shard_map/all_gather | solution.py:113
  67.2 274.2 %all-gather.25.cloned.1.call-start = ((), (), s32[]{:S(2)}) async-start(), calls=%async_computation.9 | async-start | bytes 7077888 | tf_op jit(solution)/shard_map/all_gather | solution.py:115
  67.8 840.8 %reduce-scatter.13.cloned.1.call-start = ((), (), s32[]{:S(2)}) async-start(), calls=%async_computation.13 | async-start | bytes 5308416
  381.5 26.9 %collective-permute-start = (bf16[1,256,768]{1,2,0:T(8,128)(2,1)S(1)}, bf16[1,256,768]{1,2,0:T(8,128)(2,1)}, u32[]{:S(2)}, u32[]{:S(2)}) collective-permute-start(bf16[1,256,768]{1,2,0:T(8,128)(2,1)S(1)} %get-tuple-element.1582), channel_id=1, source_target_pairs={{2,0},{4,2},{6,4},{8,6},{10,8},{12,10},{14,12},{16,14},{18,16},{20... | collective-permute-start | bytes 1179656 | tf_op jit(solution)/shard_map/while/body/eval_jaxpr/ppermute | solution.py:21
  384.1 24.4 %collective-permute-start.2 = (bf16[1,256,768]{1,2,0:T(8,128)(2,1)}, bf16[1,256,768]{1,2,0:T(8,128)(2,1)}, u32[]{:S(2)}, u32[]{:S(2)}) collective-permute-start(bf16[1,256,768]{1,2,0:T(8,128)(2,1)} %get-tuple-element.1583), channel_id=1, source_target_pairs={{2,0},{4,2},{6,4},{8,6},{10,8},{12,10},{14,12},{16,14},{18,16},{20... | collective-permute-start | bytes 1179656 | tf_op jit(solution)/shard_map/while/body/eval_jaxpr/ppermute | solution.py:21
  386.0 21.2 %collective-permute-start.1 = (f32[1,256,12]{1,2,0:T(8,128)}, f32[1,256,12]{1,2,0:T(8,128)S(1)}, u32[]{:S(2)}, u32[]{:S(2)}) collective-permute-start(f32[1,256,12]{1,2,0:T(8,128)} %get-tuple-element.1584), channel_id=1, source_target_pairs={{2,0},{4,2},{6,4},{8,6},{10,8},{12,10},{14,12},{16,14},{18,16},{20... | collective-permute-start | bytes 36872 | tf_op jit(solution)/shard_map/while/body/eval_jaxpr/ppermute | solution.py:21
  387.9 19.9 %collective-permute-start.3 = (f32[1,256,12]{1,2,0:T(8,128)}, f32[1,256,12]{1,2,0:T(8,128)S(1)}, u32[]{:S(2)}, u32[]{:S(2)}) collective-permute-start(f32[1,256,12]{1,2,0:T(8,128)} %get-tuple-element.1585), channel_id=1, source_target_pairs={{2,0},{4,2},{6,4},{8,6},{10,8},{12,10},{14,12},{16,14},{18,16},{20... | collective-permute-start | bytes 36872 | tf_op jit(solution)/shard_map/while/body/eval_jaxpr/ppermute | solution.py:21
  422.2 14.7 %collective-permute-start = (bf16[1,256,768]{1,2,0:T(8,128)(2,1)S(1)}, bf16[1,256,768]{1,2,0:T(8,128)(2,1)}, u32[]{:S(2)}, u32[]{:S(2)}) collective-permute-start(bf16[1,256,768]{1,2,0:T(8,128)(2,1)S(1)} %get-tuple-element.1582), channel_id=1, source_target_pairs={{2,0},{4,2},{6,4},{8,6},{10,8},{12,10},{14,12},{16,14},{18,16},{20... | collective-permute-start | bytes 1179656 | tf_op jit(solution)/shard_map/while/body/eval_jaxpr/ppermute | solution.py:21
  424.1 12.8 %collective-permute-start.2 = (bf16[1,256,768]{1,2,0:T(8,128)(2,1)}, bf16[1,256,768]{1,2,0:T(8,128)(2,1)}, u32[]{:S(2)}, u32[]{:S(2)}) collective-permute-start(bf16[1,256,768]{1,2,0:T(8,128)(2,1)} %get-tuple-element.1583), channel_id=1, source_target_pairs={{2,0},{4,2},{6,4},{8,6},{10,8},{12,10},{14,12},{16,14},{18,16},{20... | collective-permute-start | bytes 1179656 | tf_op jit(solution)/shard_map/while/body/eval_jaxpr/ppermute | solution.py:21
  426.0 9.6 collective-permute-start.1
  450.6 21.3 %collective-permute-start = (bf16[1,256,768]{1,2,0:T(8,128)(2,1)S(1)}, bf16[1,256,768]{1,2,0:T(8,128)(2,1)}, u32[]{:S(2)}, u32[]{:S(2)}) collective-permute-start(bf16[1,256,768]{1,2,0:T(8,128)(2,1)S(1)} %get-tuple-element.1582), channel_id=1, source_target_pairs={{2,0},{4,2},{6,4},{8,6},{10,8},{12,10},{14,12},{16,14},{18,16},{20... | collective-permute-start | bytes 1179656 | tf_op jit(solution)/shard_map/while/body/eval_jaxpr/ppermute | solution.py:21
  452.5 19.3 %collective-permute-start.2 = (bf16[1,256,768]{1,2,0:T(8,128)(2,1)}, bf16[1,256,768]{1,2,0:T(8,128)(2,1)}, u32[]{:S(2)}, u32[]{:S(2)}) collective-permute-start(bf16[1,256,768]{1,2,0:T(8,128)(2,1)} %get-tuple-element.1583), channel_id=1, source_target_pairs={{2,0},{4,2},{6,4},{8,6},{10,8},{12,10},{14,12},{16,14},{18,16},{20... | collective-permute-start | bytes 1179656 | tf_op jit(solution)/shard_map/while/body/eval_jaxpr/ppermute | solution.py:21
  454.5 16.2 %collective-permute-start.1 = (f32[1,256,12]{1,2,0:T(8,128)}, f32[1,256,12]{1,2,0:T(8,128)S(1)}, u32[]{:S(2)}, u32[]{:S(2)}) collective-permute-start(f32[1,256,12]{1,2,0:T(8,128)} %get-tuple-element.1584), channel_id=1, source_target_pairs={{2,0},{4,2},{6,4},{8,6},{10,8},{12,10},{14,12},{16,14},{18,16},{20... | collective-permute-start | bytes 36872 | tf_op jit(solution)/shard_map/while/body/eval_jaxpr/ppermute | solution.py:21
  456.4 14.9 %collective-permute-start.3 = (f32[1,256,12]{1,2,0:T(8,128)}, f32[1,256,12]{1,2,0:T(8,128)S(1)}, u32[]{:S(2)}, u32[]{:S(2)}) collective-permute-start(f32[1,256,12]{1,2,0:T(8,128)} %get-tuple-element.1585), channel_id=1, source_target_pairs={{2,0},{4,2},{6,4},{8,6},{10,8},{12,10},{14,12},{16,14},{18,16},{20... | collective-permute-start | bytes 36872 | tf_op jit(solution)/shard_map/while/body/eval_jaxpr/ppermute | solution.py:21
  485.6 15.6 %collective-permute-start = (bf16[1,256,768]{1,2,0:T(8,128)(2,1)S(1)}, bf16[1,256,768]{1,2,0:T(8,128)(2,1)}, u32[]{:S(2)}, u32[]{:S(2)}) collective-permute-start(bf16[1,256,768]{1,2,0:T(8,128)(2,1)S(1)} %get-tuple-element.1582), channel_id=1, source_target_pairs={{2,0},{4,2},{6,4},{8,6},{10,8},{12,10},{14,12},{16,14},{18,16},{20... | collective-permute-start | bytes 1179656 | tf_op jit(solution)/shard_map/while/body/eval_jaxpr/ppermute | solution.py:21
  487.5 13.7 %collective-permute-start.2 = (bf16[1,256,768]{1,2,0:T(8,128)(2,1)}, bf16[1,256,768]{1,2,0:T(8,128)(2,1)}, u32[]{:S(2)}, u32[]{:S(2)}) collective-permute-start(bf16[1,256,768]{1,2,0:T(8,128)(2,1)} %get-tuple-element.1583), channel_id=1, source_target_pairs={{2,0},{4,2},{6,4},{8,6},{10,8},{12,10},{14,12},{16,14},{18,16},{20... | collective-permute-start | bytes 1179656 | tf_op jit(solution)/shard_map/while/body/eval_jaxpr/ppermute | solution.py:21
  489.5 10.5 collective-permute-start.1
  491.4 9.2 collective-permute-start.3
  514.9 20.4 %collective-permute-start = (bf16[1,256,768]{1,2,0:T(8,128)(2,1)S(1)}, bf16[1,256,768]{1,2,0:T(8,128)(2,1)}, u32[]{:S(2)}, u32[]{:S(2)}) collective-permute-start(bf16[1,256,768]{1,2,0:T(8,128)(2,1)S(1)} %get-tuple-element.1582), channel_id=1, source_target_pairs={{2,0},{4,2},{6,4},{8,6},{10,8},{12,10},{14,12},{16,14},{18,16},{20... | collective-permute-start | bytes 1179656 | tf_op jit(solution)/shard_map/while/body/eval_jaxpr/ppermute | solution.py:21
  516.9 18.5 %collective-permute-start.2 = (bf16[1,256,768]{1,2,0:T(8,128)(2,1)}, bf16[1,256,768]{1,2,0:T(8,128)(2,1)}, u32[]{:S(2)}, u32[]{:S(2)}) collective-permute-start(bf16[1,256,768]{1,2,0:T(8,128)(2,1)} %get-tuple-element.1583), channel_id=1, source_target_pairs={{2,0},{4,2},{6,4},{8,6},{10,8},{12,10},{14,12},{16,14},{18,16},{20... | collective-permute-start | bytes 1179656 | tf_op jit(solution)/shard_map/while/body/eval_jaxpr/ppermute | solution.py:21
  518.8 15.3 %collective-permute-start.1 = (f32[1,256,12]{1,2,0:T(8,128)}, f32[1,256,12]{1,2,0:T(8,128)S(1)}, u32[]{:S(2)}, u32[]{:S(2)}) collective-permute-start(f32[1,256,12]{1,2,0:T(8,128)} %get-tuple-element.1584), channel_id=1, source_target_pairs={{2,0},{4,2},{6,4},{8,6},{10,8},{12,10},{14,12},{16,14},{18,16},{20... | collective-permute-start | bytes 36872 | tf_op jit(solution)/shard_map/while/body/eval_jaxpr/ppermute | solution.py:21
  520.7 14.0 %collective-permute-start.3 = (f32[1,256,12]{1,2,0:T(8,128)}, f32[1,256,12]{1,2,0:T(8,128)S(1)}, u32[]{:S(2)}, u32[]{:S(2)}) collective-permute-start(f32[1,256,12]{1,2,0:T(8,128)} %get-tuple-element.1585), channel_id=1, source_target_pairs={{2,0},{4,2},{6,4},{8,6},{10,8},{12,10},{14,12},{16,14},{18,16},{20... | collective-permute-start | bytes 36872 | tf_op jit(solution)/shard_map/while/body/eval_jaxpr/ppermute | solution.py:21
  549.1 15.6 %collective-permute-start = (bf16[1,256,768]{1,2,0:T(8,128)(2,1)S(1)}, bf16[1,256,768]{1,2,0:T(8,128)(2,1)}, u32[]{:S(2)}, u32[]{:S(2)}) collective-permute-start(bf16[1,256,768]{1,2,0:T(8,128)(2,1)S(1)} %get-tuple-element.1582), channel_id=1, source_target_pairs={{2,0},{4,2},{6,4},{8,6},{10,8},{12,10},{14,12},{16,14},{18,16},{20... | collective-permute-start | bytes 1179656 | tf_op jit(solution)/shard_map/while/body/eval_jaxpr/ppermute | solution.py:21
  551.0 13.7 %collective-permute-start.2 = (bf16[1,256,768]{1,2,0:T(8,128)(2,1)}, bf16[1,256,768]{1,2,0:T(8,128)(2,1)}, u32[]{:S(2)}, u32[]{:S(2)}) collective-permute-start(bf16[1,256,768]{1,2,0:T(8,128)(2,1)} %get-tuple-element.1583), channel_id=1, source_target_pairs={{2,0},{4,2},{6,4},{8,6},{10,8},{12,10},{14,12},{16,14},{18,16},{20... | collective-permute-start | bytes 1179656 | tf_op jit(solution)/shard_map/while/body/eval_jaxpr/ppermute | solution.py:21
  552.9 10.5 collective-permute-start.1
  578.4 20.4 %collective-permute-start = (bf16[1,256,768]{1,2,0:T(8,128)(2,1)S(1)}, bf16[1,256,768]{1,2,0:T(8,128)(2,1)}, u32[]{:S(2)}, u32[]{:S(2)}) collective-permute-start(bf16[1,256,768]{1,2,0:T(8,128)(2,1)S(1)} %get-tuple-element.1582), channel_id=1, source_target_pairs={{2,0},{4,2},{6,4},{8,6},{10,8},{12,10},{14,12},{16,14},{18,16},{20... | collective-permute-start | bytes 1179656 | tf_op jit(solution)/shard_map/while/body/eval_jaxpr/ppermute | solution.py:21
  580.3 18.4 %collective-permute-start.2 = (bf16[1,256,768]{1,2,0:T(8,128)(2,1)}, bf16[1,256,768]{1,2,0:T(8,128)(2,1)}, u32[]{:S(2)}, u32[]{:S(2)}) collective-permute-start(bf16[1,256,768]{1,2,0:T(8,128)(2,1)} %get-tuple-element.1583), channel_id=1, source_target_pairs={{2,0},{4,2},{6,4},{8,6},{10,8},{12,10},{14,12},{16,14},{18,16},{20... | collective-permute-start | bytes 1179656 | tf_op jit(solution)/shard_map/while/body/eval_jaxpr/ppermute | solution.py:21
  582.2 15.3 %collective-permute-start.1 = (f32[1,256,12]{1,2,0:T(8,128)}, f32[1,256,12]{1,2,0:T(8,128)S(1)}, u32[]{:S(2)}, u32[]{:S(2)}) collective-permute-start(f32[1,256,12]{1,2,0:T(8,128)} %get-tuple-element.1584), channel_id=1, source_target_pairs={{2,0},{4,2},{6,4},{8,6},{10,8},{12,10},{14,12},{16,14},{18,16},{20... | collective-permute-start | bytes 36872 | tf_op jit(solution)/shard_map/while/body/eval_jaxpr/ppermute | solution.py:21
  584.2 14.0 %collective-permute-start.3 = (f32[1,256,12]{1,2,0:T(8,128)}, f32[1,256,12]{1,2,0:T(8,128)S(1)}, u32[]{:S(2)}, u32[]{:S(2)}) collective-permute-start(f32[1,256,12]{1,2,0:T(8,128)} %get-tuple-element.1585), channel_id=1, source_target_pairs={{2,0},{4,2},{6,4},{8,6},{10,8},{12,10},{14,12},{16,14},{18,16},{20... | collective-permute-start | bytes 36872 | tf_op jit(solution)/shard_map/while/body/eval_jaxpr/ppermute | solution.py:21
  612.5 15.6 %collective-permute-start = (bf16[1,256,768]{1,2,0:T(8,128)(2,1)S(1)}, bf16[1,256,768]{1,2,0:T(8,128)(2,1)}, u32[]{:S(2)}, u32[]{:S(2)}) collective-permute-start(bf16[1,256,768]{1,2,0:T(8,128)(2,1)S(1)} %get-tuple-element.1582), channel_id=1, source_target_pairs={{2,0},{4,2},{6,4},{8,6},{10,8},{12,10},{14,12},{16,14},{18,16},{20... | collective-permute-start | bytes 1179656 | tf_op jit(solution)/shard_map/while/body/eval_jaxpr/ppermute | solution.py:21
  614.4 13.7 %collective-permute-start.2 = (bf16[1,256,768]{1,2,0:T(8,128)(2,1)}, bf16[1,256,768]{1,2,0:T(8,128)(2,1)}, u32[]{:S(2)}, u32[]{:S(2)}) collective-permute-start(bf16[1,256,768]{1,2,0:T(8,128)(2,1)} %get-tuple-element.1583), channel_id=1, source_target_pairs={{2,0},{4,2},{6,4},{8,6},{10,8},{12,10},{14,12},{16,14},{18,16},{20... | collective-permute-start | bytes 1179656 | tf_op jit(solution)/shard_map/while/body/eval_jaxpr/ppermute | solution.py:21
  616.4 10.5 collective-permute-start.1
  641.8 20.4 %collective-permute-start = (bf16[1,256,768]{1,2,0:T(8,128)(2,1)S(1)}, bf16[1,256,768]{1,2,0:T(8,128)(2,1)}, u32[]{:S(2)}, u32[]{:S(2)}) collective-permute-start(bf16[1,256,768]{1,2,0:T(8,128)(2,1)S(1)} %get-tuple-element.1582), channel_id=1, source_target_pairs={{2,0},{4,2},{6,4},{8,6},{10,8},{12,10},{14,12},{16,14},{18,16},{20... | collective-permute-start | bytes 1179656 | tf_op jit(solution)/shard_map/while/body/eval_jaxpr/ppermute | solution.py:21
  643.8 18.5 %collective-permute-start.2 = (bf16[1,256,768]{1,2,0:T(8,128)(2,1)}, bf16[1,256,768]{1,2,0:T(8,128)(2,1)}, u32[]{:S(2)}, u32[]{:S(2)}) collective-permute-start(bf16[1,256,768]{1,2,0:T(8,128)(2,1)} %get-tuple-element.1583), channel_id=1, source_target_pairs={{2,0},{4,2},{6,4},{8,6},{10,8},{12,10},{14,12},{16,14},{18,16},{20... | collective-permute-start | bytes 1179656 | tf_op jit(solution)/shard_map/while/body/eval_jaxpr/ppermute | solution.py:21
  645.7 15.3 %collective-permute-start.1 = (f32[1,256,12]{1,2,0:T(8,128)}, f32[1,256,12]{1,2,0:T(8,128)S(1)}, u32[]{:S(2)}, u32[]{:S(2)}) collective-permute-start(f32[1,256,12]{1,2,0:T(8,128)} %get-tuple-element.1584), channel_id=1, source_target_pairs={{2,0},{4,2},{6,4},{8,6},{10,8},{12,10},{14,12},{16,14},{18,16},{20... | collective-permute-start | bytes 36872 | tf_op jit(solution)/shard_map/while/body/eval_jaxpr/ppermute | solution.py:21
  647.6 14.0 %collective-permute-start.3 = (f32[1,256,12]{1,2,0:T(8,128)}, f32[1,256,12]{1,2,0:T(8,128)S(1)}, u32[]{:S(2)}, u32[]{:S(2)}) collective-permute-start(f32[1,256,12]{1,2,0:T(8,128)} %get-tuple-element.1585), channel_id=1, source_target_pairs={{2,0},{4,2},{6,4},{8,6},{10,8},{12,10},{14,12},{16,14},{18,16},{20... | collective-permute-start | bytes 36872 | tf_op jit(solution)/shard_map/while/body/eval_jaxpr/ppermute | solution.py:21
  676.0 15.6 %collective-permute-start = (bf16[1,256,768]{1,2,0:T(8,128)(2,1)S(1)}, bf16[1,256,768]{1,2,0:T(8,128)(2,1)}, u32[]{:S(2)}, u32[]{:S(2)}) collective-permute-start(bf16[1,256,768]{1,2,0:T(8,128)(2,1)S(1)} %get-tuple-element.1582), channel_id=1, source_target_pairs={{2,0},{4,2},{6,4},{8,6},{10,8},{12,10},{14,12},{16,14},{18,16},{20... | collective-permute-start | bytes 1179656 | tf_op jit(solution)/shard_map/while/body/eval_jaxpr/ppermute | solution.py:21
  677.9 13.7 %collective-permute-start.2 = (bf16[1,256,768]{1,2,0:T(8,128)(2,1)}, bf16[1,256,768]{1,2,0:T(8,128)(2,1)}, u32[]{:S(2)}, u32[]{:S(2)}) collective-permute-start(bf16[1,256,768]{1,2,0:T(8,128)(2,1)} %get-tuple-element.1583), channel_id=1, source_target_pairs={{2,0},{4,2},{6,4},{8,6},{10,8},{12,10},{14,12},{16,14},{18,16},{20... | collective-permute-start | bytes 1179656 | tf_op jit(solution)/shard_map/while/body/eval_jaxpr/ppermute | solution.py:21
  679.8 10.5 collective-permute-start.1
  705.3 20.4 %collective-permute-start = (bf16[1,256,768]{1,2,0:T(8,128)(2,1)S(1)}, bf16[1,256,768]{1,2,0:T(8,128)(2,1)}, u32[]{:S(2)}, u32[]{:S(2)}) collective-permute-start(bf16[1,256,768]{1,2,0:T(8,128)(2,1)S(1)} %get-tuple-element.1582), channel_id=1, source_target_pairs={{2,0},{4,2},{6,4},{8,6},{10,8},{12,10},{14,12},{16,14},{18,16},{20... | collective-permute-start | bytes 1179656 | tf_op jit(solution)/shard_map/while/body/eval_jaxpr/ppermute | solution.py:21
  707.2 18.5 %collective-permute-start.2 = (bf16[1,256,768]{1,2,0:T(8,128)(2,1)}, bf16[1,256,768]{1,2,0:T(8,128)(2,1)}, u32[]{:S(2)}, u32[]{:S(2)}) collective-permute-start(bf16[1,256,768]{1,2,0:T(8,128)(2,1)} %get-tuple-element.1583), channel_id=1, source_target_pairs={{2,0},{4,2},{6,4},{8,6},{10,8},{12,10},{14,12},{16,14},{18,16},{20... | collective-permute-start | bytes 1179656 | tf_op jit(solution)/shard_map/while/body/eval_jaxpr/ppermute | solution.py:21
  709.2 15.3 %collective-permute-start.1 = (f32[1,256,12]{1,2,0:T(8,128)}, f32[1,256,12]{1,2,0:T(8,128)S(1)}, u32[]{:S(2)}, u32[]{:S(2)}) collective-permute-start(f32[1,256,12]{1,2,0:T(8,128)} %get-tuple-element.1584), channel_id=1, source_target_pairs={{2,0},{4,2},{6,4},{8,6},{10,8},{12,10},{14,12},{16,14},{18,16},{20... | collective-permute-start | bytes 36872 | tf_op jit(solution)/shard_map/while/body/eval_jaxpr/ppermute | solution.py:21
  711.1 14.0 %collective-permute-start.3 = (f32[1,256,12]{1,2,0:T(8,128)}, f32[1,256,12]{1,2,0:T(8,128)S(1)}, u32[]{:S(2)}, u32[]{:S(2)}) collective-permute-start(f32[1,256,12]{1,2,0:T(8,128)} %get-tuple-element.1585), channel_id=1, source_target_pairs={{2,0},{4,2},{6,4},{8,6},{10,8},{12,10},{14,12},{16,14},{18,16},{20... | collective-permute-start | bytes 36872 | tf_op jit(solution)/shard_map/while/body/eval_jaxpr/ppermute | solution.py:21
  739.4 15.6 %collective-permute-start = (bf16[1,256,768]{1,2,0:T(8,128)(2,1)S(1)}, bf16[1,256,768]{1,2,0:T(8,128)(2,1)}, u32[]{:S(2)}, u32[]{:S(2)}) collective-permute-start(bf16[1,256,768]{1,2,0:T(8,128)(2,1)S(1)} %get-tuple-element.1582), channel_id=1, source_target_pairs={{2,0},{4,2},{6,4},{8,6},{10,8},{12,10},{14,12},{16,14},{18,16},{20... | collective-permute-start | bytes 1179656 | tf_op jit(solution)/shard_map/while/body/eval_jaxpr/ppermute | solution.py:21
  741.3 13.7 %collective-permute-start.2 = (bf16[1,256,768]{1,2,0:T(8,128)(2,1)}, bf16[1,256,768]{1,2,0:T(8,128)(2,1)}, u32[]{:S(2)}, u32[]{:S(2)}) collective-permute-start(bf16[1,256,768]{1,2,0:T(8,128)(2,1)} %get-tuple-element.1583), channel_id=1, source_target_pairs={{2,0},{4,2},{6,4},{8,6},{10,8},{12,10},{14,12},{16,14},{18,16},{20... | collective-permute-start | bytes 1179656 | tf_op jit(solution)/shard_map/while/body/eval_jaxpr/ppermute | solution.py:21
  743.3 10.5 collective-permute-start.1
  768.8 20.4 %collective-permute-start = (bf16[1,256,768]{1,2,0:T(8,128)(2,1)S(1)}, bf16[1,256,768]{1,2,0:T(8,128)(2,1)}, u32[]{:S(2)}, u32[]{:S(2)}) collective-permute-start(bf16[1,256,768]{1,2,0:T(8,128)(2,1)S(1)} %get-tuple-element.1582), channel_id=1, source_target_pairs={{2,0},{4,2},{6,4},{8,6},{10,8},{12,10},{14,12},{16,14},{18,16},{20... | collective-permute-start | bytes 1179656 | tf_op jit(solution)/shard_map/while/body/eval_jaxpr/ppermute | solution.py:21
  770.7 18.5 %collective-permute-start.2 = (bf16[1,256,768]{1,2,0:T(8,128)(2,1)}, bf16[1,256,768]{1,2,0:T(8,128)(2,1)}, u32[]{:S(2)}, u32[]{:S(2)}) collective-permute-start(bf16[1,256,768]{1,2,0:T(8,128)(2,1)} %get-tuple-element.1583), channel_id=1, source_target_pairs={{2,0},{4,2},{6,4},{8,6},{10,8},{12,10},{14,12},{16,14},{18,16},{20... | collective-permute-start | bytes 1179656 | tf_op jit(solution)/shard_map/while/body/eval_jaxpr/ppermute | solution.py:21
  772.6 15.3 %collective-permute-start.1 = (f32[1,256,12]{1,2,0:T(8,128)}, f32[1,256,12]{1,2,0:T(8,128)S(1)}, u32[]{:S(2)}, u32[]{:S(2)}) collective-permute-start(f32[1,256,12]{1,2,0:T(8,128)} %get-tuple-element.1584), channel_id=1, source_target_pairs={{2,0},{4,2},{6,4},{8,6},{10,8},{12,10},{14,12},{16,14},{18,16},{20... | collective-permute-start | bytes 36872 | tf_op jit(solution)/shard_map/while/body/eval_jaxpr/ppermute | solution.py:21
  774.5 14.0 %collective-permute-start.3 = (f32[1,256,12]{1,2,0:T(8,128)}, f32[1,256,12]{1,2,0:T(8,128)S(1)}, u32[]{:S(2)}, u32[]{:S(2)}) collective-permute-start(f32[1,256,12]{1,2,0:T(8,128)} %get-tuple-element.1585), channel_id=1, source_target_pairs={{2,0},{4,2},{6,4},{8,6},{10,8},{12,10},{14,12},{16,14},{18,16},{20... | collective-permute-start | bytes 36872 | tf_op jit(solution)/shard_map/while/body/eval_jaxpr/ppermute | solution.py:21
  802.9 15.6 %collective-permute-start = (bf16[1,256,768]{1,2,0:T(8,128)(2,1)S(1)}, bf16[1,256,768]{1,2,0:T(8,128)(2,1)}, u32[]{:S(2)}, u32[]{:S(2)}) collective-permute-start(bf16[1,256,768]{1,2,0:T(8,128)(2,1)S(1)} %get-tuple-element.1582), channel_id=1, source_target_pairs={{2,0},{4,2},{6,4},{8,6},{10,8},{12,10},{14,12},{16,14},{18,16},{20... | collective-permute-start | bytes 1179656 | tf_op jit(solution)/shard_map/while/body/eval_jaxpr/ppermute | solution.py:21
  804.8 13.7 %collective-permute-start.2 = (bf16[1,256,768]{1,2,0:T(8,128)(2,1)}, bf16[1,256,768]{1,2,0:T(8,128)(2,1)}, u32[]{:S(2)}, u32[]{:S(2)}) collective-permute-start(bf16[1,256,768]{1,2,0:T(8,128)(2,1)} %get-tuple-element.1583), channel_id=1, source_target_pairs={{2,0},{4,2},{6,4},{8,6},{10,8},{12,10},{14,12},{16,14},{18,16},{20... | collective-permute-start | bytes 1179656 | tf_op jit(solution)/shard_map/while/body/eval_jaxpr/ppermute | solution.py:21
  806.7 10.5 collective-permute-start.1
  832.2 14.7 %collective-permute-start = (bf16[1,256,768]{1,2,0:T(8,128)(2,1)S(1)}, bf16[1,256,768]{1,2,0:T(8,128)(2,1)}, u32[]{:S(2)}, u32[]{:S(2)}) collective-permute-start(bf16[1,256,768]{1,2,0:T(8,128)(2,1)S(1)} %get-tuple-element.1582), channel_id=1, source_target_pairs={{2,0},{4,2},{6,4},{8,6},{10,8},{12,10},{14,12},{16,14},{18,16},{20... | collective-permute-start | bytes 1179656 | tf_op jit(solution)/shard_map/while/body/eval_jaxpr/ppermute | solution.py:21
  834.1 12.8 %collective-permute-start.2 = (bf16[1,256,768]{1,2,0:T(8,128)(2,1)}, bf16[1,256,768]{1,2,0:T(8,128)(2,1)}, u32[]{:S(2)}, u32[]{:S(2)}) collective-permute-start(bf16[1,256,768]{1,2,0:T(8,128)(2,1)} %get-tuple-element.1583), channel_id=1, source_target_pairs={{2,0},{4,2},{6,4},{8,6},{10,8},{12,10},{14,12},{16,14},{18,16},{20... | collective-permute-start | bytes 1179656 | tf_op jit(solution)/shard_map/while/body/eval_jaxpr/ppermute | solution.py:21
  836.1 9.6 collective-permute-start.1
  859.2 74.1 %reduce-scatter.7.cloned.1.call-start = ((), (), s32[]{:S(2)}) async-start(), calls=%async_computation.10 | async-start | bytes 1769472 | tf_op jit(solution)/shard_map/reduce_scatter | solution.py:374
  861.9 134.3 %reduce-scatter.9.cloned.1.call-start = ((), (), s32[]{:S(2)}) async-start(), calls=%async_computation.11 | async-start | bytes 7077888 | tf_op jit(solution)/shard_map/reduce_scatter | solution.py:386
  866.5 192.6 %reduce-scatter.11.cloned.1.call-start = ((), (), s32[]{:S(2)}) async-start(), calls=%async_computation.12 | async-start | bytes 7077888 | tf_op jit(solution)/shard_map/reduce_scatter | solution.py:392
  872.4 343.7 %all-reduce.13.cloned.1.call-start = ((), (), s32[]{:S(2)}) async-start(), calls=%async_computation.14 | async-start | bytes 14155776 | tf_op jit(solution)/shard_map/psum | solution.py:406
  (77 other events, 1647.0 us)
Sparse Core Ops, SparseCore 0:
  9.6 51.4 all-gather.14
  65.3 62.2 all-gather.18
  130.4 60.4 all-gather.16
  192.3 20.9 all-gather.20
  214.7 62.6 all-gather.22
  278.8 62.6 all-gather.24
  859.3 49.2 reduce-scatter.12
  911.5 21.7 reduce-scatter.6
  936.2 59.9 reduce-scatter.8
  999.1 59.9 reduce-scatter.10
  1063.7 152.3 all-reduce.12
where the time goes:
time: 1250 us; the launch traced here: 1230 us
  waiting for transfers between devices  645 us (52%)
  matrix products  196 us (16%)
  starting transfers between devices  116 us (9%)
  local copies, waits for them, and re-layouts  116 us (9%)
  blocking collectives  92.9 us (7%)
  other arithmetic  48.7 us (4%)
  between operations  17 us (1%)
    ppermute x60, waiting for transfers between devices, shifted(): return lax.ppermute(value, axis, pairs)  139 us
    ppermute x60, starting transfers between devices, shifted(): return lax.ppermute(value, axis, pairs)  116 us
    psum x1, waiting for transfers between devices, on_device(): lax.psum(group_parts[0].astype(jnp.bfloat16), 'rep').astype(jnp.float32)  78.7 us
    reduce_scatter x1, waiting for transfers between devices, on_device(): lax.psum_scatter(local_grads[6].astype(jnp.bfloat16), 'shard', scatter_di...  62.9 us
    reduce_scatter x1, waiting for transfers between devices, on_device(): lax.psum_scatter(local_grads[8].astype(jnp.bfloat16), 'shard', scatter_di...  62.9 us
    all_gather x1, waiting for transfers between devices, on_device(): lax.all_gather(params[6], 'shard', axis=0, tiled=True)  61.9 us
    dot_general x15, matrix products, keys_step(): jnp.einsum('sqhk,sqhd->skhd', grad_score, query_block, preferred_element_...  60.7 us
    psum x1, blocking collectives, on_device(): lax.psum(group_parts[1].astype(jnp.bfloat16), 'rep').astype(jnp.float32)  60.2 us
  transfers between devices with their start and end apart: 71, of which 26 were waited for; matrix products, arithmetic and copies ran while one was open for 8% of the time, Pallas kernels for 0%

commit v1 on v0

v1 whole, which is shorter than its diff:
```python
import jax
import jax.numpy as jnp
from jax import lax
from jax.experimental import pallas as pl
from jax.experimental.pallas import tpu as pltpu
from jax.sharding import PartitionSpec as P

HEADS = 12
HEAD_DIM = 64
BLOCK = 256
GROUPS = 4
PER = HEADS // GROUPS
SLAB = PER * HEAD_DIM
EPSILON = 1e-05
FAR = 2.0**100
F32 = jnp.float32
BF16 = jnp.bfloat16
NN = (((1,), (0,)), ((), ()))
NT = (((1,), (1,)), ((), ()))
VMEM_SPEC = pl.BlockSpec(memory_space=pltpu.VMEM)
VMEM_LIMIT = 67043328


def mm(left, right, dims=NN):
    return lax.dot_general(left, right, dims, preferred_element_type=F32)


def forward_kernel(
    members, x_ref, w_ref, bias_ref, docs_ref,
    o_ref, low_ref, lse_ref, q_ref, k_ref, kt_ref, vt_ref,
    top_ref, sum_ref,
):
    blocks = docs_ref.shape[0]
    m = lax.rem(lax.axis_index("rep"), members)

    def project(b, carry):
        rows = pl.ds(pl.multiple_of(b * BLOCK, BLOCK), BLOCK)
        both = mm(w_ref[SLAB:, :], x_ref[rows, :], NT)
        kt = both[:SLAB].astype(BF16)
        kt_ref[b] = kt
        vt_ref[b] = (both[SLAB:] + bias_ref[SLAB:, :]).astype(BF16)
        docs = docs_ref[b]
        extra = jnp.concatenate(
            [docs * FAR - FAR, docs * (-FAR), jnp.zeros((HEAD_DIM - 2, BLOCK), F32)], axis=0
        )
        for h in range(PER):
            part = kt[h * HEAD_DIM : (h + 1) * HEAD_DIM].astype(F32)
            k_ref[h, rows, :] = jnp.concatenate([part, extra], axis=0).T.astype(BF16)
        return carry

    lax.fori_loop(0, blocks, project, 0)
    for i in range(GROUPS):
        b = i * members + m
        rows = pl.ds(pl.multiple_of(b * BLOCK, BLOCK), BLOCK)
        qt = (mm(w_ref[:SLAB, :], x_ref[rows, :], NT) + bias_ref[:SLAB, :]).astype(BF16)
        qt = qt.astype(F32) * HEAD_DIM ** (-0.5)
        docs = docs_ref[b]
        extra = jnp.concatenate(
            [docs, 1.0 - docs, jnp.zeros((HEAD_DIM - 2, BLOCK), F32)], axis=0
        )
        for h in range(PER):
            part = qt[h * HEAD_DIM : (h + 1) * HEAD_DIM]
            q_ref[i, h] = jnp.concatenate([part, extra], axis=0).astype(BF16)
        top_ref[...] = jnp.full(top_ref.shape, -jnp.inf, F32)
        sum_ref[...] = jnp.zeros(sum_ref.shape, F32)
        o_ref[i] = jnp.zeros((SLAB, BLOCK), F32)

        def attend(step, carry):
            kb = b - step
            keys = pl.ds(pl.multiple_of(kb * BLOCK, BLOCK), BLOCK)
            for h in range(PER):
                head = pl.ds(h * HEAD_DIM, HEAD_DIM)
                score = mm(k_ref[h, keys, :], q_ref[i, h])
                old = top_ref[h]
                new = jnp.maximum(old, jnp.max(score, axis=0, keepdims=True))
                probs = jnp.exp(score - new)
                shrink = jnp.exp(old - new)
                top_ref[h] = new
                sum_ref[h] = sum_ref[h] * shrink + jnp.sum(probs, axis=0, keepdims=True)
                o_ref[i, head, :] = o_ref[i, head, :] * shrink + mm(
                    vt_ref[kb, head, :], probs.astype(BF16)
                )
            return carry

        lax.fori_loop(0, b + 1, attend, 0)
        for h in range(PER):
            head = pl.ds(h * HEAD_DIM, HEAD_DIM)
            out = o_ref[i, head, :] / sum_ref[h]
            o_ref[i, head, :] = out
            low_ref[i, head, :] = out.astype(BF16)
            lse_ref[i, h] = top_ref[h] + jnp.log(sum_ref[h])


def attention_forward(x_all, w_group, bias, docs, members):
    blocks = docs.shape[0]
    shape = jax.ShapeDtypeStruct
    return pl.pallas_call(
        lambda *refs: forward_kernel(members, *refs),
        out_shape=(
            shape((GROUPS, SLAB, BLOCK), F32),
            shape((GROUPS, SLAB, BLOCK), BF16),
            shape((GROUPS, PER, 1, BLOCK), F32),
            shape((GROUPS, PER, 2 * HEAD_DIM, BLOCK), BF16),
            shape((PER, blocks * BLOCK, 2 * HEAD_DIM), BF16),
            shape((blocks, SLAB, BLOCK), BF16),
            shape((blocks, SLAB, BLOCK), BF16),
        ),
        in_specs=[VMEM_SPEC] * 4,
        out_specs=(VMEM_SPEC,) * 7,
        scratch_shapes=[pltpu.VMEM((PER, 1, BLOCK), F32), pltpu.VMEM((PER, 1, BLOCK), F32)],
        compiler_params=pltpu.CompilerParams(vmem_limit_bytes=VMEM_LIMIT),
    )(x_all, w_group, bias, docs)


def remote(src, dst, send, recv, rep, shard):
    return pltpu.make_async_remote_copy(
        src_ref=src, dst_ref=dst, send_sem=send, recv_sem=recv,
        device_id=(rep, shard), device_id_type=pl.DeviceIdType.MESH,
    )


def hello(partners):
    barrier = pltpu.get_barrier_semaphore()
    total = 0
    for rep, shard, there in partners:
        if there is True:
            pl.semaphore_signal(
                barrier, inc=1, device_id=(rep, shard), device_id_type=pl.DeviceIdType.MESH
            )
            total = total + 1
        else:

            @pl.when(there)
            def _():
                pl.semaphore_signal(
                    barrier, inc=1, device_id=(rep, shard), device_id_type=pl.DeviceIdType.MESH
                )

            total = total + there.astype(jnp.int32)
    pl.semaphore_wait(barrier, total)


def gather_kernel(
    ring, shards, parts, x_ref, *refs,
):
    n = len(parts)
    own, (xa_ref, *full) = refs[:n], refs[n : 2 * n + 1]
    send, recv, wsend, wrecv, fsend, frecv, lsem = refs[2 * n + 1 :]
    r, s = lax.axis_index("rep"), lax.axis_index("shard")
    levels = ring // 4
    z, c = r // 4, lax.rem(r, 2)
    sib = r + 1 - 2 * c
    yn = r + 2 - 4 * lax.rem(r // 2, 2)
    above, below = z < levels - 1, z > 0
    others = [lax.rem(s + d, shards) for d in range(1, shards)]
    hello(
        [(sib, s, True), (yn, s, True), (r + 4, s, above), (r - 4, s, below)]
        + [(r, t, True) for t in others]
    )

    def move(b, kind):
        src = xa_ref.at[b]
        target = (r + 4, r - 4, yn, sib)[kind]
        return remote(src, xa_ref.at[b], send.at[kind, b], recv.at[b], target, s)

    def first(kind):
        target = (r + 4, r - 4, yn, sib)[kind]
        return remote(x_ref, xa_ref.at[r], send.at[kind, r], recv.at[r], target, s)

    keep = pltpu.make_async_copy(x_ref, xa_ref.at[r], lsem)
    keep.start()
    pl.when(above)(lambda: first(0).start())
    pl.when(below)(lambda: first(1).start())
    first(2).start()
    first(3).start()

    pieces = []
    for w, count in enumerate(parts):
        size = own[w].shape[0] // 2 // count
        for j in range(count):
            pieces.append((w, j, count, size, len(pieces)))

    def across(piece, d):
        w, j, count, size, at = piece
        rows = pl.ds(pl.multiple_of((c * count + j) * size, size), size)
        return remote(
            own[w].at[rows], full[w].at[s, rows], wsend.at[at, d - 1], wrecv.at[at, d - 1],
            r, others[d - 1],
        )

    def along(piece, d, core):
        w, j, count, size, at = piece
        rows = pl.ds(pl.multiple_of((core * count + j) * size, size), size)
        place = full[w].at[lax.rem(s + shards - d, shards), rows]
        return remote(place, place, fsend.at[at, d - 1], frecv.at[at, d - 1], sib, s)

    for piece in pieces:
        for d in range(1, shards):
            across(piece, d).start()

    def pass_on(b, there, kinds):
        def go():
            move(b, 3).wait_recv()
            for kind, also in kinds:
                if also is True:
                    move(b, kind).start()
                else:
                    pl.when(also)(lambda kind=kind: move(b, kind).start())

        if there is True:
            go()
        else:
            pl.when(there)(go)

    for k in range(levels):
        low, high = z >= k, z + k < levels
        if k:
            pass_on(r - 4 * k, low, [(0, above), (2, True), (3, True)])
            pass_on(r + 4 * k, high, [(1, below), (2, True), (3, True)])
            pass_on(yn - 4 * k, low, [(3, True)])
            pass_on(yn + 4 * k, high, [(3, True)])
        else:
            pass_on(yn, True, [(3, True)])
    for piece in pieces:
        for d in range(1, shards):
            across(piece, d).wait_recv()
            along(piece, d, c).start()
    keep.wait()
    for b in range(0, ring, 2):
        move(b + 1 - c, 3).wait_recv()
    for piece in pieces:
        for d in range(1, shards):
            along(piece, d, 1 - c).wait_recv()
    pl.when(above)(lambda: first(0).wait_send())
    pl.when(below)(lambda: first(1).wait_send())
    first(2).wait_send()
    first(3).wait_send()
    for k in range(levels):
        low, high = z >= k, z + k < levels
        if k:
            for b, there, kind, also in (
                (r - 4 * k, low, 0, above), (r + 4 * k, high, 1, below),
            ):

                @pl.when(there)
                def _():
                    pl.when(also)(lambda: move(b, kind).wait_send())
                    move(b, 2).wait_send()
                    move(b, 3).wait_send()

            pl.when(low)(lambda: move(yn - 4 * k, 3).wait_send())
            pl.when(high)(lambda: move(yn + 4 * k, 3).wait_send())
        else:
            move(yn, 3).wait_send()
    for piece in pieces:
        for d in range(1, shards):
            across(piece, d).wait_send()
            along(piece, d, c).wait_send()


ANY_SPEC = pl.BlockSpec(memory_space=pl.ANY)


def gather_all(x, weights, parts, ring, shards):
    shape = jax.ShapeDtypeStruct
    dma = pltpu.SemaphoreType.DMA
    n = sum(parts)
    return pl.pallas_call(
        lambda *refs: gather_kernel(ring, shards, parts, *refs),
        out_shape=(shape((ring,) + x.shape, x.dtype),)
        + tuple(shape((shards,) + w.shape, w.dtype) for w in weights),
        in_specs=[ANY_SPEC] * (1 + len(weights)),
        out_specs=(ANY_SPEC,) * (1 + len(weights)),
        scratch_shapes=[
            dma((4, ring)), dma((ring,)), dma((n, shards - 1)), dma((n, shards - 1)),
            dma((n, shards - 1)), dma((n, shards - 1)), dma(()),
        ],
        compiler_params=pltpu.CompilerParams(collective_id=0, has_side_effects=True),
    )(x, *weights)


def exchange_kernel(ring, in_ref, out_ref, send, recv, lsem):
    r, s = lax.axis_index("rep"), lax.axis_index("shard")
    members = ring // GROUPS
    g, m = r // members, lax.rem(r, members)
    peers = [lax.rem(g + d, GROUPS) for d in range(1, GROUPS)]
    hello([(p * members + m, s, True) for p in peers])
    copies = [
        remote(
            in_ref.at[p], out_ref.at[g], send.at[d], recv.at[d], p * members + m, s
        )
        for d, p in enumerate(peers)
    ]
    for copy in copies:
        copy.start()
    keep = pltpu.make_async_copy(in_ref.at[g], out_ref.at[g], lsem)
    keep.start()
    keep.wait()
    for copy in copies:
        copy.wait()


def exchange_slabs(slabs, ring, ident):
    dma = pltpu.SemaphoreType.DMA
    return pl.pallas_call(
        lambda *refs: exchange_kernel(ring, *refs),
        out_shape=jax.ShapeDtypeStruct(slabs.shape, slabs.dtype),
        in_specs=[VMEM_SPEC],
        out_specs=VMEM_SPEC,
        scratch_shapes=[dma((GROUPS - 1,)), dma((GROUPS - 1,)), dma(())],
        compiler_params=pltpu.CompilerParams(collective_id=ident, has_side_effects=True),
    )(slabs)


def backward_kernel(
    ring, go_ref, q_ref, k_ref, kt_ref, vt_ref, o_ref, lse_ref, xa_ref, w_ref, mid_ref,
    out_ref, dw_ref, db_ref,
    g_ref, x_ref, v_ref, delta_ref, acc_ref, dk_ref, dv_ref, pq_ref, stage_ref, got_ref,
    total_ref, dx_ref, near_ref, far_ref, gsend, grecv, ksend, krecv, xsend, xrecv, lsem,
):
    r, s = lax.axis_index("rep"), lax.axis_index("shard")
    members = ring // GROUPS
    g, m = r // members, lax.rem(r, members)
    peers = [lax.rem(g + d, GROUPS) for d in range(1, GROUPS)]
    mates = [lax.rem(m + d, members) for d in range(1, members)]
    hello(
        [(p * members + m, s, True) for p in peers] + [(g * members + t, s, True) for t in mates]
    )
    loads = [
        pltpu.make_async_copy(xa_ref.at[j * members + m], x_ref.at[j], lsem.at[j])
        for j in range(GROUPS)
    ]
    for load in loads:
        load.start()

    def give(p):
        return remote(go_ref.at[p], g_ref.at[g], gsend.at[p], grecv.at[g], p * members + m, s)

    def take(p):
        return remote(go_ref.at[p], g_ref.at[p], gsend.at[p], grecv.at[p], p * members + m, s)

    for p in peers:
        give(p).start()
    g_ref[g] = go_ref[g]

    def turn(b, carry):
        rows = pl.ds(pl.multiple_of(b * BLOCK, BLOCK), BLOCK)
        for h in range(PER):
            v_ref[h, rows, :] = (
                vt_ref[b, h * HEAD_DIM : (h + 1) * HEAD_DIM, :].astype(F32).T.astype(BF16)
            )
        dk_ref[b] = jnp.zeros((SLAB, BLOCK), F32)
        dv_ref[b] = jnp.zeros((SLAB, BLOCK), F32)
        return carry

    lax.fori_loop(0, ring, turn, 0)
    total_ref[...] = jnp.zeros(total_ref.shape, F32)
    db_ref[...] = jnp.zeros(db_ref.shape, F32)

    def share(j, d):
        return remote(
            stage_ref.at[j, mates[d - 1]], got_ref.at[j, d - 1],
            ksend.at[j, d - 1], krecv.at[j, d - 1], g * members + mates[d - 1], s,
        )

    def attend_block(i):
        b = i * members + m
        pl.when(g != i)(lambda: take(i).wait_recv())
        for h in range(PER):
            head = pl.ds(h * HEAD_DIM, HEAD_DIM)
            delta_ref[h] = jnp.sum(
                g_ref[i, head, :].astype(F32) * o_ref[i, head, :], axis=0, keepdims=True
            )
        acc_ref[...] = jnp.zeros(acc_ref.shape, F32)

        def attend(kb, carry):
            keys = pl.ds(pl.multiple_of(kb * BLOCK, BLOCK), BLOCK)
            for h in range(PER):
                head = pl.ds(h * HEAD_DIM, HEAD_DIM)
                score = mm(k_ref[h, keys, :], q_ref[i, h])
                probs = jnp.exp(score - lse_ref[i, h])
                grad = g_ref[i, head, :]
                moved = (probs * (mm(v_ref[h, keys, :], grad) - delta_ref[h])).astype(BF16)
                acc_ref[h] += mm(kt_ref[kb, head, :], moved)
                dk_ref[kb, head, :] += mm(q_ref[i, h, :HEAD_DIM, :], moved, NT)
                dv_ref[kb, head, :] += mm(grad, probs.astype(BF16), NT)
            return carry

        lax.fori_loop(0, b + 1, attend, 0)
        for h in range(PER):
            pq_ref[i, pl.ds(h * HEAD_DIM, HEAD_DIM), :] = (
                acc_ref[h] * HEAD_DIM ** (-0.5)
            ).astype(BF16)
        for t in range(members):
            stage_ref[i, t, :SLAB, :] = dk_ref[i * members + t].astype(BF16)
            stage_ref[i, t, SLAB:, :] = dv_ref[i * members + t].astype(BF16)
        for d in range(1, members):
            share(i, d).start()

    def send_dx(j):
        return remote(
            dx_ref.at[j], far_ref.at[g], xsend.at[j], xrecv.at[g], j * members + m, s
        )

    def finish_block(j):
        b = j * members + m
        for d in range(1, members):
            share(j, d).wait_recv()
        dk, dv = dk_ref[b], dv_ref[b]
        for d in range(1, members):
            dk = dk + got_ref[j, d - 1, :SLAB, :].astype(F32)
            dv = dv + got_ref[j, d - 1, SLAB:, :].astype(F32)
        proj = jnp.concatenate([pq_ref[j], dk.astype(BF16), dv.astype(BF16)], axis=0)
        db_ref[...] += jnp.sum(proj.astype(F32), axis=1, keepdims=True)
        loads[j].wait()
        total_ref[...] += mm(x_ref[j], proj.T, (((0,), (0,)), ((), ())))
        dx = mm(proj, w_ref[...], (((0,), (0,)), ((), ())))

        @pl.when(g == j)
        def _():
            near_ref[...] = dx

        @pl.when(g != j)
        def _():
            dx_ref[j] = dx.astype(BF16)
            send_dx(j).start()

    order = list(range(GROUPS))[::-1]
    for at, i in enumerate(order):
        attend_block(i)
        if at:
            finish_block(order[at - 1])
    finish_block(order[-1])
    dw_ref[...] = total_ref[...].astype(BF16)
    result = near_ref[...] + mid_ref[...]
    for p in peers:
        remote(dx_ref.at[0], far_ref.at[p], xsend.at[0], xrecv.at[p], r, s).wait_recv()
        result = result + far_ref[p].astype(F32)
    out_ref[...] = result.astype(BF16)
    for p in peers:
        give(p).wait_send()
    for j in range(GROUPS):
        for d in range(1, members):
            share(j, d).wait_send()
        pl.when(g != j)(lambda: send_dx(j).wait_send())


def attention_backward(ring, grads, q, k, kt, vt, o, lse, x_all, w_group, mid, ident):
    members = ring // GROUPS
    width = x_all.shape[-1]
    shape = jax.ShapeDtypeStruct
    dma = pltpu.SemaphoreType.DMA
    vmem = pltpu.VMEM
    return pl.pallas_call(
        lambda *refs: backward_kernel(ring, *refs),
        out_shape=(
            shape((BLOCK, width), BF16), shape((width, 3 * SLAB), BF16), shape((3 * SLAB, 1), F32),
        ),
        in_specs=[VMEM_SPEC] * 7 + [ANY_SPEC] + [VMEM_SPEC] * 2,
        out_specs=(VMEM_SPEC,) * 3,
        scratch_shapes=[
            vmem((GROUPS, SLAB, BLOCK), BF16),
            vmem((GROUPS, BLOCK, width), BF16),
            vmem((PER, ring * BLOCK, HEAD_DIM), BF16),
            vmem((PER, 1, BLOCK), F32),
            vmem((PER, HEAD_DIM, BLOCK), F32),
            vmem((ring, SLAB, BLOCK), F32),
            vmem((ring, SLAB, BLOCK), F32),
            vmem((GROUPS, SLAB, BLOCK), BF16),
            vmem((GROUPS, members, 2 * SLAB, BLOCK), BF16),
            vmem((GROUPS, members - 1, 2 * SLAB, BLOCK), BF16),
            vmem((width, 3 * SLAB), F32),
            vmem((GROUPS, BLOCK, width), BF16),
            vmem((BLOCK, width), F32),
            vmem((GROUPS, BLOCK, width), BF16),
            dma((GROUPS,)), dma((GROUPS,)),
            dma((GROUPS, members - 1)), dma((GROUPS, members - 1)),
            dma((GROUPS,)), dma((GROUPS,)), dma((GROUPS,)),
        ],
        compiler_params=pltpu.CompilerParams(
            collective_id=ident, has_side_effects=True, vmem_limit_bytes=VMEM_LIMIT
        ),
    )(grads, q, k, kt, vt, o, lse, x_all, w_group, mid)


def layer_norm(hidden, gain, shift):
    centre = hidden - jnp.mean(hidden, axis=-1, keepdims=True)
    inverse = lax.rsqrt(jnp.mean(centre * centre, axis=-1, keepdims=True) + EPSILON)
    normed = centre * inverse
    return (normed * gain + shift, normed, inverse)


def norm_back(grad_output, normed, inverse, gain):
    grad_normed = grad_output * gain
    centred = grad_normed - jnp.mean(grad_normed, axis=-1, keepdims=True)
    return inverse * (centred - normed * jnp.mean(grad_normed * normed, axis=-1, keepdims=True))


def gelu_slope(value):
    return (
        0.5 * (1.0 + lax.erf(value * 0.7071067811865476))
        + value * jnp.exp(-0.5 * value * value) * 0.3989422804014327
    )


def on_device(
    tokens, doc_ids, qkv_weight, qv_bias, out_weight, out_bias, mid_gain, mid_shift,
    up_weight, up_bias, down_weight, down_bias, end_gain, end_shift, out_grad,
):
    width = tokens.shape[2]
    ring = lax.axis_size("rep")
    members = ring // GROUPS
    r = lax.axis_index("rep")
    g = r // members
    m = lax.rem(r, members)

    shards = lax.axis_size("shard")
    x = tokens[0]
    local = jnp.concatenate(
        [lax.dynamic_slice_in_dim(qkv_weight, t * width + g * SLAB, SLAB, 1) for t in range(3)], 1
    )
    small = (qv_bias, out_bias, mid_gain, mid_shift, up_bias, down_bias, end_gain, end_shift)
    sizes = [v.shape[0] for v in small]
    flat = jnp.concatenate(small)
    lanes = 128
    flat = jnp.pad(flat, (0, -flat.shape[0] % (32 * lanes))).reshape(-1, lanes)
    x_all, w_group, flat, full_out, full_up, full_down = gather_all(
        x, (local, flat, out_weight, up_weight, down_weight), (1, 1, 1, 2, 2), ring, shards
    )

    def whole(gathered, mine):
        put = lax.dynamic_update_index_in_dim(gathered, mine, lax.axis_index("shard"), 0)
        return put.reshape(shards * mine.shape[0], *mine.shape[1:])

    x_all = x_all.reshape(ring * BLOCK, width)
    w_group = whole(w_group, local).T
    flat_own = jnp.pad(jnp.concatenate(small), (0, -sum(sizes) % (32 * lanes)))
    flat = whole(flat.reshape(shards, -1), flat_own).reshape(shards, -1).astype(F32)
    vectors = []
    at = 0
    for size in sizes:
        vectors.append(flat[:, at : at + size].reshape(-1))
        at += size
    vec_qv, vec_out, gain_mid, shift_mid, vec_up, vec_down, gain_end, shift_end = vectors
    full_out, full_up, full_down = (
        whole(full_out, out_weight), whole(full_up, up_weight), whole(full_down, down_weight)
    )
    bias = jnp.concatenate(
        [
            lax.dynamic_slice_in_dim(vec_qv, g * SLAB, SLAB, 0),
            jnp.zeros((SLAB,), F32),
            lax.dynamic_slice_in_dim(vec_qv, width + g * SLAB, SLAB, 0),
        ]
    )
    bias = jnp.concatenate([bias[:SLAB], bias[2 * SLAB :]]).reshape(2 * SLAB, 1)
    docs = doc_ids.reshape(ring, 1, BLOCK).astype(F32)
    o, o_low, lse, q, k, kt, vt = attention_forward(x_all, w_group, bias, docs, members)
    attended_t = exchange_slabs(o_low, ring, 1).reshape(width, BLOCK)

    attended_low = attended_t.T
    branch = mm(attended_low, full_out) + vec_out
    mid_out, mid_norm, mid_inv = layer_norm(x.astype(F32) + branch, gain_mid, shift_mid)
    mid_low = mid_out.astype(BF16)
    pre_act = mm(mid_low, full_up) + vec_up
    activated = jax.nn.gelu(pre_act, approximate=False).astype(BF16)
    ffn_out = mm(activated, full_down) + vec_down
    end_out, end_norm, end_inv = layer_norm(mid_out + ffn_out, gain_end, shift_end)
    layer_out = end_out.astype(BF16)
    grad_top = out_grad[0].astype(F32)
    grad_end_gain = jnp.sum(grad_top * end_norm, axis=0)
    grad_end_shift = jnp.sum(grad_top, axis=0)
    grad_end_in = norm_back(grad_top, end_norm, end_inv, gain_end)
    grad_ffn = grad_end_in.astype(BF16)
    grad_down_bias = jnp.sum(grad_ffn.astype(F32), axis=0)
    grad_down_weight = mm(activated.T, grad_ffn)
    grad_act = mm(grad_ffn, full_down, NT)
    grad_pre = (grad_act * gelu_slope(pre_act)).astype(BF16)
    grad_up_bias = jnp.sum(grad_pre.astype(F32), axis=0)
    grad_up_weight = mm(mid_low.T, grad_pre)
    grad_mid_out = mm(grad_pre, full_up, NT) + grad_end_in
    grad_mid_gain = jnp.sum(grad_mid_out * mid_norm, axis=0)
    grad_mid_shift = jnp.sum(grad_mid_out, axis=0)
    grad_mid_in = norm_back(grad_mid_out, mid_norm, mid_inv, gain_mid)
    grad_branch = grad_mid_in.astype(BF16)
    grad_out_bias = jnp.sum(grad_branch.astype(F32), axis=0)
    grad_out_weight = mm(attended_t, grad_branch)
    grad_attended_t = mm(full_out, grad_branch, NT).astype(BF16)
    input_grad, dw_group, dbias = attention_backward(
        ring, grad_attended_t.reshape(GROUPS, SLAB, BLOCK), q, k, kt, vt, o, lse,
        x_all.reshape(ring, BLOCK, width), w_group, grad_mid_in, 2,
    )
    dw_group = dw_group.astype(F32)

    place = jnp.zeros((width, 3, GROUPS, SLAB), F32)
    grad_qkv = lax.dynamic_update_slice_in_dim(
        place, dw_group.reshape(width, 3, 1, SLAB), g, 2
    ).reshape(width, 3 * width)
    qv = dbias.reshape(3, SLAB)[jnp.array([0, 2])]
    grad_qv_bias = lax.dynamic_update_slice_in_dim(
        jnp.zeros((2, GROUPS, SLAB), F32), qv.reshape(2, 1, SLAB), g, 1
    ).reshape(2 * width)

    def total(value):
        part = lax.psum_scatter(value.astype(BF16), "shard", scatter_dimension=0, tiled=True)
        return lax.psum(part, "rep").astype(F32)

    return (
        layer_out[None],
        input_grad[None],
        total(grad_qkv),
        total(grad_qv_bias),
        total(grad_out_weight),
        total(grad_out_bias),
        total(grad_mid_gain),
        total(grad_mid_shift),
        total(grad_up_weight),
        total(grad_up_bias),
        total(grad_down_weight),
        total(grad_down_bias),
        total(grad_end_gain),
        total(grad_end_shift),
    )


def solution(mesh):
    rows = P("shard", None)
    flat = P("shard")
    acts = P("shard", "rep", None)
    in_specs = (
        acts, rows, rows, flat, rows, flat, flat, flat, rows, flat, rows, flat, flat, flat, acts
    )
    out_specs = (acts, acts, rows, flat, rows, flat, flat, flat, rows, flat, rows, flat, flat, flat)
    return jax.shard_map(
        on_device, mesh=mesh, in_specs=in_specs, out_specs=out_specs, check_vma=False
    )
```

time: 1250 us -> 662 us (0.53); the launches traced: 1230 us -> 660 us
  waiting for transfers between devices: 645 us -> 260 us
  Pallas kernels: 0 us -> 223 us
  matrix products: 196 us -> 32.4 us
  starting transfers between devices: 116 us -> 0.21 us
  local copies, waits for them, and re-layouts: 116 us -> 44.7 us
  other arithmetic: 48.7 us -> 17.9 us
  blocking collectives: 92.9 us -> 65.2 us
    all_gather x6 -> x0, waiting for transfers between devices: 243 us -> none  [the longest x1 61.9 us: on_device(): lax.all_gather(params[6], 'shard', axis=0, tiled=True)]
    pallas_call x0 -> x4, Pallas kernels: none -> 223 us  [the longest x1 100 us: attention_backward(): pl.pallas_call(lambda *refs: backward_kernel(ring, *refs), out_shape=(sha...]
    dot_general x61 -> x9, matrix products: 196 us -> 32.4 us  [mm(): return lax.dot_general(left, right, dims, preferred_element_type=F32)]
    ppermute x60 -> x0, waiting for transfers between devices: 139 us -> none  [shifted(): return lax.ppermute(value, axis, pairs)]
    ppermute x60 -> x0, starting transfers between devices: 116 us -> none  [shifted(): return lax.ppermute(value, axis, pairs)]
    while x61 -> x0, local copies, waits for them, and re-layouts: 59.4 us -> none
    all_gather x8 -> x0, blocking collectives: 27.3 us -> none  [the longest x1 3.73 us: on_device(): lax.all_gather(params[1], 'shard', axis=0, tiled=True)]
    and x17 -> x0, other arithmetic: 22.9 us -> none  [visible(): jnp.logical_and(causal[None], query_docs[:, :, None] == key_docs[:, None,...]
  transfers between devices with their start and end apart: 71 -> 5, of which waited for: 26 -> 5; matrix products, arithmetic and copies ran while one was open for 8% -> 3% of each run, Pallas kernels for 0% -> 0%
where the time goes in v1:
time: 662 us; the launch traced here: 660 us
  waiting for transfers between devices  260 us (39%)
  Pallas kernels  223 us (34%)
  blocking collectives  65.2 us (10%)
  local copies, waits for them, and re-layouts  44.7 us (7%)
  matrix products  32.4 us (5%)
  other arithmetic  17.9 us (3%)
  between operations  16.3 us (2%)
    reduce_scatter x3, waiting for transfers between devices, total(): lax.psum_scatter(value.astype(BF16), 'shard', scatter_dimension=0, tiled=...  147 us
    pallas_call x1, Pallas kernels, attention_backward(): pl.pallas_call(lambda *refs: backward_kernel(ring, *refs), out_shape=(sha...  100 us
    psum x1, waiting for transfers between devices, total(): return lax.psum(part, 'rep').astype(F32)  81.4 us
    pallas_call x1, Pallas kernels, gather_all(): pl.pallas_call(lambda *refs: gather_kernel(ring, shards, parts, *refs), o...  70.5 us
    psum x1, blocking collectives, total(): return lax.psum(part, 'rep').astype(F32)  59.8 us
    pallas_call x1, Pallas kernels, attention_forward(): pl.pallas_call(lambda *refs: forward_kernel(members, *refs), out_shape=(s...  41.9 us
    unnamed x6, waiting for transfers between devices  32.4 us
    dot_general x9, matrix products, mm(): return lax.dot_general(left, right, dims, preferred_element_type=F32)  32.4 us
  transfers between devices with their start and end apart: 5, of which 5 were waited for; matrix products, arithmetic and copies ran while one was open for 3% of the time, Pallas kernels for 0%

profile of v1, /device:TPU:1, one launch (start us, length us, event | category | flops | bytes accessed | tf_op | source)
XLA Modules:
  0.0 660.2 jit_solution(11077617983897909306)
XLA Ops:
  7.3 0.9 dynamic-update-slice
  8.1 0.9 dynamic-update-slice.1
  9.0 0.9 dynamic-update-slice.2
  9.9 0.9 dynamic-update-slice.3
  10.7 0.9 dynamic-update-slice.4
  11.6 0.9 dynamic-update-slice.5
  12.4 0.9 dynamic-update-slice.6
  13.3 0.9 dynamic-update-slice.7
  14.2 0.6 fusion.34
  14.8 1.4 constant_dynamic-slice_fusion.2
  16.2 0.9 pad_maximum_fusion.refs_1_
  17.1 70.5 %shard_map.263 = (bf16[16,256,768]{2,1,0:T(8,128)(2,1)}, bf16[2,384,576]{2,1,0:T(8,128)(2,1)}, bf16[2,64,128]{2,1,0:T(8,128)(2,1)}, bf16[2,384,768]{2,1,0:T(8,12...) custom-call(bf16[256,768]{1,0:T(8,128)(2,1)} %bitcast.63, ...), custom_call_target="tpu_custom_call" | custom-call | tf_op jit(solution)/shard_map/pallas_call | solution.py:268
  87.6 0.8 copy.49
  88.7 0.6 fusion.33
  89.3 0.6 add.192
  89.9 0.6 add.189
  90.5 1.7 bitcast_dynamic-update-slice_fusion.1
  92.2 0.6 add.181
  92.8 1.0 bitcast_dynamic-update-slice_fusion.3
  93.8 2.2 copy.44
  96.1 0.8 reshape.167.refs_2_
  96.9 0.6 convert_element_type.117
  97.6 41.9 %shard_map.264 = (f32[4,192,256]{2,1,0:T(8,128)}, bf16[4,192,256]{2,1,0:T(8,128)(2,1)}, f32[4,3,1,256]{3,2,1,0:T(1,128)}, bf16[4,3,128,256]{3,2,1,0:T(8,128)(2,1...) custom-call(bf16[4096,768]{1,0:T(8,128)(2,1)} %bitcast.54, ...), custom_call_target="tpu_custom_call" | custom-call | tf_op jit(solution)/shard_map/pallas_call | solution.py:97
  139.5 10.7 %shard_map.265 = bf16[4,192,256]{2,1,0:T(8,128)(2,1)} custom-call(bf16[4,192,256]{2,1,0:T(8,128)(2,1)} %get-tuple-element.33.refs_0_), custom_call_target="tpu_custom_call" | custom-call | tf_op jit(solution)/shard_map/pallas_call | solution.py:305
  150.2 1.9 bitcast_dynamic-update-slice_fusion.2
  152.2 0.7 add.186
  152.8 0.7 mul.141
  153.5 2.1 fusion.36
  155.9 1.6 bitcast_dynamic-update-slice_fusion
  157.5 10.9 %fusion.3 = (bf16[256,3072]{1,0:T(8,128)(2,1)S(1)}, f32[256,3072]{1,0:T(8,128)}) fusion(f32[3072]{0:T(1024)S(1)} %copy-done.33, bf16[768,3072]{1,0:T(8,128)(2,1)} %bitcast.73, f32[256,768]{1,0:T(8,128)S(1)} %get-tuple-element.120, f32[768]{0:T(1024)S(1)} %add.186, f32[768]{0:T(1024)S(1)} %mul.141, f32[256]{0:T(256)S(1)} %add_rsqrt_fusion.1, ...), kind=kOutput, calls=%fused_computation.10 | convolution fusion | flops 1260847104 | bytes 10244096 | tf_op jit(solution)/shard_map/dot_general | solution.py:25
  168.5 1.5 fusion.37
  170.4 1.7 fusion.23
  172.1 0.9 convert_reduce_fusion.1
  173.0 5.5 fusion.38
  178.5 2.2 multiply_reduce_fusion
  180.7 0.9 convert_reduce_fusion
  181.6 0.9 copy-done.2
  182.5 1.3 convolution_convert_fusion.3
  183.8 100.0 %shard_map.266 = (bf16[256,768]{1,0:T(8,128)(2,1)}, bf16[768,576]{1,0:T(8,128)(2,1)}, f32[576,1]{1,0:T(8,128)}) custom-call(bf16[4,192,256]{2,1,0:T(8,128)(2,1)} %bitcast.64, bf16[4,3,128,256]{3,2,1,0:T(8,128)(2,1)} %get-tuple-element.37.refs_1_, bf16[3,4096,128]{2,1,0:T(8,128)(2,1)} %get-tuple-element.38.refs_2_, ...), custom_call_target="tpu_custom_call" | custom-call | tf_op jit(solution)/shard_map/pallas_call | solution.py:454
  283.8 2.2 copy.40
  286.3 0.9 copy-done.10
  287.2 3.8 copy.45
  291.2 1.0 copy-done.3
  292.3 1.5 convolution_convert_fusion.2
  293.9 3.8 convolution_convert_fusion.1
  297.7 1.3 copy-done.8
  299.3 3.6 convolution_convert_fusion
  303.0 32.3 %reduce-scatter.13.cloned.1.call-done = bf16[384,2304]{1,0:T(8,128)(2,1)} async-done(((bf16[768,2304]{1,0:T(8,128)(2,1)}), bf16[384,2304]{1,0:T(8,128)(2,1)}) %reduce-scatter.13.cloned.1.call-update) | async-done | bytes 1769488
  335.3 3.9 copy.46
  339.1 20.9 %reduce-scatter.7.cloned.1.call-done = bf16[384,768]{1,0:T(8,128)(2,1)} async-done(((bf16[768,768]{1,0:T(8,128)(2,1)}), bf16[384,768]{1,0:T(8,128)(2,1)}) %reduce-scatter.7.cloned.1.call-update) | async-done | bytes 589840 | tf_op jit(solution)/shard_map/reduce_scatter | solution.py:604
  360.0 62.9 %reduce-scatter.9.cloned.1.call-done = bf16[384,3072]{1,0:T(8,128)(2,1)} async-done(((bf16[768,3072]{1,0:T(8,128)(2,1)}), bf16[384,3072]{1,0:T(8,128)(2,1)}) %reduce-scatter.9.cloned.1.call-update) | async-done | bytes 2359312 | tf_op jit(solution)/shard_map/reduce_scatter | solution.py:604
  422.9 62.9 %reduce-scatter.11.cloned.1.call-done = bf16[1536,768]{1,0:T(8,128)(2,1)} async-done(((bf16[3072,768]{1,0:T(8,128)(2,1)}), bf16[1536,768]{1,0:T(8,128)(2,1)}) %reduce-scatter.11.cloned.1.call-update) | async-done | bytes 2359312 | tf_op jit(solution)/shard_map/reduce_scatter | solution.py:604
  485.9 0.9 copy-done.12
  487.9 0.6 dynamic-slice
  489.8 5.4 all-reduce.11
  496.5 59.8 %all-reduce.9 = (bf16[768]{0:T(1024)(128)(2,1)S(1)}, bf16[384]{0:T(512)(128)(2,1)S(1)}, bf16[384]{0:T(512)(128)(2,1)S(1)}, bf16[384]{0:T(512)(128)(2,1)S(1)}, bf...) all-reduce(bf16[768]{0:T(1024)(128)(2,1)S(1)} %dynamic-slice.1, ...), channel_id=1, replica_groups=mesh['rep'=16,'shard'=2] {'rep'}, use_global_device_ids=true, to_apply=%region_11.12 | all-reduce | flops 4608 | bytes 18432 | tf_op jit(solution)/shard_map/psum | solution.py:605
  556.3 0.6 convert_element_type.133
  558.6 0.6 convert_element_type.143
  560.9 81.4 %all-reduce.14.cloned.1.call-done = (bf16[384,2304]{0,1:T(8,128)(2,1)}, bf16[384,768]{1,0:T(8,128)(2,1)}, bf16[384,3072]{1,0:T(8,128)(2,1)}, bf16[1536,768]{1,0:T(8,128)(2,1)}) async-done(((bf16[384,2304]{0,1:T(8,128)(2,1)}, bf16[384,768]{1,0:T(8,128)(2,1)}, bf16[384,3072]{1,0:T(8,128)(2,1)}, bf16[1536,768]{1,0:T(8,128)(2,1)}), (bf16[384,2304]{0,1:T(8,128)(2,1)}, bf16[384,768]{1,0:T(8,128)(2,1)}, ...) | async-done | bytes 7077904 | tf_op jit(solution)/shard_map/psum | solution.py:605
  642.4 4.2 copy.43
  646.5 1.1 convert_element_type.135
  647.6 2.8 convert_element_type.142
  650.4 2.5 convert_element_type.145
  652.9 0.7 copy.70
  (143 shorter events, 7.2 us)
Async XLA Ops:
  7.2 328.1 %reduce-scatter.13.cloned.1.call-start = ((), (), s32[]{:S(2)}) async-start(), calls=%async_computation.7 | async-start | bytes 5308416
  17.1 73.4 %copy-start.4 = (bf16[384,3072]{1,0:T(8,128)(2,1)S(1)}, bf16[384,3072]{1,0:T(8,128)(2,1)}, u32[]{:S(2)}) copy-start(bf16[384,3072]{1,0:T(8,128)(2,1)} %refs_4_.1) | copy-start | bytes 7077892
  90.5 6.4 copy-start.28
  139.5 16.4 %copy-start.5 = (bf16[1536,768]{1,0:T(8,128)(2,1)S(1)}, bf16[1536,768]{1,0:T(8,128)(2,1)}, u32[]{:S(2)}) copy-start(bf16[1536,768]{1,0:T(8,128)(2,1)} %refs_5_.1) | copy-start | bytes 7077892
  152.8 15.6 %copy-start.24 = (f32[768]{0:T(1024)}, f32[768]{0:T(1024)S(1)}, u32[]{:S(2)}) copy-start(f32[768]{0:T(1024)S(1)} %add.186) | copy-start | bytes 9220
  153.5 27.2 %copy-start.22 = (f32[768]{0:T(1024)}, f32[768]{0:T(1024)S(1)}, u32[]{:S(2)}) copy-start(f32[768]{0:T(1024)S(1)} %mul.141) | copy-start | bytes 9220
  155.6 25.1 %copy-start = (f32[256,768]{1,0:T(8,128)}, f32[256,768]{1,0:T(8,128)S(1)}, u32[]{:S(2)}) copy-start(f32[256,768]{1,0:T(8,128)S(1)} %get-tuple-element.120) | copy-start | bytes 2359300
  155.6 1.9 copy-start.33
  155.6 25.1 %copy-start.26 = (f32[256]{0:T(256)}, f32[256]{0:T(256)S(1)}, u32[]{:S(2)}) copy-start(f32[256]{0:T(256)S(1)} %broadcast_multiply_fusion.5) | copy-start | bytes 3076
  155.9 24.9 %copy-start.29 = (f32[256]{0:T(256)}, f32[256]{0:T(256)S(1)}, u32[]{:S(2)}) copy-start(f32[256]{0:T(256)S(1)} %add_rsqrt_fusion.1) | copy-start | bytes 3076
  157.5 10.9 %copy-start.38 = (f32[768]{0:T(1024)S(1)}, f32[768]{0:T(1024)}, u32[]{:S(2)}) copy-start(f32[768]{0:T(1024)} %add.192) | copy-start | bytes 9220
  157.5 10.9 %copy-start.41 = (bf16[2,1536,768]{2,1,0:T(8,128)(2,1)S(1)}, bf16[2,1536,768]{2,1,0:T(8,128)(2,1)}, u32[]{:S(2)}) copy-start(bf16[2,1536,768]{2,1,0:T(8,128)(2,1)} %bitcast_dynamic-update-slice_fusion) | copy-start | bytes 14155780
  168.5 1.6 copy-start.7
  168.5 1.8 copy-start.32
  168.5 1.8 copy-start.31
  168.5 1.8 copy-start.11
  170.3 2.6 copy-start.43
  172.1 6.4 slice-start
  173.0 5.5 copy-start.13
  173.0 5.5 slice-start.1
  178.4 2.3 copy-start.17
  178.5 4.0 copy-start.6
  181.6 0.9 copy-start.2
  286.0 1.2 copy-start.10
  291.0 1.1 copy-start.3
  291.1 1.2 copy-start.9
  291.1 2.8 copy-start.1
  291.1 2.8 copy-start.18
  291.1 2.8 copy-start.23
  291.1 2.8 copy-start.25
  291.1 2.8 copy-start.27
  291.1 2.8 copy-start.30
  291.1 68.9 %reduce-scatter.7.cloned.1.call-start = ((), (), s32[]{:S(2)}) async-start(), calls=%async_computation.4 | async-start | bytes 1769472 | tf_op jit(solution)/shard_map/reduce_scatter | solution.py:604
  293.8 129.1 %reduce-scatter.9.cloned.1.call-start = ((), (), s32[]{:S(2)}) async-start(), calls=%async_computation.5 | async-start | bytes 7077888 | tf_op jit(solution)/shard_map/reduce_scatter | solution.py:604
  297.7 1.4 copy-start.8
  297.7 1.6 copy-start.14
  297.7 188.1 %reduce-scatter.11.cloned.1.call-start = ((), (), s32[]{:S(2)}) async-start(), calls=%async_computation.6 | async-start | bytes 7077888 | tf_op jit(solution)/shard_map/reduce_scatter | solution.py:604
  302.9 339.4 %all-reduce.14.cloned.1.call-start = ((), (), s32[]{:S(2)}) async-start(), calls=%async_computation.8 | async-start | bytes 14155776 | tf_op jit(solution)/shard_map/psum | solution.py:605
  485.8 1.0 copy-start.12
  485.8 1.1 copy-start.21
  485.8 2.1 copy-start.42
  485.8 4.0 copy-start.34
  485.8 4.0 copy-start.35
  485.8 4.0 copy-start.36
  485.8 4.0 copy-start.37
  485.8 4.0 copy-start.39
  485.8 4.0 copy-start.40
  642.4 4.2 copy-start.19
  642.4 5.3 copy-start.16
  647.6 2.8 copy-start.15
  650.4 2.5 copy-start.20
Sparse Core Ops, SparseCore 0:
  291.2 43.9 reduce-scatter.12
  338.2 21.7 reduce-scatter.6
  362.9 59.9 reduce-scatter.8
  425.7 59.9 reduce-scatter.10
  490.2 152.0 all-reduce.13

commit v2 on v1

--- a/solution.py
+++ b/solution.py
@@ -15,6 +15,7 @@
 FAR = 2.0**100
 F32 = jnp.float32
 BF16 = jnp.bfloat16
+LANES = 128
 NN = (((1,), (0,)), ((), ()))
 NT = (((1,), (1,)), ((), ()))
 VMEM_SPEC = pl.BlockSpec(memory_space=pltpu.VMEM)
@@ -483,6 +484,265 @@
     )(grads, q, k, kt, vt, o, lse, x_all, w_group, mid)
 
 
+class Links:
+    def __init__(self, ring, shards):
+        self.ring, self.shards = ring, shards
+        self.r, self.s = lax.axis_index("rep"), lax.axis_index("shard")
+        self.levels = ring // 4
+        self.z, self.c = self.r // 4, lax.rem(self.r, 2)
+        self.y = lax.rem(self.r // 2, 2)
+        self.sib = self.r + 1 - 2 * self.c
+        self.yn = self.r + 2 - 4 * self.y
+        self.others = [lax.rem(self.s + d, shards) for d in range(1, shards)]
+        self.heights = [lax.rem(self.z + d, self.levels) for d in range(1, self.levels)]
+        self.line = lax.rem(self.r, 4)
+
+    def partners(self):
+        return (
+            [(self.sib, self.s, True), (self.yn, self.s, True)]
+            + [(self.r, t, True) for t in self.others]
+            + [(h * 4 + self.line, self.s, True) for h in self.heights]
+        )
+
+
+def add_rows(out, terms):
+    total = terms[0][...].astype(F32)
+    for term in terms[1:]:
+        total = total + term[...].astype(F32)
+    out[...] = total.astype(out.dtype)
+
+
+def reduce_steps(net, slab, out, own, near, side, mate, tall, sems, group):
+    asend, arecv, bsend, brecv, csend, crecv, dsend, drecv, esend, erecv, fsend, frecv, gsend, grecv, lsem = sems
+    r, s, z, y, c = net.r, net.s, net.z, net.y, net.c
+    base = z // group * group
+    zz = lax.rem(z, group)
+    inner = [lax.rem(zz + d, group) for d in range(1, group)]
+    near_copy = lambda: remote(slab(1 - c), near, asend, arecv, net.sib, s)
+    own_copy = lambda: pltpu.make_async_copy(slab(c), own, lsem)
+    across = lambda d: remote(
+        near.at[net.others[d]], side.at[d], bsend.at[d], brecv.at[d], r, net.others[d]
+    )
+    over = lambda: remote(near.at[s, 1 - y], mate, csend, crecv, net.yn, s)
+    along = lambda d: remote(
+        near.at[s, y, inner[d]], tall.at[d], dsend.at[d], drecv.at[d],
+        (base + inner[d]) * 4 + net.line, s,
+    )
+    mine = out.at[c, y, z]
+    spread = lambda d: remote(
+        mine, mine, esend.at[d], erecv.at[d], net.heights[d] * 4 + net.line, s
+    )
+    pair = lambda: remote(out.at[c, y], out.at[c, y], fsend, frecv, net.yn, s)
+    last = lambda: remote(out.at[c], out.at[c], gsend, grecv, net.sib, s)
+    n_side, n_inner, n_tall = len(net.others), len(inner), len(net.heights)
+
+    def step0():
+        near_copy().start()
+        own_copy().start()
+
+    def step1():
+        near_copy().wait_recv()
+        own_copy().wait()
+        for t in range(net.shards):
+            for half in range(2):
+                add_rows(near.at[t, half], [own.at[t, half], near.at[t, half]])
+        for d in range(n_side):
+            across(d).start()
+
+    def step2():
+        for d in range(n_side):
+            across(d).wait_recv()
+        for half in range(2):
+            add_rows(
+                near.at[s, half], [near.at[s, half]] + [side.at[d, half] for d in range(n_side)]
+            )
+        over().start()
+
+    def step3():
+        over().wait_recv()
+        add_rows(near.at[s, y], [near.at[s, y], mate])
+        for d in range(n_inner):
+            along(d).start()
+
+    def step4():
+        for d in range(n_inner):
+            along(d).wait_recv()
+        add_rows(mine, [near.at[s, y, zz]] + [tall.at[d] for d in range(n_inner)])
+        for d in range(n_tall):
+            spread(d).start()
+
+    def step5():
+        for d in range(n_tall):
+            spread(d).wait_recv()
+        pair().start()
+
+    def step6():
+        pair().wait_recv()
+        last().start()
+
+    def step7():
+        last().wait_recv()
+
+    def drain():
+        near_copy().wait_send()
+        for d in range(n_side):
+            across(d).wait_send()
+        over().wait_send()
+        for d in range(n_inner):
+            along(d).wait_send()
+        for d in range(n_tall):
+            spread(d).wait_send()
+        pair().wait_send()
+        last().wait_send()
+
+    return [step0, step1, step2, step3, step4, step5, step6, step7], drain
+
+
+def reduce_scratch(shards, levels, group, rows, cols):
+    dma = pltpu.SemaphoreType.DMA
+    vmem = pltpu.VMEM
+    many = lambda n: dma((max(n, 1),))
+    buffers = [
+        vmem((shards, 2, group, rows, cols), BF16),
+        vmem((shards, 2, group, rows, cols), BF16),
+        vmem((max(shards - 1, 1), 2, group, rows, cols), BF16),
+        vmem((group, rows, cols), BF16),
+        vmem((max(group - 1, 1), rows, cols), BF16),
+    ]
+    sems = [
+        dma(()), dma(()), many(shards - 1), many(shards - 1), dma(()), dma(()),
+        many(group - 1), many(group - 1), many(levels - 1), many(levels - 1),
+        dma(()), dma(()), dma(()), dma(()), dma(()),
+    ]
+    return buffers + sems
+
+
+SCRATCH = 20
+
+
+def small_steps(net, src, out, near, side, mate, tall, sems):
+    asend, arecv, bsend, brecv, csend, crecv, dsend, drecv = sems
+    r, s, z, y, c = net.r, net.s, net.z, net.y, net.c
+    near_copy = lambda: remote(src, near.at[1], asend, arecv, net.sib, s)
+    across = lambda d: remote(
+        near.at[0, net.others[d]], side.at[s], bsend.at[d], brecv.at[d], r, net.others[d]
+    )
+    over = lambda: remote(mate.at[0], mate.at[1], csend, crecv, net.yn, s)
+    along = lambda d: remote(
+        tall.at[z], tall.at[z], dsend.at[d], drecv.at[d], net.heights[d] * 4 + net.line, s
+    )
+
+    def step0():
+        near_copy().start()
+
+    def step1():
+        near_copy().wait_recv()
+        near[0] = src[...] + near[1]
+        side[s] = near[0, s]
+        for d in range(len(net.others)):
+            across(d).start()
+
+    def step2():
+        for d in range(len(net.others)):
+            across(d).wait_recv()
+        total = side[0]
+        for t in range(1, net.shards):
+            total = total + side[t]
+        mate[0] = total
+        over().start()
+
+    def step3():
+        over().wait_recv()
+        tall[z] = mate[0] + mate[1]
+        for d in range(len(net.heights)):
+            along(d).start()
+
+    def step4():
+        for d in range(len(net.heights)):
+            along(d).wait_recv()
+        total = tall[0]
+        for t in range(1, net.levels):
+            total = total + tall[t]
+        out[...] = total
+
+    def drain():
+        near_copy().wait_send()
+        for d in range(len(net.others)):
+            across(d).wait_send()
+        over().wait_send()
+        for d in range(len(net.heights)):
+            along(d).wait_send()
+
+    return [step0, step1, step2, step3, step4], drain
+
+
+def small_scratch(shards, levels, rows):
+    dma = pltpu.SemaphoreType.DMA
+    vmem = pltpu.VMEM
+    return [
+        vmem((2, shards, rows, LANES), F32), vmem((shards, rows, LANES), F32),
+        vmem((2, rows, LANES), F32), vmem((levels, rows, LANES), F32),
+        dma(()), dma(()), dma((max(shards - 1, 1),)), dma((max(shards - 1, 1),)),
+        dma(()), dma(()), dma((levels - 1,)), dma((levels - 1,)),
+    ]
+
+
+def run_steps(jobs):
+    deepest = max(at + len(steps) for at, (steps, _) in enumerate(jobs))
+    for tick in range(deepest):
+        for at in range(len(jobs)):
+            steps = jobs[at][0]
+            if 0 <= tick - at < len(steps):
+                steps[tick - at]()
+    for _, drain in jobs:
+        drain()
+
+
+def total_kernel(ring, shards, specs, *refs):
+    n_in = 1 + max(spec[0] for spec in specs)
+    terms, small, outs, small_out = refs[:n_in], refs[n_in], refs[n_in + 1 : 2 * n_in + 1], refs[2 * n_in + 1]
+    rest = refs[2 * n_in + 2 :]
+    net = Links(ring, shards)
+    hello(net.partners())
+    jobs = []
+    for number, (which, k, core_first, group) in enumerate(specs):
+        scratch = rest[number * SCRATCH : (number + 1) * SCRATCH]
+        ref = terms[which]
+        if core_first:
+            slab = lambda core, ref=ref, k=k: ref.at[k, core]
+        else:
+            slab = lambda core, ref=ref, k=k: ref.at[:, k, core]
+        jobs.append(reduce_steps(net, slab, outs[which].at[k], *scratch[:5], scratch[5:], group))
+    scratch = rest[len(specs) * SCRATCH :]
+    jobs.insert(1, small_steps(net, small, small_out, *scratch[:4], scratch[4:]))
+    run_steps(jobs)
+
+
+def total_all(terms, orders, groups, small, ring, shards, ident):
+    shape = jax.ShapeDtypeStruct
+    levels = ring // 4
+    specs, scratch, out_shape = [], [], []
+    for i, (term, core_first, group) in enumerate(zip(terms, orders, groups)):
+        chunks = term.shape[0] if core_first else term.shape[1]
+        rows, cols = term.shape[-2:]
+        out_shape.append(shape((chunks, 2, 2, levels, rows, cols), BF16))
+        for k in range(chunks):
+            specs.append((i, k, core_first, group))
+            scratch += reduce_scratch(shards, levels, group, rows, cols)
+    scratch += small_scratch(shards, levels, small.shape[1])
+    out_shape.append(shape(small.shape[1:], F32))
+    return pl.pallas_call(
+        lambda *refs: total_kernel(ring, shards, specs, *refs),
+        out_shape=tuple(out_shape),
+        in_specs=[ANY_SPEC] * len(terms) + [VMEM_SPEC],
+        out_specs=(VMEM_SPEC,) * (len(terms) + 1),
+        scratch_shapes=scratch,
+        compiler_params=pltpu.CompilerParams(
+            collective_id=ident, has_side_effects=True, vmem_limit_bytes=VMEM_LIMIT
+        ),
+    )(*terms, small)
+
+
 def layer_norm(hidden, gain, shift):
     centre = hidden - jnp.mean(hidden, axis=-1, keepdims=True)
     inverse = lax.rsqrt(jnp.mean(centre * centre, axis=-1, keepdims=True) + EPSILON)
@@ -589,36 +849,49 @@
         ring, grad_attended_t.reshape(GROUPS, SLAB, BLOCK), q, k, kt, vt, o, lse,
         x_all.reshape(ring, BLOCK, width), w_group, grad_mid_in, 2,
     )
-    dw_group = dw_group.astype(F32)
-
-    place = jnp.zeros((width, 3, GROUPS, SLAB), F32)
-    grad_qkv = lax.dynamic_update_slice_in_dim(
-        place, dw_group.reshape(width, 3, 1, SLAB), g, 2
-    ).reshape(width, 3 * width)
+
+    levels = ring // 4
+    sub = levels // GROUPS
+    hidden = up_weight.shape[1]
+    down_chunks = 6 if down_weight.shape[0] % (6 * ring * 16) == 0 else 1
+    down_terms = grad_down_weight.astype(BF16).reshape(
+        shards, down_chunks, 2, 2, levels, -1, width
+    )
+    up_chunks = 6
+    up_terms = grad_up_weight.astype(BF16).reshape(width, up_chunks, 2, -1).transpose(1, 2, 0, 3)
+    up_terms = up_terms.reshape(up_chunks, 2, shards, 2, levels, -1, hidden // up_chunks // 2)
+    out_terms = grad_out_weight.astype(BF16).reshape(width, 1, 2, -1).transpose(1, 2, 0, 3)
+    out_terms = out_terms.reshape(1, 2, shards, 2, levels, -1, width // 2)
+    qkv_terms = dw_group.reshape(shards, 1, 2, 2, sub, -1, 3 * SLAB)
     qv = dbias.reshape(3, SLAB)[jnp.array([0, 2])]
     grad_qv_bias = lax.dynamic_update_slice_in_dim(
         jnp.zeros((2, GROUPS, SLAB), F32), qv.reshape(2, 1, SLAB), g, 1
     ).reshape(2 * width)
-
-    def total(value):
-        part = lax.psum_scatter(value.astype(BF16), "shard", scatter_dimension=0, tiled=True)
-        return lax.psum(part, "rep").astype(F32)
-
+    vectors = (
+        grad_qv_bias, grad_out_bias, grad_mid_gain, grad_mid_shift, grad_up_bias, grad_down_bias,
+        grad_end_gain, grad_end_shift,
+    )
+    flat = jnp.concatenate([v.reshape(shards, -1) for v in vectors], axis=1)
+    flat = jnp.pad(flat, ((0, 0), (0, -flat.shape[1] % (8 * LANES)))).reshape(shards, -1, LANES)
+    down, up, out, qkv, flat = total_all(
+        (down_terms, up_terms, out_terms, qkv_terms), (False, True, True, False),
+        (levels, levels, levels, sub), flat, ring, shards, 3,
+    )
+    total_down = down.reshape(-1, width).astype(F32)
+    total_up = up.reshape(up_chunks * 2, width // shards, -1).transpose(1, 0, 2)
+    total_up = total_up.reshape(-1, hidden).astype(F32)
+    total_out = out.reshape(2, width // shards, -1).transpose(1, 0, 2)
+    total_out = total_out.reshape(-1, width).astype(F32)
+    total_qkv = qkv.reshape(2, 2, GROUPS, sub, -1, 3, SLAB).transpose(0, 1, 3, 4, 5, 2, 6)
+    total_qkv = total_qkv.reshape(-1, 3 * width).astype(F32)
+    flat = flat.reshape(-1)
+    totals, at = [], 0
+    for size in sizes:
+        totals.append(flat[at : at + size])
+        at += size
     return (
-        layer_out[None],
-        input_grad[None],
-        total(grad_qkv),
-        total(grad_qv_bias),
-        total(grad_out_weight),
-        total(grad_out_bias),
-        total(grad_mid_gain),
-        total(grad_mid_shift),
-        total(grad_up_weight),
-        total(grad_up_bias),
-        total(grad_down_weight),
-        total(grad_down_bias),
-        total(grad_end_gain),
-        total(grad_end_shift),
+        layer_out[None], input_grad[None], total_qkv, totals[0], total_out, totals[1], totals[2],
+        totals[3], total_up, totals[4], total_down, totals[5], totals[6], totals[7],
     )
 
 

time: 662 us -> 483 us (0.73)
  waiting for transfers between devices: 260 us -> 0 us
  Pallas kernels: 223 us -> 345 us
  blocking collectives: 65.2 us -> 0 us
  local copies, waits for them, and re-layouts: 44.7 us -> 82.8 us
  between operations: 16.3 us -> 1.6 us
    reduce_scatter x3 -> x0, waiting for transfers between devices: 147 us -> none  [total(): lax.psum_scatter(value.astype(BF16), 'shard', scatter_dimension=0, tiled=...]
    pallas_call x0 -> x1, Pallas kernels: none -> 122 us  [total_all(): pl.pallas_call(lambda *refs: total_kernel(ring, shards, specs, *refs), ou...]
    psum x1 -> x0, waiting for transfers between devices: 81.4 us -> none  [total(): return lax.psum(part, 'rep').astype(F32)]
    psum x1 -> x0, blocking collectives: 59.8 us -> none  [total(): return lax.psum(part, 'rep').astype(F32)]
    unnamed x6 -> x0, waiting for transfers between devices: 32.4 us -> none
    reshape x1 -> x10, local copies, waits for them, and re-layouts: 2.19 us -> 22.8 us  [the longest x2 17.2 us: on_device(): grad_up_weight.astype(BF16).reshape(width, up_chunks, 2, -1)]
    convert_element_type x1 -> x5, local copies, waits for them, and re-layouts: 0.09 us -> 20 us  [the longest x3 15.9 us: on_device(): total_qkv = total_qkv.reshape(-1, 3 * width).astype(F32)]
    convert_element_type x11 -> x1, other arithmetic: 11.1 us -> 2.7 us  [on_device(): total_down = down.reshape(-1, width).astype(F32)]
  transfers between devices with their start and end apart: 5 -> 0, of which waited for: 5 -> 0; matrix products, arithmetic and copies ran while one was open for 3% -> 0% of each run, Pallas kernels for 0% -> 0%
where the time goes in v2:
time: 483 us; the launch traced here: 477 us
  Pallas kernels  345 us (71%)
  local copies, waits for them, and re-layouts  82.8 us (17%)
  matrix products  35.7 us (7%)
  other arithmetic  12.2 us (3%)
    pallas_call x1, Pallas kernels, total_all(): pl.pallas_call(lambda *refs: total_kernel(ring, shards, specs, *refs), ou...  122 us
    pallas_call x1, Pallas kernels, attention_backward(): pl.pallas_call(lambda *refs: backward_kernel(ring, *refs), out_shape=(sha...  100 us
    pallas_call x1, Pallas kernels, gather_all(): pl.pallas_call(lambda *refs: gather_kernel(ring, shards, parts, *refs), o...  70.5 us
    pallas_call x1, Pallas kernels, attention_forward(): pl.pallas_call(lambda *refs: forward_kernel(members, *refs), out_shape=(s...  42.1 us
    dot_general x9, matrix products, mm(): return lax.dot_general(left, right, dims, preferred_element_type=F32)  35.7 us
    unnamed x85, local copies, waits for them, and re-layouts  19.7 us
    reshape x2, local copies, waits for them, and re-layouts, on_device(): grad_up_weight.astype(BF16).reshape(width, up_chunks, 2, -1)  17.2 us
    convert_element_type x3, local copies, waits for them, and re-layouts, on_device(): total_qkv = total_qkv.reshape(-1, 3 * width).astype(F32)  15.9 us

profile of v2, /device:TPU:1, one launch (start us, length us, event | category | flops | bytes accessed | tf_op | source)
XLA Modules:
  0.0 477.1 jit_solution(2795497074858942400)
XLA Ops:
  1.3 1.1 convert_reduce_fusion.1
  3.0 0.8 dynamic-update-slice.8
  3.8 0.9 dynamic-update-slice.9
  4.7 0.9 dynamic-update-slice.10
  5.5 0.9 dynamic-update-slice.11
  6.4 0.9 dynamic-update-slice.12
  7.3 0.9 dynamic-update-slice.13
  8.1 0.9 dynamic-update-slice.14
  9.0 0.9 dynamic-update-slice.15
  9.8 1.3 convert_element_type.105
  11.2 0.6 fusion.36
  11.8 1.4 constant_dynamic-slice_fusion.2
  13.2 0.9 pad_maximum_fusion.refs_1_
  14.2 70.5 %shard_map.263 = (bf16[16,256,768]{2,1,0:T(8,128)(2,1)}, bf16[2,384,576]{2,1,0:T(8,128)(2,1)}, bf16[2,64,128]{2,1,0:T(8,128)(2,1)}, bf16[2,384,768]{2,1,0:T(8,12...) custom-call(bf16[256,768]{1,0:T(8,128)(2,1)} %bitcast.123, ...), custom_call_target="tpu_custom_call" | custom-call | tf_op jit(solution)/shard_map/pallas_call | solution.py:269
  84.6 0.9 bitcast_dynamic-update-slice_fusion.3
  85.6 2.2 copy.56
  87.8 0.8 copy.63
  88.8 1.7 bitcast_dynamic-update-slice_fusion
  90.5 0.8 copy-done.4
  91.3 1.6 bitcast_dynamic-update-slice_fusion.1
  92.9 0.9 bitcast_dynamic-update-slice_fusion.2
  94.0 0.6 add.142
  98.2 0.8 reshape.244.refs_2_
  99.0 42.1 %shard_map.264 = (f32[4,192,256]{2,1,0:T(8,128)}, bf16[4,192,256]{2,1,0:T(8,128)(2,1)}, f32[4,3,1,256]{3,2,1,0:T(1,128)}, bf16[4,3,128,256]{3,2,1,0:T(8,128)(2,1...) custom-call(bf16[4096,768]{1,0:T(8,128)(2,1)} %bitcast.112, ...), custom_call_target="tpu_custom_call" | custom-call | tf_op jit(solution)/shard_map/pallas_call | solution.py:98
  141.1 10.6 %shard_map.265 = bf16[4,192,256]{2,1,0:T(8,128)(2,1)} custom-call(bf16[4,192,256]{2,1,0:T(8,128)(2,1)} %get-tuple-element.38.refs_0_), custom_call_target="tpu_custom_call" | custom-call | tf_op jit(solution)/shard_map/pallas_call | solution.py:306
  151.7 2.2 fusion.38
  154.3 10.8 %fusion.3 = (bf16[256,3072]{1,0:T(8,128)(2,1)S(1)}, f32[256,3072]{1,0:T(8,128)}) fusion(f32[3072]{0:T(1024)S(1)} %copy-done.27, bf16[768,3072]{1,0:T(8,128)(2,1)} %bitcast.135, f32[256,768]{1,0:T(8,128)S(1)} %get-tuple-element.116, f32[768]{0:T(1024)S(1)} %copy-done.19, f32[768]{0:T(1024)S(1)} %copy-done.17, f32[256]{0:T(256)S(1)} %add_rsqrt_fusion.1, ...), kind=kOutput, calls=%fused_computation.10 | convolution fusion | flops 1260847104 | bytes 10244096 | tf_op jit(solution)/shard_map/dot_general | solution.py:26
  165.2 1.5 fusion.39
  168.0 1.1 convert_reduce_fusion.2
  169.1 7.1 %convert_reduce_fusion = (f32[3072]{0:T(1024)S(1)}, bf16[256,3072]{1,0:T(8,128)(2,1)S(1)}) fusion(f32[256,3072]{1,0:T(8,128)} %get-tuple-element.118, bf16[3072,768]{1,0:T(8,128)(2,1)} %bitcast.139, f32[256,768]{1,0:T(8,128)S(1)} %get-tuple-element.92), kind=kOutput, calls=%fused_computation.15 | convolution fusion | flops 1217590272 | bytes 10235904 | tf_op jit(solution)/shard_map/dot_general | solution.py:26
  176.3 2.2 multiply_reduce_fusion
  178.5 0.6 reshape.223
  180.6 0.9 copy-done.2
  181.5 2.5 convolution_convert_fusion.3
  184.6 100.0 %shard_map.266 = (bf16[256,768]{1,0:T(8,128)(2,1)}, bf16[768,576]{1,0:T(8,128)(2,1)}, f32[576,1]{1,0:T(8,128)}) custom-call(bf16[4,192,256]{2,1,0:T(8,128)(2,1)} %bitcast.124, bf16[4,3,128,256]{3,2,1,0:T(8,128)(2,1)} %get-tuple-element.42.refs_1_, bf16[3,4096,128]{2,1,0:T(8,128)(2,1)} %get-tuple-element.43.refs_2_, ...), custom_call_target="tpu_custom_call" | custom-call | tf_op jit(solution)/shard_map/pallas_call | solution.py:455
  284.7 1.9 convolution_convert_fusion.2
  286.6 1.4 copy.49
  288.1 0.7 reshape.222
  288.7 1.1 reduce.1
  290.0 0.7 gather_fusion
  290.8 0.7 constant_dynamic-update-slice_fusion.6
  291.5 0.7 constant_dynamic-update-slice_fusion.5
  292.2 0.7 constant_dynamic-update-slice_fusion.3
  292.9 0.7 constant_dynamic-update-slice_fusion.2
  293.6 0.7 constant_dynamic-update-slice_fusion.1
  294.3 0.7 constant_dynamic-update-slice_fusion
  294.9 0.6 copy.62
  295.6 3.8 convolution_convert_fusion
  299.4 11.9 %reshape.213 = bf16[768,6,2,256]{3,2,1,0:T(2,128)(2,1)} reshape(bf16[768,3072]{1,0:T(8,128)(2,1)} %convolution_convert_fusion) | data formatting | bytes 9437184 | tf_op jit(solution)/shard_map/reshape | solution.py:861
  311.2 5.3 %copy.48 = bf16[768,6,2,256]{3,0,2,1:T(8,128)(2,1)} copy(bf16[768,6,2,256]{3,2,1,0:T(2,128)(2,1)} %reshape.213) | data formatting | bytes 9437184 | tf_op jit(solution)/shard_map/reshape | solution.py:861
  316.5 3.6 convolution_convert_fusion.1
  320.2 121.6 %shard_map.267 = (bf16[6,2,2,4,16,768]{5,4,3,2,1,0:T(8,128)(2,1)}, bf16[6,2,2,4,48,256]{5,4,3,2,1,0:T(8,128)(2,1)}, bf16[1,2,2,4,48,384]{5,4,3,2,1,0:T(8,128)(2,...) custom-call(bf16[2,6,2,2,4,16,768]{6,5,4,3,2,1,0:T(8,128)(2,1)} %bitcast.111, ...), custom_call_target="tpu_custom_call" | custom-call | tf_op jit(solution)/shard_map/pallas_call | solution.py:734
  441.8 1.4 slice_bitcast_fusion.1
  443.2 1.3 slice_bitcast_fusion
  444.5 1.4 slice_bitcast_fusion.2
  445.9 1.1 convert_bitcast_fusion
  447.1 1.1 copy.57
  448.2 3.0 copy.51
  451.2 6.8 %copy.52 = f32[2,2,1,96,3,4,192]{6,5,4,3,1,0,2:T(4,128)} copy(f32[2,2,1,96,3,4,192]{3,6,4,5,1,0,2:T(8,128)} %bitcast.114) | data formatting | bytes 7077888 | tf_op jit(solution)/shard_map/convert_element_type | solution.py:886
  458.0 6.1 %reshape.228 = f32[384,2304]{1,0:T(8,128)} reshape(f32[2,2,1,96,3,4,192]{6,5,4,3,1,0,2:T(4,128)} %copy.52) | data formatting | bytes 7077888 | tf_op jit(solution)/shard_map/convert_element_type | solution.py:886
  464.1 2.9 copy.54
  467.1 6.2 %copy.55 = f32[384,3072]{1,0:T(8,128)} copy(f32[384,3072]{0,1:T(8,128)} %bitcast.115) | data formatting | bytes 9437184
  473.3 2.7 bitcast_convert_fusion
  476.0 0.7 copy.86
  (107 shorter events, 9.2 us)
Async XLA Ops:
  14.2 74.6 %copy-start.3 = (bf16[1536,768]{1,0:T(8,128)(2,1)S(1)}, bf16[1536,768]{1,0:T(8,128)(2,1)}, u32[]{:S(2)}) copy-start(bf16[1536,768]{1,0:T(8,128)(2,1)} %refs_5_.1) | copy-start | bytes 7077892
  88.8 2.5 copy-start.4
  90.5 2.4 copy-start.10
  141.1 13.2 %copy-start.17 = (f32[768]{0:T(1024)S(1)}, f32[768]{0:T(1024)}, u32[]{:S(2)}) copy-start(f32[768]{0:T(1024)} %mul.141) | copy-start | bytes 9220
  141.1 13.2 %copy-start.19 = (f32[768]{0:T(1024)S(1)}, f32[768]{0:T(1024)}, u32[]{:S(2)}) copy-start(f32[768]{0:T(1024)} %add.139) | copy-start | bytes 9220
  141.1 13.2 %copy-start.27 = (f32[3072]{0:T(1024)S(1)}, f32[3072]{0:T(1024)}, u32[]{:S(2)}) copy-start(f32[3072]{0:T(1024)} %add.142) | copy-start | bytes 36868
  151.7 13.4 %slice-start.2 = ((s8[4718592]{0:T(1024)(128)(4,1)}), s8[4194304]{0:T(1024)(128)(4,1)S(1)}, s32[]{:S(2)}) async-start(s8[4718592]{0:T(1024)(128)(4,1)} %bitcast.140), calls=%async_computation.2 | async-start | bytes 8388608
  154.0 26.3 %copy-start = (f32[256,768]{1,0:T(8,128)}, f32[256,768]{1,0:T(8,128)S(1)}, u32[]{:S(2)}) copy-start(f32[256,768]{1,0:T(8,128)S(1)} %get-tuple-element.116) | copy-start | bytes 2359300
  154.0 26.3 %copy-start.22 = (f32[256]{0:T(256)}, f32[256]{0:T(256)S(1)}, u32[]{:S(2)}) copy-start(f32[256]{0:T(256)S(1)} %broadcast_multiply_fusion.5) | copy-start | bytes 3076
  154.2 26.0 %copy-start.25 = (f32[256]{0:T(256)}, f32[256]{0:T(256)S(1)}, u32[]{:S(2)}) copy-start(f32[256]{0:T(256)S(1)} %add_rsqrt_fusion.1) | copy-start | bytes 3076
  154.3 10.9 %copy-start.28 = (f32[768]{0:T(1024)S(1)}, f32[768]{0:T(1024)}, u32[]{:S(2)}) copy-start(f32[768]{0:T(1024)} %add.145) | copy-start | bytes 9220
  154.3 10.9 %slice-start.3 = ((s8[4718592]{0:T(1024)(128)(4,1)}), s8[524288]{0:T(1024)(128)(4,1)S(1)}, s32[]{:S(2)}) async-start(s8[4718592]{0:T(1024)(128)(4,1)} %bitcast.140), calls=%async_computation.3 | async-start | bytes 1048576
  165.1 1.6 copy-start.5
  165.1 1.8 copy-start.7
  165.2 1.8 copy-start.21
  165.2 2.8 copy-start.24
  168.0 8.2 %slice-start = ((s8[4718592]{0:T(1024)(128)(4,1)}), s8[4194304]{0:T(1024)(128)(4,1)S(1)}, s32[]{:S(2)}) async-start(s8[4718592]{0:T(1024)(128)(4,1)} %bitcast.136), calls=%async_computation | async-start | bytes 8388608
  169.1 7.1 %copy-start.8 = (f32[256,768]{1,0:T(8,128)}, f32[256,768]{1,0:T(8,128)S(1)}, u32[]{:S(2)}) copy-start(f32[256,768]{1,0:T(8,128)S(1)} %get-tuple-element.92) | copy-start | bytes 2359300
  169.1 7.1 %slice-start.1 = ((s8[4718592]{0:T(1024)(128)(4,1)}), s8[524288]{0:T(1024)(128)(4,1)S(1)}, s32[]{:S(2)}) async-start(s8[4718592]{0:T(1024)(128)(4,1)} %bitcast.136), calls=%async_computation.1 | async-start | bytes 1048576
  176.2 2.3 copy-start.14
  180.6 0.9 copy-start.2
  284.7 10.9 %copy-start.1 = (f32[256,768]{1,0:T(8,128)S(1)}, f32[256,768]{1,0:T(8,128)}, u32[]{:S(2)}) copy-start(f32[256,768]{1,0:T(8,128)} %copy-done) | copy-start | bytes 2359300
  284.7 10.9 %copy-start.15 = (bf16[256,3072]{1,0:T(8,128)(2,1)S(1)}, bf16[256,3072]{1,0:T(8,128)(2,1)}, u32[]{:S(2)}) copy-start(bf16[256,3072]{1,0:T(8,128)(2,1)} %copy-done.14) | copy-start | bytes 4718596
  284.7 10.9 %copy-start.18 = (f32[768]{0:T(1024)S(1)}, f32[768]{0:T(1024)}, u32[]{:S(2)}) copy-start(f32[768]{0:T(1024)} %mul.141) | copy-start | bytes 9220
  284.7 10.9 %copy-start.20 = (f32[768]{0:T(1024)S(1)}, f32[768]{0:T(1024)}, u32[]{:S(2)}) copy-start(f32[768]{0:T(1024)} %add.139) | copy-start | bytes 9220
  284.7 10.9 %copy-start.23 = (f32[256]{0:T(256)S(1)}, f32[256]{0:T(256)}, u32[]{:S(2)}) copy-start(f32[256]{0:T(256)} %copy-done.22) | copy-start | bytes 3076
  284.7 10.9 %copy-start.26 = (f32[256]{0:T(256)S(1)}, f32[256]{0:T(256)}, u32[]{:S(2)}) copy-start(f32[256]{0:T(256)} %copy-done.25) | copy-start | bytes 3076
  311.2 5.3 %copy-start.6 = (bf16[256,3072]{1,0:T(8,128)(2,1)S(1)}, bf16[256,3072]{1,0:T(8,128)(2,1)}, u32[]{:S(2)}) copy-start(bf16[256,3072]{1,0:T(8,128)(2,1)} %copy-done.5) | copy-start | bytes 4718596
  311.2 5.3 %copy-start.9 = (f32[256,768]{1,0:T(8,128)S(1)}, f32[256,768]{1,0:T(8,128)}, u32[]{:S(2)}) copy-start(f32[256,768]{1,0:T(8,128)} %copy-done.8) | copy-start | bytes 2359300
  441.8 6.4 %copy-start.13 = (bf16[1,2,2,4,96,576]{5,4,3,2,1,0:T(8,128)(2,1)S(1)}, bf16[1,2,2,4,96,576]{5,4,3,2,1,0:T(8,128)(2,1)}, u32[]{:S(2)}) copy-start(bf16[1,2,2,4,96,576]{5,4,3,2,1,0:T(8,128)(2,1)} %get-tuple-element.51) | copy-start | bytes 5308420
  458.0 6.1 %copy-start.12 = (bf16[6,2,2,4,48,256]{5,4,3,2,1,0:T(8,128)(2,1)S(1)}, bf16[6,2,2,4,48,256]{5,4,3,2,1,0:T(8,128)(2,1)}, u32[]{:S(2)}) copy-start(bf16[6,2,2,4,48,256]{5,4,3,2,1,0:T(8,128)(2,1)} %get-tuple-element.54) | copy-start | bytes 7077892
  467.1 6.2 %copy-start.11 = (bf16[6,2,2,4,16,768]{5,4,3,2,1,0:T(8,128)(2,1)S(1)}, bf16[6,2,2,4,16,768]{5,4,3,2,1,0:T(8,128)(2,1)}, u32[]{:S(2)}) copy-start(bf16[6,2,2,4,16,768]{5,4,3,2,1,0:T(8,128)(2,1)} %get-tuple-element.55) | copy-start | bytes 7077892
  473.3 2.7 copy-start.16

commit v3 on v2

v3 whole, which is shorter than its diff:
```python
import jax
import jax.numpy as jnp
from jax import lax
from jax.experimental import pallas as pl
from jax.experimental.pallas import tpu as pltpu
from jax.sharding import PartitionSpec as P

HEADS = 12
HEAD_DIM = 64
BLOCK = 256
GROUPS = 4
PER = HEADS // GROUPS
SLAB = PER * HEAD_DIM
EPSILON = 1e-05
FAR = 2.0**100
F32 = jnp.float32
BF16 = jnp.bfloat16
LANES = 128
NN = (((1,), (0,)), ((), ()))
NT = (((1,), (1,)), ((), ()))
TN = (((0,), (0,)), ((), ()))
VMEM_SPEC = pl.BlockSpec(memory_space=pltpu.VMEM)
VMEM_LIMIT = 67043328


def mm(left, right, dims=NN):
    return lax.dot_general(left, right, dims, preferred_element_type=F32)


ANY_SPEC = pl.BlockSpec(memory_space=pl.ANY)


def remote(src, dst, send, recv, rep, shard):
    return pltpu.make_async_remote_copy(
        src_ref=src, dst_ref=dst, send_sem=send, recv_sem=recv,
        device_id=(rep, shard), device_id_type=pl.DeviceIdType.MESH,
    )


def hello(partners):
    barrier = pltpu.get_barrier_semaphore()
    total = 0
    for rep, shard, there in partners:
        if there is True:
            pl.semaphore_signal(
                barrier, inc=1, device_id=(rep, shard), device_id_type=pl.DeviceIdType.MESH
            )
            total = total + 1
        else:

            @pl.when(there)
            def _():
                pl.semaphore_signal(
                    barrier, inc=1, device_id=(rep, shard), device_id_type=pl.DeviceIdType.MESH
                )

            total = total + there.astype(jnp.int32)
    pl.semaphore_wait(barrier, total)


class Links:
    def __init__(self, ring, shards):
        self.ring, self.shards = ring, shards
        self.r, self.s = lax.axis_index("rep"), lax.axis_index("shard")
        self.levels = ring // 4
        self.z, self.c = self.r // 4, lax.rem(self.r, 2)
        self.y = lax.rem(self.r // 2, 2)
        self.sib = self.r + 1 - 2 * self.c
        self.yn = self.r + 2 - 4 * self.y
        self.others = [lax.rem(self.s + d, shards) for d in range(1, shards)]
        self.heights = [lax.rem(self.z + d, self.levels) for d in range(1, self.levels)]
        self.line = lax.rem(self.r, 4)

    def partners(self):
        return (
            [(self.sib, self.s, True), (self.yn, self.s, True)]
            + [(self.r, t, True) for t in self.others]
            + [(h * 4 + self.line, self.s, True) for h in self.heights]
        )


def forward_kernel(ring, shards, parts, sizes, *refs):
    n_vec = len(sizes)
    x_ref, w_ref, docs_ref = refs[:3]
    vec_refs, own = refs[3 : 3 + n_vec], refs[3 + n_vec : 6 + n_vec]
    outs, rest = refs[6 + n_vec : 19 + n_vec], refs[19 + n_vec :]
    att_ref, flat_ref, wg_ref, lse_ref, o_out, q_out, k_out, kt_out, vt_out, xr_out = outs[:10]
    full = outs[10:]
    (
        xa_ref, wl_ref, low_ref, bias_ref, o_ref, q_ref, k_ref, kt_ref, vt_ref, top_ref, sum_ref,
        send, recv, wsend, wrecv, fsend, frecv, vsend, vrecv, asend, arecv, osem,
    ) = rest
    net = Links(ring, shards)
    r, s, z, y, c = net.r, net.s, net.z, net.y, net.c
    levels, members = net.levels, ring // GROUPS
    g, m = r // members, lax.rem(r, members)
    sib, yn, line, others = net.sib, net.yn, net.line, net.others
    above, below = z < levels - 1, z > 0
    hello(net.partners())

    def move(b, kind, src=None):
        target = (r + 4, r - 4, yn, sib)[kind]
        src = xa_ref.at[b] if src is None else src
        return remote(src, xa_ref.at[b], send.at[kind, b], recv.at[b], target, s)

    pl.when(above)(lambda: move(r, 0, x_ref).start())
    pl.when(below)(lambda: move(r, 1, x_ref).start())
    move(r, 2, x_ref).start()
    move(r, 3, x_ref).start()
    xa_ref[r] = x_ref[...]

    width = x_ref.shape[1]
    for k in range(GROUPS):

        @pl.when(g == k)
        def _():
            wl_ref[s] = jnp.concatenate(
                [w_ref[:, t * width + k * SLAB : t * width + (k + 1) * SLAB] for t in range(3)], 1
            )

    flat_ref[s] = jnp.concatenate([v[...].astype(F32) for v in vec_refs], axis=1)
    lists = [
        remote(flat_ref.at[s], flat_ref.at[s], vsend.at[d], vrecv.at[d], r, t)
        for d, t in enumerate(others)
    ]
    pieces = [(lambda rows: wl_ref.at[s, rows], wl_ref, w_ref.shape[0] // 2, 0, False)]
    for w, first, count, quad in parts:
        size = own[w].shape[0] // (4 if quad else 2) // count
        for j in range(count):
            pieces.append((lambda rows, w=w: own[w].at[rows], full[w], size, (count, j), quad))

    def span(piece, yy, cc):
        size, where, quad = piece[2:]
        count, j = where or (1, 0)
        part = (yy * 2 + cc) if quad else cc
        return pl.ds(pl.multiple_of((part * count + j) * size, size), size)

    def across(at, d):
        rows = span(pieces[at], y, c)
        return remote(
            pieces[at][0](rows), pieces[at][1].at[s, rows], wsend.at[at, d], wrecv.at[at, d],
            r, others[d],
        )

    def shifted(at, d, kind, yy, cc, target):
        rows = span(pieces[at], yy, cc)
        spot = pieces[at][1].at[others[d], rows]
        return remote(spot, spot, fsend.at[at, d, kind], frecv.at[at, d, kind], target, s)

    def relay(at):
        for d in range(shards - 1):
            across(at, d).wait_recv()
            shifted(at, d, 0, y, c, sib).start()
            if pieces[at][4]:
                shifted(at, d, 1, y, c, yn).start()

    def relay_far(at):
        for d in range(shards - 1):
            shifted(at, d, 1, 1 - y, c, yn).wait_recv()
            shifted(at, d, 2, 1 - y, c, sib).start()

    def relayed(at):
        for d in range(shards - 1):
            shifted(at, d, 0, y, 1 - c, sib).wait_recv()
            if pieces[at][4]:
                shifted(at, d, 2, 1 - y, 1 - c, sib).wait_recv()

    for copy in lists:
        copy.start()
    for at in range(len(pieces)):
        for d in range(shards - 1):
            across(at, d).start()
    relay(0)
    for copy in lists:
        copy.wait_recv()
    n0 = sizes[0]
    qv = jnp.concatenate([flat_ref[t, :, :n0] for t in range(shards)], axis=1)
    for k in range(GROUPS):

        @pl.when(g == k)
        def _():
            row = jnp.concatenate(
                [qv[:, k * SLAB : (k + 1) * SLAB], qv[:, width + k * SLAB : width + (k + 1) * SLAB]],
                axis=1,
            )
            bias_ref[...] = jnp.broadcast_to(row, (8, 2 * SLAB)).T[:, :1]

    relayed(0)
    part = width // shards
    for t in range(shards):
        wg_ref[:, t * part : (t + 1) * part] = wl_ref[t].astype(F32).T.astype(BF16)

    def level(q):
        lo, hi = z, levels - 1 - z
        turn = jnp.minimum(lo, hi)
        swing = jnp.where(lax.rem(q, 2) == 1, z - (q + 1) // 2, z + q // 2)
        rest = jnp.where(lo > hi, z - (q - turn), z + (q - turn))
        return jnp.where(q <= 2 * turn, swing, rest)

    def event(n):
        k, t = (n - 2) // 4, lax.rem(n + 2, 4)
        q = jnp.where(n < 2, 0, jnp.where(lax.rem(t, 2) == 0, k + 1, k))
        j = jnp.where(n < 2, 2 * n, t)
        q = jnp.where(n >= ring - 2, levels - 1, q)
        j = jnp.where(n >= ring - 2, 2 * (n - ring + 2) + 1, j)
        lv = level(q)
        return lv * 4 + lax.rem(y + lax.rem(j, 2), 2) * 2 + lax.rem(c + j // 2, 2), lv, j

    sub = levels // GROUPS

    def arrive(n):
        b, lv, j = event(n)

        @pl.when(n > 0)
        def _():
            move(b, 3).wait_recv()

            @pl.when(j == 0)
            def _():
                pl.when(jnp.logical_and(lv < z, above))(lambda: move(b, 0).start())
                pl.when(jnp.logical_and(lv > z, below))(lambda: move(b, 1).start())
                move(b, 2).start()

            pl.when(j < 2)(lambda: move(b, 3).start())

        both = mm(wg_ref[SLAB:, :], xa_ref[b], NT)
        kt = both[:SLAB].astype(BF16)
        kt_ref[b] = kt
        vt_ref[b] = (both[SLAB:] + bias_ref[SLAB:, :]).astype(BF16)
        at = pl.multiple_of(b * BLOCK, BLOCK)
        docs = docs_ref[:, pl.ds(at, BLOCK)].astype(F32)
        blank = jnp.zeros((HEAD_DIM - 2, BLOCK), F32)
        extra = jnp.concatenate([docs * FAR - FAR, docs * (-FAR), blank], axis=0)
        for h in range(PER):
            part = kt[h * HEAD_DIM : (h + 1) * HEAD_DIM].astype(F32)
            k_ref[h, pl.ds(at, BLOCK), :] = jnp.concatenate([part, extra], axis=0).T.astype(BF16)

        @pl.when(jnp.logical_and(j == 0, lax.rem(lv, sub) == lax.rem(z, sub)))
        def _():
            i = lv // sub
            qt = (mm(wg_ref[:SLAB, :], xa_ref[b], NT) + bias_ref[:SLAB, :]).astype(BF16)
            qt = qt.astype(F32) * HEAD_DIM ** (-0.5)
            extra = jnp.concatenate([docs, 1.0 - docs, blank], axis=0)
            for h in range(PER):
                part = qt[h * HEAD_DIM : (h + 1) * HEAD_DIM]
                q_ref[i, h] = jnp.concatenate([part, extra], axis=0).astype(BF16)

    def unit(i, kb):
        keys = pl.ds(pl.multiple_of(kb * BLOCK, BLOCK), BLOCK)
        for h in range(PER):
            head = pl.ds(h * HEAD_DIM, HEAD_DIM)
            score = mm(k_ref[h, keys, :], q_ref[i, h])
            old = top_ref[i, h]
            new = jnp.maximum(old, jnp.max(score, axis=0, keepdims=True))
            probs = jnp.exp(score - new)
            shrink = jnp.exp(old - new)
            top_ref[i, h] = new
            sum_ref[i, h] = sum_ref[i, h] * shrink + jnp.sum(probs, axis=0, keepdims=True)
            o_ref[i, head, :] = o_ref[i, head, :] * shrink + mm(
                vt_ref[kb, head, :], probs.astype(BF16)
            )

    def attend(n):
        b, lv, j = event(n)
        first = jnp.logical_and(j == 0, lax.rem(lv, sub) == lax.rem(z, sub))
        known = jnp.where(n < 2, 1, jnp.minimum((n - 2) // 4 + 2, levels))

        def pair(u, carry):
            near = u < known
            seen = level(jnp.minimum(u, known - 1))
            old = event(jnp.maximum(u - known, 0))[0]
            i = jnp.where(near, seen, lv) // sub
            kb = jnp.where(near, b, old)
            query = i * members + m
            mine = jnp.where(near, lax.rem(seen, sub) == lax.rem(z, sub), old < b)
            pl.when(jnp.logical_and(mine, kb <= query))(lambda: unit(i, kb))
            return carry

        lax.fori_loop(0, known + jnp.where(first, n, 0), pair, 0)

    top_ref[...] = jnp.full(top_ref.shape, -jnp.inf, F32)
    sum_ref[...] = jnp.zeros(sum_ref.shape, F32)
    o_ref[...] = jnp.zeros(o_ref.shape, F32)
    lag = 5
    turn_on = ring - 5

    def advance(n, carry):
        pl.when(n < ring)(lambda: arrive(n))

        @pl.when(n == turn_on)
        def _():
            for at in range(len(pieces)):
                if pieces[at][4]:
                    relay(at)

        pl.when(n >= lag)(lambda: attend(n - lag))
        return carry

    lax.fori_loop(0, ring + lag, advance, 0)
    saves = [
        pltpu.make_async_copy(src, dst, osem.at[n])
        for n, (src, dst) in enumerate(
            ((k_ref, k_out), (kt_ref, kt_out), (vt_ref, vt_out), (q_ref, q_out), (o_ref, o_out))
        )
    ]
    saves += [
        pltpu.make_async_copy(xa_ref.at[i * members + m], xr_out.at[i], osem.at[5 + i])
        for i in range(GROUPS)
    ]
    for save in saves[:3] + saves[5:]:
        save.start()

    def give(i):
        return remote(low_ref.at[i], att_ref.at[g], asend.at[i], arecv.at[g], i * members + m, s)

    for i in range(GROUPS):
        for h in range(PER):
            head = pl.ds(h * HEAD_DIM, HEAD_DIM)
            out = o_ref[i, head, :] / sum_ref[i, h]
            o_ref[i, head, :] = out
            low_ref[i, head, :] = out.astype(BF16)
            lse_ref[i, h] = top_ref[i, h] + jnp.log(sum_ref[i, h])

        @pl.when(g == i)
        def _():
            att_ref[g] = low_ref[i]

        pl.when(g != i)(lambda: give(i).start())
    for save in saves[3:5]:
        save.start()
    for at in range(1, len(pieces)):
        if pieces[at][4]:
            relay_far(at)
        else:
            relay(at)
    for d in range(1, GROUPS):
        p = lax.rem(g + d, GROUPS)
        remote(low_ref.at[0], att_ref.at[p], asend.at[0], arecv.at[p], r, s).wait_recv()
    for at in range(1, len(pieces)):
        relayed(at)
    for i in range(GROUPS):
        pl.when(g != i)(lambda: give(i).wait_send())

    def sent(e, carry):
        b, lv, j = event(e)

        @pl.when(j == 0)
        def _():
            pl.when(jnp.logical_and(lv <= z, above))(lambda: move(b, 0).wait_send())
            pl.when(jnp.logical_and(lv >= z, below))(lambda: move(b, 1).wait_send())
            move(b, 2).wait_send()

        pl.when(j < 2)(lambda: move(b, 3).wait_send())
        return carry

    lax.fori_loop(0, ring, sent, 0)
    for copy in lists:
        copy.wait_send()
    for at in range(len(pieces)):
        for d in range(shards - 1):
            across(at, d).wait_send()
            shifted(at, d, 0, y, c, sib).wait_send()
            if pieces[at][4]:
                shifted(at, d, 1, y, c, yn).wait_send()
                shifted(at, d, 2, 1 - y, c, sib).wait_send()
    for save in saves:
        save.wait()


def forward_all(x, qkv_weight, docs, vectors, weights, parts, ring, shards, ident):
    shape = jax.ShapeDtypeStruct
    dma = pltpu.SemaphoreType.DMA
    vmem = pltpu.VMEM
    n = 1 + sum(part[2] for part in parts)
    width = x.shape[1]
    sizes = [v.shape[1] for v in vectors]
    per = max(shards - 1, 1)
    o = (GROUPS, SLAB, BLOCK)
    q = (GROUPS, PER, 2 * HEAD_DIM, BLOCK)
    k = (PER, ring * BLOCK, 2 * HEAD_DIM)
    t = (ring, SLAB, BLOCK)
    return pl.pallas_call(
        lambda *refs: forward_kernel(ring, shards, parts, sizes, *refs),
        out_shape=(
            shape(o, BF16), shape((shards, 1, sum(sizes)), F32), shape((3 * SLAB, width), BF16),
            shape((GROUPS, PER, 1, BLOCK), F32), shape(o, F32), shape(q, BF16), shape(k, BF16),
            shape(t, BF16), shape(t, BF16), shape((GROUPS,) + x.shape, BF16),
        )
        + tuple(shape((shards,) + w.shape, w.dtype) for w in weights),
        in_specs=[VMEM_SPEC] * (3 + len(vectors)) + [ANY_SPEC] * 3,
        out_specs=(VMEM_SPEC,) * 4 + (ANY_SPEC,) * 9,
        scratch_shapes=[
            vmem((ring,) + x.shape, BF16), vmem((shards, width // shards, 3 * SLAB), BF16),
            vmem(o, BF16), vmem((2 * SLAB, 1), F32), vmem(o, F32), vmem(q, BF16), vmem(k, BF16),
            vmem(t, BF16), vmem(t, BF16),
            vmem((GROUPS, PER, 1, BLOCK), F32), vmem((GROUPS, PER, 1, BLOCK), F32),
            dma((4, ring)), dma((ring,)), dma((n, per)), dma((n, per)), dma((n, per, 3)),
            dma((n, per, 3)), dma((per,)), dma((per,)),
            dma((GROUPS,)), dma((GROUPS,)), dma((5 + GROUPS,)),
        ],
        compiler_params=pltpu.CompilerParams(
            collective_id=ident, has_side_effects=True, vmem_limit_bytes=VMEM_LIMIT
        ),
    )(x, qkv_weight, docs, *vectors, *weights)


def layer_norm(hidden, gain, shift):
    centre = hidden - jnp.mean(hidden, axis=-1, keepdims=True)
    inverse = lax.rsqrt(jnp.mean(centre * centre, axis=-1, keepdims=True) + EPSILON)
    normed = centre * inverse
    return (normed * gain + shift, normed, inverse)


def norm_back(grad_output, normed, inverse, gain):
    grad_normed = grad_output * gain
    centred = grad_normed - jnp.mean(grad_normed, axis=-1, keepdims=True)
    return inverse * (centred - normed * jnp.mean(grad_normed * normed, axis=-1, keepdims=True))


def mlp_kernel(
    shards, sizes, att_ref, x_ref, og_ref, flat_ref, *refs,
):
    own, full = refs[:3], refs[3:6]
    out_ref, gat_ref, mid_ref, small_ref, down_out, up_out, outw_out = refs[6:13]
    wo_ref, wu_ref, wd_ref, act_ref, slope_ref, gd_ref, gu_ref, go_ref, lsem, ssem = refs[13:]
    s = lax.axis_index("shard")
    width = x_ref.shape[1]
    hidden = wu_ref.shape[1]
    loads = []
    for w, ref in enumerate((wo_ref, wu_ref, wd_ref)):
        size = own[w].shape[0]
        group = []
        for d in range(shards):
            t = lax.rem(s + d, shards)
            rows = pl.ds(pl.multiple_of(t * size, size), size)
            src = own[w] if d == 0 else full[w].at[t]
            group.append(pltpu.make_async_copy(src, ref.at[rows], lsem.at[w * shards + d]))
        loads.append(group)
        for load in group:
            load.start()

    def ready(w):
        for load in loads[w]:
            load.wait()

    starts = [sum(sizes[:n]) for n in range(len(sizes))]

    def vector(n):
        return jnp.concatenate(
            [flat_ref[t, :, starts[n] : starts[n] + sizes[n]] for t in range(shards)], axis=1
        )

    def put(n, row):
        for t in range(shards):
            small_ref[t, :, starts[n] : starts[n] + sizes[n]] = row[
                :, t * sizes[n] : (t + 1) * sizes[n]
            ]

    small_ref[...] = jnp.zeros(small_ref.shape, F32)
    att = att_ref[...].reshape(width, BLOCK)
    ready(0)
    branch = mm(att, wo_ref[...], TN) + vector(1)
    gain_mid = vector(2)
    mid_out, mid_norm, mid_inv = layer_norm(x_ref[...].astype(F32) + branch, gain_mid, vector(3))
    mid_low = mid_out.astype(BF16)
    up_bias = vector(4)
    cols = 512
    ready(1)
    for at in range(0, hidden, cols):
        block = slice(at, at + cols)
        pre = mm(mid_low, wu_ref[:, block]) + up_bias[:, block]
        phi = 0.5 * (1.0 + lax.erf(pre * 0.7071067811865476))
        act_ref[:, block] = (pre * phi).astype(BF16)
        slope_ref[:, block] = phi + pre * jnp.exp(-0.5 * pre * pre) * 0.3989422804014327
    ready(2)
    ffn = mm(act_ref[...], wd_ref[...]) + vector(5)
    gain_end = vector(6)
    end_out, end_norm, end_inv = layer_norm(mid_out + ffn, gain_end, vector(7))
    out_ref[...] = end_out.astype(BF16)
    top = og_ref[...].astype(F32)

    def column(value):
        return jnp.sum(value, axis=0, keepdims=True)

    put(6, column(top * end_norm))
    put(7, column(top))
    grad_end_in = norm_back(top, end_norm, end_inv, gain_end)
    grad_ffn = grad_end_in.astype(BF16)
    put(5, column(grad_ffn.astype(F32)))
    saves = []

    def save(src, dst):
        copy = pltpu.make_async_copy(src, dst, ssem.at[len(saves)])
        copy.start()
        saves.append(copy)

    chunks = gd_ref.shape[1]
    rows = hidden // shards // chunks
    for t in range(shards):
        for k in range(chunks):
            at = t * (hidden // shards) + k * rows
            value = mm(act_ref[:, at : at + rows], grad_ffn, TN)
            gd_ref[t, k] = value.astype(BF16).reshape(gd_ref.shape[2:])
        save(gd_ref.at[t], down_out.at[t])
    grad_mid_out = grad_end_in
    ups = []
    wide = hidden // gu_ref.shape[0]
    for k in range(gu_ref.shape[0]):
        block = slice(k * wide, (k + 1) * wide)
        grad_act = mm(grad_ffn, wd_ref[block, :], NT)
        grad_pre = (grad_act * slope_ref[:, block]).astype(BF16)
        ups.append(column(grad_pre.astype(F32)))
        value = mm(mid_low, grad_pre, TN).astype(BF16)
        for half in range(2):
            gu_ref[k, half] = value[:, half * (wide // 2) : (half + 1) * (wide // 2)].reshape(
                gu_ref.shape[2:]
            )
        save(gu_ref.at[k], up_out.at[k])
        grad_mid_out = grad_mid_out + mm(grad_pre, wu_ref[:, block], NT)
    put(4, jnp.concatenate(ups, axis=1))
    put(2, column(grad_mid_out * mid_norm))
    put(3, column(grad_mid_out))
    grad_mid_in = norm_back(grad_mid_out, mid_norm, mid_inv, gain_mid)
    mid_ref[...] = grad_mid_in
    grad_branch = grad_mid_in.astype(BF16)
    put(1, column(grad_branch.astype(F32)))
    gat_ref[...] = mm(wo_ref[...], grad_branch, NT).astype(BF16).reshape(gat_ref.shape)
    value = mm(att, grad_branch).astype(BF16)
    for half in range(2):
        go_ref[0, half] = value[:, half * (width // 2) : (half + 1) * (width // 2)].reshape(
            go_ref.shape[2:]
        )
    save(go_ref, outw_out)
    for copy in saves:
        copy.wait()


def mlp_all(att, x, out_grad, flat, own, full, sizes, shards, levels, down_chunks, up_chunks):
    shape = jax.ShapeDtypeStruct
    dma = pltpu.SemaphoreType.DMA
    vmem = pltpu.VMEM
    width, hidden = own[0].shape[1], own[1].shape[1]
    gd = (shards, down_chunks, 2, 2, levels, hidden // shards // down_chunks // 4 // levels, width)
    gu = (up_chunks, 2, shards, 2, levels, width // shards // 2 // levels, hidden // up_chunks // 2)
    go = (1, 2, shards, 2, levels, width // shards // 2 // levels, width // 2)
    return pl.pallas_call(
        lambda *refs: mlp_kernel(shards, sizes, *refs),
        out_shape=(
            shape((BLOCK, width), BF16), shape((GROUPS, SLAB, BLOCK), BF16),
            shape((BLOCK, width), F32), shape(flat.shape, F32),
            shape(gd, BF16), shape(gu, BF16), shape(go, BF16),
        ),
        in_specs=[VMEM_SPEC] * 4 + [ANY_SPEC] * 6,
        out_specs=(VMEM_SPEC,) * 4 + (ANY_SPEC,) * 3,
        scratch_shapes=[
            vmem((width, width), BF16), vmem((width, hidden), BF16), vmem((hidden, width), BF16),
            vmem((BLOCK, hidden), BF16), vmem((BLOCK, hidden), F32),
            vmem(gd, BF16), vmem(gu, BF16), vmem(go, BF16),
            dma((3 * shards,)), dma((shards + up_chunks + 1,)),
        ],
        compiler_params=pltpu.CompilerParams(vmem_limit_bytes=VMEM_LIMIT),
    )(att, x, out_grad, flat, *own, *full)


def add_rows(out, terms):
    total = terms[0][...].astype(F32)
    for term in terms[1:]:
        total = total + term[...].astype(F32)
    out[...] = total.astype(out.dtype)


def reduce_steps(net, slab, out, own, near, side, mate, tall, sems, group):
    asend, arecv, bsend, brecv, csend, crecv, dsend, drecv, esend, erecv, fsend, frecv, gsend, grecv, lsem = sems
    r, s, z, y, c = net.r, net.s, net.z, net.y, net.c
    base = z // group * group
    zz = lax.rem(z, group)
    inner = [lax.rem(zz + d, group) for d in range(1, group)]
    near_copy = lambda: remote(slab(1 - c), near, asend, arecv, net.sib, s)
    own_copy = lambda: pltpu.make_async_copy(slab(c), own, lsem)
    across = lambda d: remote(
        near.at[net.others[d]], side.at[d], bsend.at[d], brecv.at[d], r, net.others[d]
    )
    over = lambda: remote(near.at[s, 1 - y], mate, csend, crecv, net.yn, s)
    along = lambda d: remote(
        near.at[s, y, inner[d]], tall.at[d], dsend.at[d], drecv.at[d],
        (base + inner[d]) * 4 + net.line, s,
    )
    one, two, four = out
    mine = one(c, y, z)
    spread = lambda d: remote(
        mine, mine, esend.at[d], erecv.at[d], net.heights[d] * 4 + net.line, s
    )
    pair = lambda: remote(two(c, y), two(c, y), fsend, frecv, net.yn, s)
    last = lambda: remote(four(c), four(c), gsend, grecv, net.sib, s)
    n_side, n_inner, n_tall = len(net.others), len(inner), len(net.heights)

    def step0():
        near_copy().start()
        own_copy().start()

    def step1():
        near_copy().wait_recv()
        own_copy().wait()
        for t in range(net.shards):
            for half in range(2):
                add_rows(near.at[t, half], [own.at[t, half], near.at[t, half]])
        for d in range(n_side):
            across(d).start()

    def step2():
        for d in range(n_side):
            across(d).wait_recv()
        for half in range(2):
            add_rows(
                near.at[s, half], [near.at[s, half]] + [side.at[d, half] for d in range(n_side)]
            )
        over().start()

    def step3():
        over().wait_recv()
        add_rows(near.at[s, y], [near.at[s, y], mate])
        for d in range(n_inner):
            along(d).start()

    def step4():
        for d in range(n_inner):
            along(d).wait_recv()
        add_rows(mine, [near.at[s, y, zz]] + [tall.at[d] for d in range(n_inner)])
        for d in range(n_tall):
            spread(d).start()

    def step5():
        for d in range(n_tall):
            spread(d).wait_recv()
        pair().start()

    def step6():
        pair().wait_recv()
        last().start()

    def step7():
        last().wait_recv()

    def drain():
        near_copy().wait_send()
        for d in range(n_side):
            across(d).wait_send()
        over().wait_send()
        for d in range(n_inner):
            along(d).wait_send()
        for d in range(n_tall):
            spread(d).wait_send()
        pair().wait_send()
        last().wait_send()

    return [step0, step1, step2, step3, step4, step5, step6, step7], drain


def reduce_scratch(shards, levels, group, rows, cols):
    dma = pltpu.SemaphoreType.DMA
    vmem = pltpu.VMEM
    many = lambda n: dma((max(n, 1),))
    buffers = [
        vmem((shards, 2, group, rows, cols), BF16),
        vmem((shards, 2, group, rows, cols), BF16),
        vmem((max(shards - 1, 1), 2, group, rows, cols), BF16),
        vmem((group, rows, cols), BF16),
        vmem((max(group - 1, 1), rows, cols), BF16),
    ]
    sems = [
        dma(()), dma(()), many(shards - 1), many(shards - 1), dma(()), dma(()),
        many(group - 1), many(group - 1), many(levels - 1), many(levels - 1),
        dma(()), dma(()), dma(()), dma(()), dma(()),
    ]
    return buffers + sems


SCRATCH = 20


def small_steps(net, src, out, near, side, mate, tall, sems):
    asend, arecv, bsend, brecv, csend, crecv, dsend, drecv = sems
    r, s, z, y, c = net.r, net.s, net.z, net.y, net.c
    near_copy = lambda: remote(src, near.at[1], asend, arecv, net.sib, s)
    across = lambda d: remote(
        near.at[0, net.others[d]], side.at[s], bsend.at[d], brecv.at[d], r, net.others[d]
    )
    over = lambda: remote(mate.at[0], mate.at[1], csend, crecv, net.yn, s)
    along = lambda d: remote(
        tall.at[z], tall.at[z], dsend.at[d], drecv.at[d], net.heights[d] * 4 + net.line, s
    )

    def step0():
        near_copy().start()

    def step1():
        near_copy().wait_recv()
        near[0] = src[...] + near[1]
        side[s] = near[0, s]
        for d in range(len(net.others)):
            across(d).start()

    def step2():
        for d in range(len(net.others)):
            across(d).wait_recv()
        total = side[0]
        for t in range(1, net.shards):
            total = total + side[t]
        mate[0] = total
        over().start()

    def step3():
        over().wait_recv()
        tall[z] = mate[0] + mate[1]
        for d in range(len(net.heights)):
            along(d).start()

    def step4():
        for d in range(len(net.heights)):
            along(d).wait_recv()
        total = tall[0]
        for t in range(1, net.levels):
            total = total + tall[t]
        out[...] = total

    def drain():
        near_copy().wait_send()
        for d in range(len(net.others)):
            across(d).wait_send()
        over().wait_send()
        for d in range(len(net.heights)):
            along(d).wait_send()

    return [step0, step1, step2, step3, step4], drain


def small_scratch(shards, levels, rows):
    dma = pltpu.SemaphoreType.DMA
    vmem = pltpu.VMEM
    return [
        vmem((2, shards, 1, rows), F32), vmem((shards, 1, rows), F32),
        vmem((2, 1, rows), F32), vmem((levels, 1, rows), F32),
        dma(()), dma(()), dma((max(shards - 1, 1),)), dma((max(shards - 1, 1),)),
        dma(()), dma(()), dma((levels - 1,)), dma((levels - 1,)),
    ]


def places(ref, chunk, core_first, levels, rows, cols):
    if len(ref.shape) != 2:
        return (
            lambda c, y, z: ref.at[chunk, c, y, z], lambda c, y: ref.at[chunk, c, y],
            lambda c: ref.at[chunk, c],
        )
    if core_first:

        def view(c, at, size):
            lanes = pl.ds(pl.multiple_of((chunk * 2 + c) * cols, cols), cols)
            return ref.at[pl.ds(pl.multiple_of(at, rows), size), lanes]

        return (
            lambda c, y, z: view(c, (y * levels + z) * rows, rows),
            lambda c, y: view(c, y * levels * rows, levels * rows),
            lambda c: view(c, 0, 2 * levels * rows),
        )

    def span(at, count):
        first = (chunk * 4 * levels + at) * rows
        return ref.at[pl.ds(pl.multiple_of(first, rows), count * rows)]

    return (
        lambda c, y, z: span((c * 2 + y) * levels + z, 1),
        lambda c, y: span((c * 2 + y) * levels, levels),
        lambda c: span(c * 2 * levels, 2 * levels),
    )


def spread_out(jobs, offsets):
    ticks = {}
    for n, steps in enumerate(jobs):
        for t, step in enumerate(steps):
            ticks.setdefault(n + offsets[t], []).append(step)
    return [ticks.get(t, []) for t in range(max(ticks, default=-1) + 1)]


def term_jobs(net, specs, chunk_shapes, terms, outs, rest):
    jobs, drains = [], []
    for number, (which, k, core_first) in enumerate(specs):
        scratch = rest[number * SCRATCH : (number + 1) * SCRATCH]
        ref = terms[which]
        if core_first:
            slab = lambda core, ref=ref, k=k: ref.at[k, core]
        else:
            slab = lambda core, ref=ref, k=k: ref.at[:, k, core]
        spot = places(outs[which], k, core_first, net.levels, *chunk_shapes[which])
        steps, drain = reduce_steps(net, slab, spot, *scratch[:5], scratch[5:], net.levels)
        jobs.append(steps)
        drains.append(drain)
    return jobs, drains, rest[len(specs) * SCRATCH :]


def sums_kernel(ring, shards, specs, chunk_shapes, *refs):
    n = len(chunk_shapes)
    net = Links(ring, shards)
    hello(net.partners())
    jobs, drains, _ = term_jobs(net, specs, chunk_shapes, refs[:n], refs[n : 2 * n], refs[2 * n :])
    for steps in spread_out(jobs, OFFSETS):
        for step in steps:
            step()
    for drain in drains:
        drain()


def tail_kernel(ring, shards, specs, chunk_shapes, n0, *refs):
    (
        go_ref, lse_ref, w_ref, mid_ref, small_ref, q_in, k_in, kt_in, vt_in, o_in, xr_in,
    ) = refs[:11]
    n_terms = len(chunk_shapes)
    terms, refs = refs[11 : 11 + n_terms], refs[11 + n_terms :]
    out_ref, outs, (qkv_ref, total_small) = refs[0], refs[1 : 1 + n_terms], refs[1 + n_terms : 3 + n_terms]
    (
        q_ref, k_ref, kt_ref, vt_ref, o_ref,
        g_ref, x_ref, v_ref, delta_ref, acc_ref, dk_ref, dv_ref, pq_ref, stage_ref, got_ref, got2_ref,
        dw_ref, dx_ref, near_ref, far_ref, db_ref, dwl_ref, row_ref, all_ref,
        gsend, grecv, ksend, krecv, xsend, xrecv, lsem,
    ) = refs[3 + n_terms : 34 + n_terms]
    rest = refs[34 + n_terms :]
    net = Links(ring, shards)
    r, s = net.r, net.s
    levels, members = net.levels, ring // GROUPS
    sub = levels // GROUPS
    g, m = r // members, lax.rem(r, members)
    peers = [lax.rem(g + d, GROUPS) for d in range(1, GROUPS)]
    mates = [lax.rem(m + d, members) for d in range(1, members)]
    partners = net.partners()
    if levels != GROUPS:
        partners = partners + [(p * members + m, s, True) for p in peers]
        partners = partners + [(g * members + t, s, True) for t in mates]
    else:
        partners = partners + [(g * members + 3 - m, s, True)]
    hello(partners)

    def give(p):
        return remote(go_ref.at[p], g_ref.at[g], gsend.at[p], grecv.at[g], p * members + m, s)

    def take(p):
        return remote(go_ref.at[p], g_ref.at[p], gsend.at[p], grecv.at[p], p * members + m, s)

    for p in peers:
        give(p).start()
    loads = [
        pltpu.make_async_copy(src, dst, lsem.at[n])
        for n, (src, dst) in enumerate(
            ((vt_in, vt_ref), (k_in, k_ref), (q_in, q_ref), (kt_in, kt_ref), (o_in, o_ref),
             (xr_in, x_ref))
        )
    ]
    for load in loads:
        load.start()
    g_ref[g] = go_ref[g]

    jobs, drains, rest = term_jobs(net, specs, chunk_shapes, terms, outs, rest)
    qkv_jobs = []
    for k in range(2):
        steps, drain = reduce_steps(
            net, lambda core, k=k: dwl_ref.at[:, k, core], places(all_ref, k, False, levels, 0, 0),
            *rest[:5], rest[5:SCRATCH], sub
        )
        qkv_jobs.append(steps)
        drains.append(drain)
        rest = rest[SCRATCH:]
    vec_steps, drain = small_steps(net, small_ref, total_small, *rest[:4], rest[4:])
    drains.append(drain)
    ticks = spread_out(jobs, OFFSETS)

    def tick(t, lo, hi):
        if hi - lo == 1:
            for step in ticks[lo]:
                step()
        else:
            mid = (lo + hi) // 2
            pl.when(t < mid)(lambda: tick(t, lo, mid))
            pl.when(t >= mid)(lambda: tick(t, mid, hi))

    for load in loads[:1]:
        load.wait()

    def turn(b, carry):
        rows = pl.ds(pl.multiple_of(b * BLOCK, BLOCK), BLOCK)
        for h in range(PER):
            v_ref[h, rows, :] = (
                vt_ref[b, h * HEAD_DIM : (h + 1) * HEAD_DIM, :].astype(F32).T.astype(BF16)
            )
        dk_ref[b] = jnp.zeros((SLAB, BLOCK), F32)
        dv_ref[b] = jnp.zeros((SLAB, BLOCK), F32)
        return carry

    lax.fori_loop(0, ring, turn, 0)
    dw_ref[...] = jnp.zeros(dw_ref.shape, F32)
    db_ref[...] = jnp.zeros(db_ref.shape, F32)
    for load in loads[1:]:
        load.wait()

    pairs = members // 2
    c, mt = net.c, m // 2
    fellows = [lax.rem(mt + d, pairs) for d in range(1, pairs)]
    pieces = 4
    size = BLOCK // pieces

    def cross():
        return lambda j: remote(
            stage_ref.at[j], got_ref.at[j], ksend.at[j, 0], krecv.at[j, 0], net.sib, s
        )

    to_core = cross()

    def share(j, d):
        t = fellows[d]
        return remote(
            got_ref.at[j, t], got2_ref.at[j, d], ksend.at[j, d + 1], krecv.at[j, d + 1],
            g * members + t * 2 + c, s,
        )

    def hop(j, u, side, target):
        rows = pl.ds(u * size, size)
        return remote(
            dx_ref.at[j, rows], far_ref.at[j, side, rows], xsend.at[j, u], xrecv.at[j, side, u],
            target, s,
        )

    def pass_dx(j, u):
        down = lambda: hop(j, u, 0, r - members)
        up = lambda: hop(j, u, 1, r + members)
        return down, up

    def begin(i):
        pl.when(g != i)(lambda: take(i).wait_recv())
        for h in range(PER):
            head = pl.ds(h * HEAD_DIM, HEAD_DIM)
            delta_ref[h] = jnp.sum(
                g_ref[i, head, :].astype(F32) * o_ref[i, head, :], axis=0, keepdims=True
            )
        acc_ref[...] = jnp.zeros(acc_ref.shape, F32)

    def unit(i, kb):
        keys = pl.ds(pl.multiple_of(kb * BLOCK, BLOCK), BLOCK)
        for h in range(PER):
            head = pl.ds(h * HEAD_DIM, HEAD_DIM)
            score = mm(k_ref[h, keys, :], q_ref[i, h])
            probs = jnp.exp(score - lse_ref[i, h])
            grad = g_ref[i, head, :]
            moved = (probs * (mm(v_ref[h, keys, :], grad) - delta_ref[h])).astype(BF16)
            acc_ref[h] += mm(kt_ref[kb, head, :], moved)
            dk_ref[kb, head, :] += mm(q_ref[i, h, :HEAD_DIM, :], moved, NT)
            dv_ref[kb, head, :] += mm(grad, probs.astype(BF16), NT)

    def end(i):
        for h in range(PER):
            pq_ref[i, pl.ds(h * HEAD_DIM, HEAD_DIM), :] = (
                acc_ref[h] * HEAD_DIM ** (-0.5)
            ).astype(BF16)
        for t in range(pairs):
            b = i * members + t * 2 + 1 - c
            stage_ref[i, t, :SLAB, :] = dk_ref[b].astype(BF16)
            stage_ref[i, t, SLAB:, :] = dv_ref[b].astype(BF16)
        to_core(i).start()

    def merge(j):
        to_core(j).wait_recv()
        for d, t in enumerate(fellows):
            b = j * members + t * 2 + c
            for half, ref in enumerate((dk_ref, dv_ref)):
                rows = pl.ds(half * SLAB, SLAB)
                got_ref[j, t, rows, :] = (ref[b] + got_ref[j, t, rows, :].astype(F32)).astype(BF16)
            share(j, d).start()

    def finish(j):
        b = j * members + m
        dk = dk_ref[b] + got_ref[j, mt, :SLAB, :].astype(F32)
        dv = dv_ref[b] + got_ref[j, mt, SLAB:, :].astype(F32)
        for d in range(pairs - 1):
            share(j, d).wait_recv()
            dk = dk + got2_ref[j, d, :SLAB, :].astype(F32)
            dv = dv + got2_ref[j, d, SLAB:, :].astype(F32)
        proj = jnp.concatenate([pq_ref[j], dk.astype(BF16), dv.astype(BF16)], axis=0)
        db_ref[...] += jnp.sum(proj.astype(F32), axis=1, keepdims=True)
        dx = mm(proj, w_ref[...], TN)
        near_ref[j] = dx
        dx_ref[j] = dx.astype(BF16)
        start_dx(j, 0)
        dw_ref[...] += mm(x_ref[j], proj.T, TN)

    def start_dx(j, depth):
        from_below = jnp.logical_and(g < j, g == depth)
        from_above = jnp.logical_and(g > j, GROUPS - 1 - g == depth)
        for u in range(pieces):
            rows = pl.ds(u * size, size)
            down, up = pass_dx(j, u)

            @pl.when(from_below)
            def _():
                if depth:
                    hop(j, u, 1, r).wait_recv()
                    dx_ref[j, rows] = (near_ref[j, rows] + far_ref[j, 1, rows].astype(F32)).astype(BF16)
                up().start()

            @pl.when(from_above)
            def _():
                if depth:
                    hop(j, u, 0, r).wait_recv()
                    dx_ref[j, rows] = (near_ref[j, rows] + far_ref[j, 0, rows].astype(F32)).astype(BF16)
                down().start()

    def own_dx():
        for side, there in ((0, g < GROUPS - 1), (1, g > 0)):

            @pl.when(there)
            def _():
                for u in range(pieces):
                    hop(g, u, side, r).wait_recv()
                near_ref[g] += far_ref[g, side].astype(F32)

    sizes = [i * members + m + 1 for i in range(GROUPS)][::-1]
    ends = [sum(sizes[: n + 1]) for n in range(GROUPS)]
    units = ends[-1]
    finishes = [members * n + 2 for n in (4, 7, 9, 10)]

    def advance(it, carry):
        past = [(it >= e).astype(jnp.int32) for e in ends]
        i = GROUPS - 1 - past[0] - past[1] - past[2]
        first = jnp.where(i == 3, 0, jnp.where(i == 2, ends[0], jnp.where(i == 1, ends[1], ends[2])))
        kb = it - first

        t = it // PACE
        if ticks:
            pl.when(jnp.logical_and(lax.rem(it, PACE) == 0, t < len(ticks)))(
                lambda: tick(t, 0, len(ticks))
            )

        @pl.when(it < units)
        def _():
            pl.when(kb == 0)(lambda: begin(i))
            unit(i, kb)

            @pl.when(kb == i * members + m)
            def _():
                end(i)

        def at_times(shift, act):
            n_due = sum((it - shift >= at).astype(jnp.int32) for at in finishes)
            n_done = sum((it - shift > at).astype(jnp.int32) for at in finishes)
            pl.when(n_due > n_done)(lambda: act(GROUPS - n_due))

        at_times(0, merge)
        at_times(1, finish)
        for depth in range(1, GROUPS - 1):
            at_times(1 + depth, lambda j, depth=depth: start_dx(j, depth))
        return carry

    count = max(finishes[-1] + 2, PACE * len(ticks))
    lax.fori_loop(0, count, advance, 0)

    width = w_ref.shape[1]
    dwl_ref[...] = dw_ref[...].astype(BF16).reshape(dwl_ref.shape)
    row = jnp.broadcast_to(db_ref[...], (3 * SLAB, 8)).T[:1]
    row_ref[...] = jnp.zeros(row_ref.shape, F32)
    for k in range(GROUPS):

        @pl.when(g == k)
        def _():
            row_ref[:, k * SLAB : (k + 1) * SLAB] = row[:, :SLAB]
            row_ref[:, width + k * SLAB : width + (k + 1) * SLAB] = row[:, 2 * SLAB :]

    for t in range(shards):
        small_ref[t, :, :n0] = row_ref[:, t * n0 : (t + 1) * n0]
    for job in qkv_jobs:
        job[0]()
    vec_steps[0]()
    for depth in range(1, GROUPS - 1):
        if count <= finishes[-1] + 1 + depth:
            start_dx(0, depth)
    for job in qkv_jobs:
        job[1]()
    vec_steps[1]()
    own_dx()
    out_ref[...] = (near_ref[g] + mid_ref[...]).astype(BF16)
    for t in range(2, 8):
        for job in qkv_jobs:
            job[t]()
        if t < len(vec_steps):
            vec_steps[t]()
    if len(qkv_ref.shape) == 2:
        rows = all_ref.shape[-2]
        for part in range(8):
            for z in range(levels):
                at = (part * sub + z % sub) * rows
                piece = all_ref[part // 4, part // 2 % 2, part % 2, z]
                for t in range(3):
                    lane = t * width + z // sub * SLAB
                    qkv_ref[at : at + rows, lane : lane + SLAB] = piece[
                        :, t * SLAB : (t + 1) * SLAB
                    ]
    else:
        qkv_ref[...] = all_ref[...]
    for p in peers:
        give(p).wait_send()
    for j in range(GROUPS):
        to_core(j).wait_send()
        for d in range(pairs - 1):
            share(j, d).wait_send()
        for u in range(pieces):
            pl.when(g != j)(lambda: hop(j, u, 0, r).wait_send())
    for drain in drains:
        drain()


PACE = 2
OFFSETS = (0, 1, 3, 4, 5, 6, 7, 8)


def tail_all(gat, lse, w_group, mid, small, saved, terms, n0, ring, shards, ident):
    members, levels = ring // GROUPS, ring // 4
    sub = levels // GROUPS
    width = mid.shape[1]
    part = width // shards
    shape = jax.ShapeDtypeStruct
    dma = pltpu.SemaphoreType.DMA
    vmem = pltpu.VMEM
    specs, scratch, out_shape, chunk_shapes = [], [], [], []
    for i, term in enumerate(terms):
        core_first = i > 0
        chunks = term.shape[0] if core_first else term.shape[1]
        rows, cols = term.shape[-2:]
        chunk_shapes.append((rows, cols))
        if rows % 16:
            out_shape.append(shape((chunks, 2, 2, levels, rows, cols), BF16))
        elif core_first:
            out_shape.append(shape((2 * levels * rows, chunks * 2 * cols), BF16))
        else:
            out_shape.append(shape((chunks * 4 * levels * rows, cols), BF16))
        for k in range(chunks):
            specs.append((i, k, core_first))
            scratch += reduce_scratch(shards, levels, levels, rows, cols)
    term_scratch, term_shapes = scratch, out_shape
    apart = ring * BLOCK > 4096
    if apart:
        sums = pl.pallas_call(
            lambda *refs: sums_kernel(ring, shards, specs, chunk_shapes, *refs),
            out_shape=tuple(term_shapes),
            in_specs=[ANY_SPEC] * 3,
            out_specs=(VMEM_SPEC,) * 3,
            scratch_shapes=term_scratch,
            compiler_params=pltpu.CompilerParams(
                collective_id=ident + 1, has_side_effects=True, vmem_limit_bytes=VMEM_LIMIT
            ),
        )(*terms)
    specs, chunk_shapes = ([], []) if apart else (specs, chunk_shapes)
    scratch = [] if apart else list(term_scratch)
    out_shape = [] if apart else list(term_shapes)
    terms = () if apart else terms
    rows = part // 8 // sub
    buffer = (2, 2, 2, levels, rows, 3 * SLAB)
    scratch += reduce_scratch(shards, levels, sub, rows, 3 * SLAB)
    scratch += reduce_scratch(shards, levels, sub, rows, 3 * SLAB)
    scratch += small_scratch(shards, levels, small.shape[2])
    out_shape.append(shape(buffer if rows % 16 else (part, 3 * width), BF16))
    slab = (GROUPS, SLAB, BLOCK)
    tall = (ring, SLAB, BLOCK)
    result = pl.pallas_call(
        lambda *refs: tail_kernel(ring, shards, specs, chunk_shapes, n0, *refs),
        out_shape=(shape((BLOCK, width), BF16), *out_shape, shape((1, small.shape[2]), F32)),
        in_specs=[VMEM_SPEC] * 5 + [ANY_SPEC] * (6 + len(terms)),
        out_specs=(VMEM_SPEC,) * (3 + len(terms)),
        scratch_shapes=[
            vmem((GROUPS, PER, 2 * HEAD_DIM, BLOCK), BF16),
            vmem((PER, ring * BLOCK, 2 * HEAD_DIM), BF16),
            vmem(tall, BF16), vmem(tall, BF16), vmem(slab, F32),
            vmem(slab, BF16),
            vmem((GROUPS, BLOCK, width), BF16),
            vmem((PER, ring * BLOCK, HEAD_DIM), BF16),
            vmem((PER, 1, BLOCK), F32),
            vmem((PER, HEAD_DIM, BLOCK), F32),
            vmem(tall, F32), vmem(tall, F32), vmem(slab, BF16),
            vmem((GROUPS, members // 2, 2 * SLAB, BLOCK), BF16),
            vmem((GROUPS, members // 2, 2 * SLAB, BLOCK), BF16),
            vmem((GROUPS, members // 2 - 1, 2 * SLAB, BLOCK), BF16),
            vmem((width, 3 * SLAB), F32),
            vmem((GROUPS, BLOCK, width), BF16),
            vmem((GROUPS, BLOCK, width), F32),
            vmem((GROUPS, 2, BLOCK, width), BF16),
            vmem((3 * SLAB, 1), F32),
            vmem((shards, 2, 2, 2, sub, rows, 3 * SLAB), BF16),
            vmem((1, 2 * width), F32),
            vmem(buffer, BF16),
            dma((GROUPS,)), dma((GROUPS,)),
            dma((GROUPS, members // 2)), dma((GROUPS, members // 2)),
            dma((GROUPS, 4)), dma((GROUPS, 2, 4)), dma((6,)),
            *scratch,
        ],
        compiler_params=pltpu.CompilerParams(
            collective_id=ident, has_side_effects=True, vmem_limit_bytes=VMEM_LIMIT
        ),
    )(gat, lse, w_group, mid, small, *saved, *terms)
    return (result[0], *sums, *result[1:]) if apart else result


def on_device(
    tokens, doc_ids, qkv_weight, qv_bias, out_weight, out_bias, mid_gain, mid_shift,
    up_weight, up_bias, down_weight, down_bias, end_gain, end_shift, out_grad,
):
    width, hidden = tokens.shape[2], up_weight.shape[1]
    ring, shards = lax.axis_size("rep"), lax.axis_size("shard")
    levels = ring // 4
    sub = levels // GROUPS
    x = tokens[0]
    small = (qv_bias, out_bias, mid_gain, mid_shift, up_bias, down_bias, end_gain, end_shift)
    sizes = [v.shape[0] for v in small]
    own = (out_weight, up_weight, down_weight)
    att, flat, w_group, lse, o, q, k, kt, vt, x_rows, *full = forward_all(
        x, qkv_weight, doc_ids, [v.reshape(1, -1) for v in small], own, ((2, 0, 1, True), (0, 0, 1, False), (1, 0, 2, False)), ring, shards, 0
    )
    down_chunks = 6 if hidden % (6 * shards * ring * 16) == 0 else 1
    layer_out, gat, mid, flat, down, up, out = mlp_all(
        att, x, out_grad[0], flat, own, full, sizes, shards, levels, down_chunks, 6
    )
    input_grad, down, up, out, qkv, flat = tail_all(
        gat, lse, w_group, mid, flat, (q, k, kt, vt, o, x_rows), (down, up, out), sizes[0],
        ring, shards, 1,
    )
    total_down = down.reshape(-1, width).astype(F32)
    if up.ndim > 2:
        up = up.reshape(12, width // shards, -1).transpose(1, 0, 2).reshape(-1, hidden)
        out = out.reshape(2, width // shards, -1).transpose(1, 0, 2).reshape(-1, width)
    if qkv.ndim > 2:
        qkv = qkv.reshape(8, GROUPS, sub, -1, 3, SLAB).transpose(0, 2, 3, 4, 1, 5)
        qkv = qkv.reshape(-1, 3 * width)
    total_up, total_out, total_qkv = up.astype(F32), out.astype(F32), qkv.astype(F32)
    flat = flat.reshape(-1)
    totals, at = [], 0
    for size in sizes:
        totals.append(flat[at : at + size])
        at += size
    return (
        layer_out[None], input_grad[None], total_qkv, totals[0], total_out, totals[1], totals[2],
        totals[3], total_up, totals[4], total_down, totals[5], totals[6], totals[7],
    )


def solution(mesh):
    rows = P("shard", None)
    flat = P("shard")
    acts = P("shard", "rep", None)
    in_specs = (
        acts, rows, rows, flat, rows, flat, flat, flat, rows, flat, rows, flat, flat, flat, acts
    )
    out_specs = (acts, acts, rows, flat, rows, flat, flat, flat, rows, flat, rows, flat, flat, flat)
    return jax.shard_map(
        on_device, mesh=mesh, in_specs=in_specs, out_specs=out_specs, check_vma=False
    )
```

time: 483 us -> 330 us (0.68)
  local copies, waits for them, and re-layouts: 82.8 us -> 15.6 us
  Pallas kernels: 345 us -> 302 us
  matrix products: 35.7 us -> 0 us
    pallas_call x5 -> x3, Pallas kernels: 345 us -> 302 us  [the longest x1 204 us: tail_all(): pl.pallas_call(lambda *refs: tail_kernel(ring, shards, specs, chunk_shape...]
    dot_general x9 -> x0, matrix products: 35.7 us -> none  [mm(): return lax.dot_general(left, right, dims, preferred_element_type=F32)]
    convert_element_type x5 -> x0, local copies, waits for them, and re-layouts: 20 us -> none  [the longest x3 15.9 us: on_device(): total_qkv = total_qkv.reshape(-1, 3 * width).astype(F32)]
    unnamed x85 -> x9, local copies, waits for them, and re-layouts: 19.7 us -> 1.56 us
    reshape x15 -> x8, local copies, waits for them, and re-layouts: 25.9 us -> 10 us  [on_device(): v.reshape(1, -1)]
    convert_element_type x1 -> x3, other arithmetic: 1.33 us -> 6.94 us  [the longest x1 2.76 us: on_device(): up.astype(F32)]
where the time goes in v3:
time: 330 us; the launch traced here: 328 us
  Pallas kernels  302 us (92%)
  local copies, waits for them, and re-layouts  15.6 us (5%)
  other arithmetic  9.48 us (3%)
    pallas_call x1, Pallas kernels, tail_all(): pl.pallas_call(lambda *refs: tail_kernel(ring, shards, specs, chunk_shape...  204 us
    pallas_call x1, Pallas kernels, forward_all(): pl.pallas_call(lambda *refs: forward_kernel(ring, shards, parts, sizes, *...  80.2 us
    pallas_call x1, Pallas kernels, mlp_all(): pl.pallas_call(lambda *refs: mlp_kernel(shards, sizes, *refs), out_shape=...  18.1 us
    reshape x8, local copies, waits for them, and re-layouts, on_device(): v.reshape(1, -1)  10 us

profile of v3, /device:TPU:1, one launch (start us, length us, event | category | flops | bytes accessed | tf_op | source)
XLA Modules:
  0.0 327.7 jit_solution(10605626041743747741)
XLA Ops:
  0.6 1.2 reshape.62.refs_4_
  1.9 1.2 reshape.63.refs_5_
  3.1 1.2 reshape.64.refs_6_
  4.4 1.2 reshape.66.refs_8_
  5.6 1.2 reshape.67.refs_9_
  6.9 1.2 reshape.68.refs_10_
  8.1 1.3 reshape.61.refs_3_
  9.4 1.3 reshape.65.refs_7_
  10.7 80.2 %shard_map.254 = (bf16[4,192,256]{2,1,0:T(8,128)(2,1)}, f32[2,1,4608]{2,1,0:T(1,128)}, bf16[576,768]{1,0:T(8,128)(2,1)}, f32[4,3,1,256]{3,2,1,0:T(1,128)}, f32[4...) custom-call(bf16[256,768]{1,0:T(8,128)(2,1)} %bitcast.4, ...), custom_call_target="tpu_custom_call" | custom-call | tf_op jit(solution)/shard_map/pallas_call | solution.py:382
  90.8 18.1 %shard_map.255 = (bf16[256,768]{1,0:T(8,128)(2,1)}, bf16[4,192,256]{2,1,0:T(8,128)(2,1)}, f32[256,768]{1,0:T(8,128)}, f32[2,1,4608]{2,1,0:T(1,128)}, bf16[2,6,2,...) custom-call(bf16[4,192,256]{2,1,0:T(8,128)(2,1)} %get-tuple-element., ...), custom_call_target="tpu_custom_call" | custom-call | tf_op jit(solution)/shard_map/pallas_call | solution.py:546
  109.0 203.6 %shard_map.256 = (bf16[256,768]{1,0:T(8,128)(2,1)}, bf16[1536,768]{1,0:T(8,128)(2,1)}, bf16[384,3072]{1,0:T(8,128)(2,1)}, bf16[384,768]{1,0:T(8,128)(2,1)}, bf16...) custom-call(bf16[4,192,256]{2,1,0:T(8,128)(2,1)} %get-tuple-element.46.refs_0_, f32[4,3,1,256]{3,2,1,0:T(1,128)} %get-tuple-element.47.refs_1_, ...), custom_call_target="tpu_custom_call" | custom-call | tf_op jit(solution)/shard_map/pallas_call | solution.py:1168
  312.6 0.0 copy-start.2
  312.6 1.4 slice_reduce_fusion.1
  314.0 1.3 slice_reduce_fusion
  315.3 1.3 slice_reduce_fusion.2
  316.6 2.2 convert_element_type.13
  318.8 0.0 copy-done.2
  318.8 0.0 copy-start.1
  318.8 2.0 convert_element_type.12
  320.8 0.8 copy-done.1
  321.6 0.0 copy-start
  321.6 2.8 convert_element_type.14
  324.4 0.0 copy-done
  324.4 0.0 copy-start.3
  324.4 2.5 convert_element_type.15
  326.9 0.0 copy-done.3
  326.9 0.7 copy.30
Async XLA Ops:
  312.6 6.2 %copy-start.2 = (bf16[384,2304]{1,0:T(8,128)(2,1)S(1)}, bf16[384,2304]{1,0:T(8,128)(2,1)}, u32[]{:S(2)}) copy-start(bf16[384,2304]{1,0:T(8,128)(2,1)} %get-tuple-element.61) | copy-start | bytes 5308420
  318.8 2.8 copy-start.1
  321.6 2.8 copy-start
  324.4 2.5 copy-start.3

commit v4 on v3

--- a/solution.py
+++ b/solution.py
@@ -98,15 +98,19 @@
     above, below = z < levels - 1, z > 0
     hello(net.partners())
 
-    def move(b, kind, src=None):
+    halves = 2
+
+    def move(b, kind, u, src=None):
         target = (r + 4, r - 4, yn, sib)[kind]
-        src = xa_ref.at[b] if src is None else src
-        return remote(src, xa_ref.at[b], send.at[kind, b], recv.at[b], target, s)
-
-    pl.when(above)(lambda: move(r, 0, x_ref).start())
-    pl.when(below)(lambda: move(r, 1, x_ref).start())
-    move(r, 2, x_ref).start()
-    move(r, 3, x_ref).start()
+        rows = pl.ds(u * (BLOCK // halves), BLOCK // halves)
+        src = xa_ref.at[b, rows] if src is None else src.at[rows]
+        return remote(src, xa_ref.at[b, rows], send.at[kind, b, u], recv.at[b, u], target, s)
+
+    for u in range(halves):
+        pl.when(above)(lambda: move(r, 0, u, x_ref).start())
+        pl.when(below)(lambda: move(r, 1, u, x_ref).start())
+        move(r, 2, u, x_ref).start()
+        move(r, 3, u, x_ref).start()
     xa_ref[r] = x_ref[...]
 
     width = x_ref.shape[1]
@@ -118,13 +122,13 @@
                 [w_ref[:, t * width + k * SLAB : t * width + (k + 1) * SLAB] for t in range(3)], 1
             )
 
-    flat_ref[s] = jnp.concatenate([v[...].astype(F32) for v in vec_refs], axis=1)
+    flat_ref[s] = jnp.concatenate([v[...].astype(F32).reshape(1, -1) for v in vec_refs], axis=1)
     lists = [
         remote(flat_ref.at[s], flat_ref.at[s], vsend.at[d], vrecv.at[d], r, t)
         for d, t in enumerate(others)
     ]
     pieces = [(lambda rows: wl_ref.at[s, rows], wl_ref, w_ref.shape[0] // 2, 0, False)]
-    for w, first, count, quad in parts:
+    for w, count, quad in parts:
         size = own[w].shape[0] // (4 if quad else 2) // count
         for j in range(count):
             pieces.append((lambda rows, w=w: own[w].at[rows], full[w], size, (count, j), quad))
@@ -213,15 +217,16 @@
 
         @pl.when(n > 0)
         def _():
-            move(b, 3).wait_recv()
-
-            @pl.when(j == 0)
-            def _():
-                pl.when(jnp.logical_and(lv < z, above))(lambda: move(b, 0).start())
-                pl.when(jnp.logical_and(lv > z, below))(lambda: move(b, 1).start())
-                move(b, 2).start()
-
-            pl.when(j < 2)(lambda: move(b, 3).start())
+            for u in range(halves):
+                move(b, 3, u).wait_recv()
+
+                @pl.when(j == 0)
+                def _():
+                    pl.when(jnp.logical_and(lv < z, above))(lambda: move(b, 0, u).start())
+                    pl.when(jnp.logical_and(lv > z, below))(lambda: move(b, 1, u).start())
+                    move(b, 2, u).start()
+
+                pl.when(j < 2)(lambda: move(b, 3, u).start())
 
         both = mm(wg_ref[SLAB:, :], xa_ref[b], NT)
         kt = both[:SLAB].astype(BF16)
@@ -281,7 +286,7 @@
     top_ref[...] = jnp.full(top_ref.shape, -jnp.inf, F32)
     sum_ref[...] = jnp.zeros(sum_ref.shape, F32)
     o_ref[...] = jnp.zeros(o_ref.shape, F32)
-    lag = 5
+    lag = 4
     turn_on = ring - 5
 
     def advance(n, carry):
@@ -344,13 +349,15 @@
     def sent(e, carry):
         b, lv, j = event(e)
 
-        @pl.when(j == 0)
-        def _():
-            pl.when(jnp.logical_and(lv <= z, above))(lambda: move(b, 0).wait_send())
-            pl.when(jnp.logical_and(lv >= z, below))(lambda: move(b, 1).wait_send())
-            move(b, 2).wait_send()
-
-        pl.when(j < 2)(lambda: move(b, 3).wait_send())
+        for u in range(halves):
+
+            @pl.when(j == 0)
+            def _():
+                pl.when(jnp.logical_and(lv <= z, above))(lambda: move(b, 0, u).wait_send())
+                pl.when(jnp.logical_and(lv >= z, below))(lambda: move(b, 1, u).wait_send())
+                move(b, 2, u).wait_send()
+
+            pl.when(j < 2)(lambda: move(b, 3, u).wait_send())
         return carry
 
     lax.fori_loop(0, ring, sent, 0)
@@ -371,9 +378,9 @@
     shape = jax.ShapeDtypeStruct
     dma = pltpu.SemaphoreType.DMA
     vmem = pltpu.VMEM
-    n = 1 + sum(part[2] for part in parts)
+    n = 1 + sum(part[1] for part in parts)
     width = x.shape[1]
-    sizes = [v.shape[1] for v in vectors]
+    sizes = [v.shape[0] for v in vectors]
     per = max(shards - 1, 1)
     o = (GROUPS, SLAB, BLOCK)
     q = (GROUPS, PER, 2 * HEAD_DIM, BLOCK)
@@ -394,7 +401,7 @@
             vmem(o, BF16), vmem((2 * SLAB, 1), F32), vmem(o, F32), vmem(q, BF16), vmem(k, BF16),
             vmem(t, BF16), vmem(t, BF16),
             vmem((GROUPS, PER, 1, BLOCK), F32), vmem((GROUPS, PER, 1, BLOCK), F32),
-            dma((4, ring)), dma((ring,)), dma((n, per)), dma((n, per)), dma((n, per, 3)),
+            dma((4, ring, 2)), dma((ring, 2)), dma((n, per)), dma((n, per)), dma((n, per, 3)),
             dma((n, per, 3)), dma((per,)), dma((per,)),
             dma((GROUPS,)), dma((GROUPS,)), dma((5 + GROUPS,)),
         ],
@@ -587,12 +594,32 @@
     )
     one, two, four = out
     mine = one(c, y, z)
-    spread = lambda d: remote(
-        mine, mine, esend.at[d], erecv.at[d], net.heights[d] * 4 + net.line, s
-    )
+    levels = net.levels
+
+    def climb(k, up):
+        at = z - k if up else z + k
+        piece = one(c, y, at)
+        target = (z + 1 if up else z - 1) * 4 + net.line
+        return remote(piece, piece, esend.at[int(up), k], erecv.at[int(up), k], target, s)
+
+    def landed(k, up):
+        at = z - k if up else z + k
+        piece = one(c, y, at)
+        return remote(piece, piece, esend.at[int(up), k], erecv.at[int(up), k - 1], net.r, s)
+
+    def both_ways(k, act):
+        here = (z - k >= 0, z + k < levels)
+        more = (z + 1 < levels, z > 0)
+        pl.when(jnp.logical_and(here[0], more[0]))(lambda: act(True))
+        pl.when(jnp.logical_and(here[1], more[1]))(lambda: act(False))
+
+    def wait_from(k):
+        pl.when(z - k >= 0)(lambda: landed(k, True).wait_recv())
+        pl.when(z + k < levels)(lambda: landed(k, False).wait_recv())
+
     pair = lambda: remote(two(c, y), two(c, y), fsend, frecv, net.yn, s)
     last = lambda: remote(four(c), four(c), gsend, grecv, net.sib, s)
-    n_side, n_inner, n_tall = len(net.others), len(inner), len(net.heights)
+    n_side, n_inner = len(net.others), len(inner)
 
     def step0():
         near_copy().start()
@@ -626,12 +653,17 @@
         for d in range(n_inner):
             along(d).wait_recv()
         add_rows(mine, [near.at[s, y, zz]] + [tall.at[d] for d in range(n_inner)])
-        for d in range(n_tall):
-            spread(d).start()
+        both_ways(0, lambda up: climb(0, up).start())
+
+    def onward(k):
+        def step():
+            wait_from(k)
+            both_ways(k, lambda up: climb(k, up).start())
+
+        return step
 
     def step5():
-        for d in range(n_tall):
-            spread(d).wait_recv()
+        wait_from(levels - 1)
         pair().start()
 
     def step6():
@@ -648,12 +680,13 @@
         over().wait_send()
         for d in range(n_inner):
             along(d).wait_send()
-        for d in range(n_tall):
-            spread(d).wait_send()
+        for k in range(levels - 1):
+            both_ways(k, lambda up: climb(k, up).wait_send())
         pair().wait_send()
         last().wait_send()
 
-    return [step0, step1, step2, step3, step4, step5, step6, step7], drain
+    middle = [onward(k) for k in range(1, levels - 1)]
+    return [step0, step1, step2, step3, step4, *middle, step5, step6, step7], drain
 
 
 def reduce_scratch(shards, levels, group, rows, cols):
@@ -669,7 +702,7 @@
     ]
     sems = [
         dma(()), dma(()), many(shards - 1), many(shards - 1), dma(()), dma(()),
-        many(group - 1), many(group - 1), many(levels - 1), many(levels - 1),
+        many(group - 1), many(group - 1), dma((2, levels)), dma((2, levels)),
         dma(()), dma(()), dma(()), dma(()), dma(()),
     ]
     return buffers + sems
@@ -803,7 +836,7 @@
     net = Links(ring, shards)
     hello(net.partners())
     jobs, drains, _ = term_jobs(net, specs, chunk_shapes, refs[:n], refs[n : 2 * n], refs[2 * n :])
-    for steps in spread_out(jobs, OFFSETS):
+    for steps in spread_out(jobs, offsets(net.levels)):
         for step in steps:
             step()
     for drain in drains:
@@ -860,7 +893,7 @@
 
     jobs, drains, rest = term_jobs(net, specs, chunk_shapes, terms, outs, rest)
     qkv_jobs = []
-    for k in range(2):
+    for k in range(QKV_CHUNKS):
         steps, drain = reduce_steps(
             net, lambda core, k=k: dwl_ref.at[:, k, core], places(all_ref, k, False, levels, 0, 0),
             *rest[:5], rest[5:SCRATCH], sub
@@ -870,7 +903,31 @@
         rest = rest[SCRATCH:]
     vec_steps, drain = small_steps(net, small_ref, total_small, *rest[:4], rest[4:])
     drains.append(drain)
-    ticks = spread_out(jobs, OFFSETS)
+    ticks = spread_out(jobs, offsets(levels))
+
+    width = w_ref.shape[1]
+
+    def prepare():
+        dwl_ref[...] = dw_ref[...].astype(BF16).reshape(dwl_ref.shape)
+        row = jnp.broadcast_to(db_ref[...], (3 * SLAB, 8)).T[:1]
+        row_ref[...] = jnp.zeros(row_ref.shape, F32)
+        for k in range(GROUPS):
+
+            @pl.when(g == k)
+            def _():
+                row_ref[:, k * SLAB : (k + 1) * SLAB] = row[:, :SLAB]
+                row_ref[:, width + k * SLAB : width + (k + 1) * SLAB] = row[:, 2 * SLAB :]
+
+        for t in range(shards):
+            small_ref[t, :, :n0] = row_ref[:, t * n0 : (t + 1) * n0]
+
+    ready = -(-(10 * members + 2 + SHIFTS[0] + 1) // PACE)
+    late = [[list(steps) for steps in zip(*qkv_jobs)], [[step] for step in vec_steps]]
+    ticks += [[] for _ in range(ready + max(map(len, late)) - len(ticks))]
+    ticks[ready].append(prepare)
+    for series in late:
+        for t, steps in enumerate(series):
+            ticks[ready + t] += steps
 
     def tick(t, lo, hi):
         if hi - lo == 1:
@@ -1051,46 +1108,18 @@
             pl.when(n_due > n_done)(lambda: act(GROUPS - n_due))
 
         at_times(0, merge)
-        at_times(1, finish)
+        at_times(SHIFTS[0], finish)
         for depth in range(1, GROUPS - 1):
-            at_times(1 + depth, lambda j, depth=depth: start_dx(j, depth))
+            at_times(SHIFTS[depth], lambda j, depth=depth: start_dx(j, depth))
         return carry
 
-    count = max(finishes[-1] + 2, PACE * len(ticks))
-    lax.fori_loop(0, count, advance, 0)
-
-    width = w_ref.shape[1]
-    dwl_ref[...] = dw_ref[...].astype(BF16).reshape(dwl_ref.shape)
-    row = jnp.broadcast_to(db_ref[...], (3 * SLAB, 8)).T[:1]
-    row_ref[...] = jnp.zeros(row_ref.shape, F32)
-    for k in range(GROUPS):
-
-        @pl.when(g == k)
-        def _():
-            row_ref[:, k * SLAB : (k + 1) * SLAB] = row[:, :SLAB]
-            row_ref[:, width + k * SLAB : width + (k + 1) * SLAB] = row[:, 2 * SLAB :]
-
-    for t in range(shards):
-        small_ref[t, :, :n0] = row_ref[:, t * n0 : (t + 1) * n0]
-    for job in qkv_jobs:
-        job[0]()
-    vec_steps[0]()
-    for depth in range(1, GROUPS - 1):
-        if count <= finishes[-1] + 1 + depth:
-            start_dx(0, depth)
-    for job in qkv_jobs:
-        job[1]()
-    vec_steps[1]()
+    lax.fori_loop(0, PACE * len(ticks), advance, 0)
+
     own_dx()
     out_ref[...] = (near_ref[g] + mid_ref[...]).astype(BF16)
-    for t in range(2, 8):
-        for job in qkv_jobs:
-            job[t]()
-        if t < len(vec_steps):
-            vec_steps[t]()
     if len(qkv_ref.shape) == 2:
         rows = all_ref.shape[-2]
-        for part in range(8):
+        for part in range(4 * QKV_CHUNKS):
             for z in range(levels):
                 at = (part * sub + z % sub) * rows
                 piece = all_ref[part // 4, part // 2 % 2, part % 2, z]
@@ -1114,7 +1143,15 @@
 
 
 PACE = 2
-OFFSETS = (0, 1, 3, 4, 5, 6, 7, 8)
+QKV_CHUNKS = 3
+
+
+def offsets(levels, gaps=(2, 2, 2, 2, 2, 2, 2, 2)):
+    steps = gaps[:4] + gaps[4:5] * (levels - 2) + gaps[5:]
+    return [sum(steps[:t]) for t in range(len(steps) + 1)]
+
+
+SHIFTS = (2, 5, 7)
 
 
 def tail_all(gat, lse, w_group, mid, small, saved, terms, n0, ring, shards, ident):
@@ -1157,10 +1194,10 @@
     scratch = [] if apart else list(term_scratch)
     out_shape = [] if apart else list(term_shapes)
     terms = () if apart else terms
-    rows = part // 8 // sub
-    buffer = (2, 2, 2, levels, rows, 3 * SLAB)
-    scratch += reduce_scratch(shards, levels, sub, rows, 3 * SLAB)
-    scratch += reduce_scratch(shards, levels, sub, rows, 3 * SLAB)
+    rows = part // (4 * QKV_CHUNKS) // sub
+    buffer = (QKV_CHUNKS, 2, 2, levels, rows, 3 * SLAB)
+    for _ in range(QKV_CHUNKS):
+        scratch += reduce_scratch(shards, levels, sub, rows, 3 * SLAB)
     scratch += small_scratch(shards, levels, small.shape[2])
     out_shape.append(shape(buffer if rows % 16 else (part, 3 * width), BF16))
     slab = (GROUPS, SLAB, BLOCK)
@@ -1188,7 +1225,7 @@
             vmem((GROUPS, BLOCK, width), F32),
             vmem((GROUPS, 2, BLOCK, width), BF16),
             vmem((3 * SLAB, 1), F32),
-            vmem((shards, 2, 2, 2, sub, rows, 3 * SLAB), BF16),
+            vmem((shards, QKV_CHUNKS, 2, 2, sub, rows, 3 * SLAB), BF16),
             vmem((1, 2 * width), F32),
             vmem(buffer, BF16),
             dma((GROUPS,)), dma((GROUPS,)),
@@ -1216,7 +1253,7 @@
     sizes = [v.shape[0] for v in small]
     own = (out_weight, up_weight, down_weight)
     att, flat, w_group, lse, o, q, k, kt, vt, x_rows, *full = forward_all(
-        x, qkv_weight, doc_ids, [v.reshape(1, -1) for v in small], own, ((2, 0, 1, True), (0, 0, 1, False), (1, 0, 2, False)), ring, shards, 0
+        x, qkv_weight, doc_ids, list(small), own, ((2, 1, True), (0, 1, False), (1, 2, False)), ring, shards, 0
     )
     down_chunks = 6 if hidden % (6 * shards * ring * 16) == 0 else 1
     layer_out, gat, mid, flat, down, up, out = mlp_all(
@@ -1231,7 +1268,7 @@
         up = up.reshape(12, width // shards, -1).transpose(1, 0, 2).reshape(-1, hidden)
         out = out.reshape(2, width // shards, -1).transpose(1, 0, 2).reshape(-1, width)
     if qkv.ndim > 2:
-        qkv = qkv.reshape(8, GROUPS, sub, -1, 3, SLAB).transpose(0, 2, 3, 4, 1, 5)
+        qkv = qkv.reshape(4 * QKV_CHUNKS, GROUPS, sub, -1, 3, SLAB).transpose(0, 2, 3, 4, 1, 5)
         qkv = qkv.reshape(-1, 3 * width)
     total_up, total_out, total_qkv = up.astype(F32), out.astype(F32), qkv.astype(F32)
     flat = flat.reshape(-1)

time: 330 us -> 278 us (0.84)
  Pallas kernels: 302 us -> 262 us
  local copies, waits for them, and re-layouts: 15.6 us -> 5.59 us
    pallas_call x1, Pallas kernels: 204 us -> 166 us  [tail_all(): pl.pallas_call(lambda *refs: tail_kernel(ring, shards, specs, chunk_shape...]
    reshape x8 -> x0, local copies, waits for them, and re-layouts: 10 us -> none  [on_device(): v.reshape(1, -1)]
where the time goes in v4:
time: 278 us
  Pallas kernels  262 us (94%)
  other arithmetic  9.48 us (3%)
  local copies, waits for them, and re-layouts  5.59 us (2%)
    pallas_call x1, Pallas kernels, tail_all(): pl.pallas_call(lambda *refs: tail_kernel(ring, shards, specs, chunk_shape...  166 us
    pallas_call x1, Pallas kernels, forward_all(): pl.pallas_call(lambda *refs: forward_kernel(ring, shards, parts, sizes, *...  77.6 us
    pallas_call x1, Pallas kernels, mlp_all(): pl.pallas_call(lambda *refs: mlp_kernel(shards, sizes, *refs), out_shape=...  18.1 us

profile of v4, /device:TPU:1, one launch (start us, length us, event | category | flops | bytes accessed | tf_op | source)
XLA Modules:
  0.0 277.6 jit_solution(16024982588606295428)
XLA Ops:
  0.6 77.6 %shard_map.254 = (bf16[4,192,256]{2,1,0:T(8,128)(2,1)}, f32[2,1,4608]{2,1,0:T(1,128)}, bf16[576,768]{1,0:T(8,128)(2,1)}, f32[4,3,1,256]{3,2,1,0:T(1,128)}, f32[4...) custom-call(bf16[256,768]{1,0:T(8,128)(2,1)} %bitcast.4, ...), custom_call_target="tpu_custom_call" | custom-call | tf_op jit(solution)/shard_map/pallas_call | solution.py:389
  78.3 18.1 %shard_map.255 = (bf16[256,768]{1,0:T(8,128)(2,1)}, bf16[4,192,256]{2,1,0:T(8,128)(2,1)}, f32[256,768]{1,0:T(8,128)}, f32[2,1,4608]{2,1,0:T(1,128)}, bf16[2,6,2,...) custom-call(bf16[4,192,256]{2,1,0:T(8,128)(2,1)} %get-tuple-element., ...), custom_call_target="tpu_custom_call" | custom-call | tf_op jit(solution)/shard_map/pallas_call | solution.py:553
  96.4 166.1 %shard_map.256 = (bf16[256,768]{1,0:T(8,128)(2,1)}, bf16[1536,768]{1,0:T(8,128)(2,1)}, bf16[384,3072]{1,0:T(8,128)(2,1)}, bf16[384,768]{1,0:T(8,128)(2,1)}, bf16...) custom-call(bf16[4,192,256]{2,1,0:T(8,128)(2,1)} %get-tuple-element.46.refs_0_, f32[4,3,1,256]{3,2,1,0:T(1,128)} %get-tuple-element.47.refs_1_, ...), custom_call_target="tpu_custom_call" | custom-call | tf_op jit(solution)/shard_map/pallas_call | solution.py:1205
  262.5 0.0 copy-start.2
  262.5 1.4 slice_reduce_fusion.1
  263.9 1.3 slice_reduce_fusion
  265.2 1.3 slice_reduce_fusion.2
  266.5 2.2 convert_element_type.13
  268.7 0.0 copy-done.2
  268.7 0.0 copy-start.1
  268.7 2.0 convert_element_type.12
  270.7 0.8 copy-done.1
  271.5 0.0 copy-start
  271.5 2.8 convert_element_type.14
  274.3 0.0 copy-done
  274.3 0.0 copy-start.3
  274.3 2.5 convert_element_type.15
  276.8 0.0 copy-done.3
  276.8 0.7 copy.30
Async XLA Ops:
  262.5 6.2 %copy-start.2 = (bf16[384,2304]{1,0:T(8,128)(2,1)S(1)}, bf16[384,2304]{1,0:T(8,128)(2,1)}, u32[]{:S(2)}) copy-start(bf16[384,2304]{1,0:T(8,128)(2,1)} %get-tuple-element.61) | copy-start | bytes 5308420
  268.7 2.8 %copy-start.1 = (bf16[384,3072]{1,0:T(8,128)(2,1)S(1)}, bf16[384,3072]{1,0:T(8,128)(2,1)}, u32[]{:S(2)}) copy-start(bf16[384,3072]{1,0:T(8,128)(2,1)} %get-tuple-element.64) | copy-start | bytes 7077892
  271.5 2.8 copy-start
  274.3 2.5 copy-start.3

commit v5 on v4

--- a/solution.py
+++ b/solution.py
@@ -592,7 +592,7 @@
         near.at[s, y, inner[d]], tall.at[d], dsend.at[d], drecv.at[d],
         (base + inner[d]) * 4 + net.line, s,
     )
-    one, two, four = out
+    one, four = out
     mine = one(c, y, z)
     levels = net.levels
 
@@ -617,7 +617,17 @@
         pl.when(z - k >= 0)(lambda: landed(k, True).wait_recv())
         pl.when(z + k < levels)(lambda: landed(k, False).wait_recv())
 
-    pair = lambda: remote(two(c, y), two(c, y), fsend, frecv, net.yn, s)
+
+    def pair(at):
+        return remote(one(c, y, at), one(c, y, at), fsend.at[at], frecv.at[at], net.yn, s)
+
+    def pair_from(k):
+        if k:
+            pl.when(z - k >= 0)(lambda: pair(z - k).start())
+            pl.when(z + k < levels)(lambda: pair(z + k).start())
+        else:
+            pair(z).start()
+
     last = lambda: remote(four(c), four(c), gsend, grecv, net.sib, s)
     n_side, n_inner = len(net.others), len(inner)
 
@@ -654,20 +664,24 @@
             along(d).wait_recv()
         add_rows(mine, [near.at[s, y, zz]] + [tall.at[d] for d in range(n_inner)])
         both_ways(0, lambda up: climb(0, up).start())
+        pair_from(0)
 
     def onward(k):
         def step():
             wait_from(k)
             both_ways(k, lambda up: climb(k, up).start())
+            pair_from(k)
 
         return step
 
     def step5():
         wait_from(levels - 1)
-        pair().start()
+        pair_from(levels - 1)
 
     def step6():
-        pair().wait_recv()
+        for at in range(levels):
+            piece = one(c, 1 - y, at)
+            remote(piece, piece, fsend.at[at], frecv.at[at], net.yn, s).wait_recv()
         last().start()
 
     def step7():
@@ -682,7 +696,8 @@
             along(d).wait_send()
         for k in range(levels - 1):
             both_ways(k, lambda up: climb(k, up).wait_send())
-        pair().wait_send()
+        for at in range(levels):
+            pair(at).wait_send()
         last().wait_send()
 
     middle = [onward(k) for k in range(1, levels - 1)]
@@ -703,7 +718,7 @@
     sems = [
         dma(()), dma(()), many(shards - 1), many(shards - 1), dma(()), dma(()),
         many(group - 1), many(group - 1), dma((2, levels)), dma((2, levels)),
-        dma(()), dma(()), dma(()), dma(()), dma(()),
+        dma((levels,)), dma((levels,)), dma(()), dma(()), dma(()),
     ]
     return buffers + sems
 
@@ -781,8 +796,7 @@
 def places(ref, chunk, core_first, levels, rows, cols):
     if len(ref.shape) != 2:
         return (
-            lambda c, y, z: ref.at[chunk, c, y, z], lambda c, y: ref.at[chunk, c, y],
-            lambda c: ref.at[chunk, c],
+            lambda c, y, z: ref.at[chunk, c, y, z], lambda c: ref.at[chunk, c],
         )
     if core_first:
 
@@ -792,7 +806,6 @@
 
         return (
             lambda c, y, z: view(c, (y * levels + z) * rows, rows),
-            lambda c, y: view(c, y * levels * rows, levels * rows),
             lambda c: view(c, 0, 2 * levels * rows),
         )
 
@@ -802,7 +815,6 @@
 
     return (
         lambda c, y, z: span((c * 2 + y) * levels + z, 1),
-        lambda c, y: span((c * 2 + y) * levels, levels),
         lambda c: span(c * 2 * levels, 2 * levels),
     )
 
@@ -1240,6 +1252,53 @@
     return (result[0], *sums, *result[1:]) if apart else result
 
 
+def widen_kernel(sizes, cuts, flat_ref, *refs):
+    n = len(cuts)
+    sources, targets, vectors = refs[:n], refs[n : 2 * n], refs[2 * n : 2 * n + len(sizes)]
+    low, wide, isem, osem = refs[-2 * n - 2 : -n - 2], refs[-n - 2 : -2], refs[-2], refs[-1]
+    loads, saves = [], []
+    for w, parts in enumerate(cuts):
+        size = sources[w].shape[0] // parts
+        for j in range(parts):
+            rows = pl.ds(j * size, size)
+            at = len(loads)
+            loads.append(pltpu.make_async_copy(sources[w].at[rows], low[w].at[rows], isem.at[at]))
+            saves.append(
+                (w, rows, pltpu.make_async_copy(wide[w].at[rows], targets[w].at[rows], osem.at[at]))
+            )
+    for load in loads:
+        load.start()
+    at = 0
+    for ref, size in zip(vectors, sizes):
+        ref[...] = flat_ref[:, at : at + size].reshape(size)
+        at += size
+    for load, (w, rows, save) in zip(loads, saves):
+        load.wait()
+        wide[w][rows] = low[w][rows].astype(wide[w].dtype)
+        save.start()
+    for _, _, save in saves:
+        save.wait()
+
+
+def widen_all(flat, arrays, same, sizes):
+    shape = jax.ShapeDtypeStruct
+    arrays = (*arrays, same)
+    types = [F32] * (len(arrays) - 1) + [same.dtype]
+    dma = pltpu.SemaphoreType.DMA
+    cuts = [next(n for n in (4, 3, 2, 1) if a.shape[0] % (16 * n) == 0 or n == 1) for a in arrays]
+    return pl.pallas_call(
+        lambda *refs: widen_kernel(sizes, cuts, *refs),
+        out_shape=tuple(shape(a.shape, t) for a, t in zip(arrays, types))
+        + tuple(shape((size,), F32) for size in sizes),
+        in_specs=[VMEM_SPEC] + [ANY_SPEC] * len(arrays),
+        out_specs=(ANY_SPEC,) * len(arrays) + (VMEM_SPEC,) * len(sizes),
+        scratch_shapes=[pltpu.VMEM(a.shape, BF16) for a in arrays]
+        + [pltpu.VMEM(a.shape, t) for a, t in zip(arrays, types)]
+        + [dma((sum(cuts),)), dma((sum(cuts),))],
+        compiler_params=pltpu.CompilerParams(vmem_limit_bytes=VMEM_LIMIT),
+    )(flat, *arrays)
+
+
 def on_device(
     tokens, doc_ids, qkv_weight, qv_bias, out_weight, out_bias, mid_gain, mid_shift,
     up_weight, up_bias, down_weight, down_bias, end_gain, end_shift, out_grad,
@@ -1263,22 +1322,17 @@
         gat, lse, w_group, mid, flat, (q, k, kt, vt, o, x_rows), (down, up, out), sizes[0],
         ring, shards, 1,
     )
-    total_down = down.reshape(-1, width).astype(F32)
+    down = down.reshape(-1, width)
     if up.ndim > 2:
         up = up.reshape(12, width // shards, -1).transpose(1, 0, 2).reshape(-1, hidden)
         out = out.reshape(2, width // shards, -1).transpose(1, 0, 2).reshape(-1, width)
     if qkv.ndim > 2:
         qkv = qkv.reshape(4 * QKV_CHUNKS, GROUPS, sub, -1, 3, SLAB).transpose(0, 2, 3, 4, 1, 5)
         qkv = qkv.reshape(-1, 3 * width)
-    total_up, total_out, total_qkv = up.astype(F32), out.astype(F32), qkv.astype(F32)
-    flat = flat.reshape(-1)
-    totals, at = [], 0
-    for size in sizes:
-        totals.append(flat[at : at + size])
-        at += size
+    down, up, out, qkv, input_grad, *totals = widen_all(flat, (down, up, out, qkv), input_grad, sizes)
     return (
-        layer_out[None], input_grad[None], total_qkv, totals[0], total_out, totals[1], totals[2],
-        totals[3], total_up, totals[4], total_down, totals[5], totals[6], totals[7],
+        layer_out[None], input_grad[None], qkv, totals[0], out, totals[1], totals[2],
+        totals[3], up, totals[4], down, totals[5], totals[6], totals[7],
     )
 
 

time: 278 us -> 269 us (0.968)
  other arithmetic: 9.48 us -> 0 us
  Pallas kernels: 262 us -> 268 us
  local copies, waits for them, and re-layouts: 5.59 us -> 0 us
    convert_element_type x4 -> x0, other arithmetic: 9.48 us -> none  [the longest x1 2.76 us: on_device(): up.astype(F32)]
    pallas_call x0 -> x1, Pallas kernels: none -> 8.67 us  [widen_all(): pl.pallas_call(lambda *refs: widen_kernel(sizes, cuts, *refs), out_shape=...]
    slice x3 -> x0, local copies, waits for them, and re-layouts: 4.03 us -> none  [on_device(): totals.append(flat[at:at + size])]
where the time goes in v5:
time: 269 us
  Pallas kernels  268 us (100%)
    pallas_call x1, Pallas kernels, tail_all(): pl.pallas_call(lambda *refs: tail_kernel(ring, shards, specs, chunk_shape...  164 us
    pallas_call x1, Pallas kernels, forward_all(): pl.pallas_call(lambda *refs: forward_kernel(ring, shards, parts, sizes, *...  77.6 us
    pallas_call x1, Pallas kernels, mlp_all(): pl.pallas_call(lambda *refs: mlp_kernel(shards, sizes, *refs), out_shape=...  18.1 us
    pallas_call x1, Pallas kernels, widen_all(): pl.pallas_call(lambda *refs: widen_kernel(sizes, cuts, *refs), out_shape=...  8.67 us

profile of v5, /device:TPU:1, one launch (start us, length us, event | category | flops | bytes accessed | tf_op | source)
XLA Modules:
  0.0 268.9 jit_solution(826327772964819150)
XLA Ops:
  0.6 77.6 %shard_map.254 = (bf16[4,192,256]{2,1,0:T(8,128)(2,1)}, f32[2,1,4608]{2,1,0:T(1,128)}, bf16[576,768]{1,0:T(8,128)(2,1)}, f32[4,3,1,256]{3,2,1,0:T(1,128)}, f32[4...) custom-call(bf16[256,768]{1,0:T(8,128)(2,1)} %bitcast.4, ...), custom_call_target="tpu_custom_call" | custom-call | tf_op jit(solution)/shard_map/pallas_call | solution.py:389
  78.3 18.1 %shard_map.255 = (bf16[256,768]{1,0:T(8,128)(2,1)}, bf16[4,192,256]{2,1,0:T(8,128)(2,1)}, f32[256,768]{1,0:T(8,128)}, f32[2,1,4608]{2,1,0:T(1,128)}, bf16[2,6,2,...) custom-call(bf16[4,192,256]{2,1,0:T(8,128)(2,1)} %get-tuple-element., ...), custom_call_target="tpu_custom_call" | custom-call | tf_op jit(solution)/shard_map/pallas_call | solution.py:553
  96.4 163.6 %shard_map.256 = (bf16[256,768]{1,0:T(8,128)(2,1)}, bf16[1536,768]{1,0:T(8,128)(2,1)}, bf16[384,3072]{1,0:T(8,128)(2,1)}, bf16[384,768]{1,0:T(8,128)(2,1)}, bf16...) custom-call(bf16[4,192,256]{2,1,0:T(8,128)(2,1)} %get-tuple-element.59.refs_0_, f32[4,3,1,256]{3,2,1,0:T(1,128)} %get-tuple-element.60.refs_1_, ...), custom_call_target="tpu_custom_call" | custom-call | tf_op jit(solution)/shard_map/pallas_call | solution.py:1217
  260.0 8.7 %shard_map.257 = (f32[1536,768]{1,0:T(8,128)}, f32[384,3072]{1,0:T(8,128)}, f32[384,768]{1,0:T(8,128)}, f32[384,2304]{1,0:T(8,128)}, bf16[256,768]{1,0:T(8,128)(...) custom-call(f32[1,4608]{1,0:T(1,128)} %get-tuple-element.73.refs_0_,, ...), custom_call_target="tpu_custom_call" | custom-call | tf_op jit(solution)/shard_map/pallas_call | solution.py:1289

commit v6 on v5

--- a/solution.py
+++ b/solution.py
@@ -865,10 +865,15 @@
     (
         q_ref, k_ref, kt_ref, vt_ref, o_ref,
         g_ref, x_ref, v_ref, delta_ref, acc_ref, dk_ref, dv_ref, pq_ref, stage_ref, got_ref, got2_ref,
-        dw_ref, dx_ref, near_ref, far_ref, db_ref, dwl_ref, row_ref, all_ref,
+        dw_ref, dx_ref, near_ref, far_ref, db_ref, dwl_ref, row_ref, sum_ref, all_ref,
         gsend, grecv, ksend, krecv, xsend, xrecv, lsem,
-    ) = refs[3 + n_terms : 34 + n_terms]
-    rest = refs[34 + n_terms :]
+    ) = refs[3 + n_terms : 35 + n_terms]
+    finals, rest = outs, refs[35 + n_terms :]
+    outs, rest = rest[:n_terms], rest[n_terms:]
+    copies = [
+        pltpu.make_async_copy(src, dst, lsem.at[6 + n])
+        for n, (src, dst) in enumerate(zip(outs, finals))
+    ]
     net = Links(ring, shards)
     r, s = net.r, net.s
     levels, members = net.levels, ring // GROUPS
@@ -913,7 +918,7 @@
         qkv_jobs.append(steps)
         drains.append(drain)
         rest = rest[SCRATCH:]
-    vec_steps, drain = small_steps(net, small_ref, total_small, *rest[:4], rest[4:])
+    vec_steps, drain = small_steps(net, sum_ref, total_small, *rest[:4], rest[4:])
     drains.append(drain)
     ticks = spread_out(jobs, offsets(levels))
 
@@ -930,10 +935,12 @@
                 row_ref[:, k * SLAB : (k + 1) * SLAB] = row[:, :SLAB]
                 row_ref[:, width + k * SLAB : width + (k + 1) * SLAB] = row[:, 2 * SLAB :]
 
+        sum_ref[...] = small_ref[...]
         for t in range(shards):
-            small_ref[t, :, :n0] = row_ref[:, t * n0 : (t + 1) * n0]
+            sum_ref[t, :, :n0] = row_ref[:, t * n0 : (t + 1) * n0]
 
     ready = -(-(10 * members + 2 + SHIFTS[0] + 1) // PACE)
+    ticks.append([copy.start for copy in copies])
     late = [[list(steps) for steps in zip(*qkv_jobs)], [[step] for step in vec_steps]]
     ticks += [[] for _ in range(ready + max(map(len, late)) - len(ticks))]
     ticks[ready].append(prepare)
@@ -1127,6 +1134,8 @@
 
     lax.fori_loop(0, PACE * len(ticks), advance, 0)
 
+    for copy in copies:
+        copy.wait()
     own_dx()
     out_ref[...] = (near_ref[g] + mid_ref[...]).astype(BF16)
     if len(qkv_ref.shape) == 2:
@@ -1218,7 +1227,7 @@
         lambda *refs: tail_kernel(ring, shards, specs, chunk_shapes, n0, *refs),
         out_shape=(shape((BLOCK, width), BF16), *out_shape, shape((1, small.shape[2]), F32)),
         in_specs=[VMEM_SPEC] * 5 + [ANY_SPEC] * (6 + len(terms)),
-        out_specs=(VMEM_SPEC,) * (3 + len(terms)),
+        out_specs=(VMEM_SPEC,) + (ANY_SPEC,) * len(terms) + (VMEM_SPEC,) * 2,
         scratch_shapes=[
             vmem((GROUPS, PER, 2 * HEAD_DIM, BLOCK), BF16),
             vmem((PER, ring * BLOCK, 2 * HEAD_DIM), BF16),
@@ -1239,10 +1248,12 @@
             vmem((3 * SLAB, 1), F32),
             vmem((shards, QKV_CHUNKS, 2, 2, sub, rows, 3 * SLAB), BF16),
             vmem((1, 2 * width), F32),
+            vmem(small.shape, F32),
             vmem(buffer, BF16),
             dma((GROUPS,)), dma((GROUPS,)),
             dma((GROUPS, members // 2)), dma((GROUPS, members // 2)),
-            dma((GROUPS, 4)), dma((GROUPS, 2, 4)), dma((6,)),
+            dma((GROUPS, 4)), dma((GROUPS, 2, 4)), dma((9,)),
+            *(vmem(o.shape, BF16) for o in out_shape[: len(terms)]),
             *scratch,
         ],
         compiler_params=pltpu.CompilerParams(

time: 269 us -> 268 us (level)
  no operation moved by 1% of the time
where the time goes in v6:
time: 268 us; the launch traced here: 267 us
  Pallas kernels  267 us (100%)
    pallas_call x1, Pallas kernels, tail_all(): pl.pallas_call(lambda *refs: tail_kernel(ring, shards, specs, chunk_shape...  162 us
    pallas_call x1, Pallas kernels, forward_all(): pl.pallas_call(lambda *refs: forward_kernel(ring, shards, parts, sizes, *...  77.6 us
    pallas_call x1, Pallas kernels, mlp_all(): pl.pallas_call(lambda *refs: mlp_kernel(shards, sizes, *refs), out_shape=...  18.1 us
    pallas_call x1, Pallas kernels, widen_all(): pl.pallas_call(lambda *refs: widen_kernel(sizes, cuts, *refs), out_shape=...  8.67 us

profile of v6, /device:TPU:1, one launch (start us, length us, event | category | flops | bytes accessed | tf_op | source)
XLA Modules:
  0.0 267.5 jit_solution(6773806986461667298)
XLA Ops:
  0.6 77.6 %shard_map.254 = (bf16[4,192,256]{2,1,0:T(8,128)(2,1)}, f32[2,1,4608]{2,1,0:T(1,128)}, bf16[576,768]{1,0:T(8,128)(2,1)}, f32[4,3,1,256]{3,2,1,0:T(1,128)}, f32[4...) custom-call(bf16[256,768]{1,0:T(8,128)(2,1)} %bitcast.4, ...), custom_call_target="tpu_custom_call" | custom-call | tf_op jit(solution)/shard_map/pallas_call | solution.py:389
  78.3 18.1 %shard_map.255 = (bf16[256,768]{1,0:T(8,128)(2,1)}, bf16[4,192,256]{2,1,0:T(8,128)(2,1)}, f32[256,768]{1,0:T(8,128)}, f32[2,1,4608]{2,1,0:T(1,128)}, bf16[2,6,2,...) custom-call(bf16[4,192,256]{2,1,0:T(8,128)(2,1)} %get-tuple-element., ...), custom_call_target="tpu_custom_call" | custom-call | tf_op jit(solution)/shard_map/pallas_call | solution.py:553
  96.4 162.2 %shard_map.256 = (bf16[256,768]{1,0:T(8,128)(2,1)}, bf16[1536,768]{1,0:T(8,128)(2,1)}, bf16[384,3072]{1,0:T(8,128)(2,1)}, bf16[384,768]{1,0:T(8,128)(2,1)}, bf16...) custom-call(bf16[4,192,256]{2,1,0:T(8,128)(2,1)} %get-tuple-element.59.refs_0_, f32[4,3,1,256]{3,2,1,0:T(1,128)} %get-tuple-element.60.refs_1_, ...), custom_call_target="tpu_custom_call" | custom-call | tf_op jit(solution)/shard_map/pallas_call | solution.py:1226
  258.6 8.7 %shard_map.257 = (f32[1536,768]{1,0:T(8,128)}, f32[384,3072]{1,0:T(8,128)}, f32[384,768]{1,0:T(8,128)}, f32[384,2304]{1,0:T(8,128)}, bf16[256,768]{1,0:T(8,128)(...) custom-call(f32[1,4608]{1,0:T(1,128)} %get-tuple-element.73.refs_0_,, ...), custom_call_target="tpu_custom_call" | custom-call | tf_op jit(solution)/shard_map/pallas_call | solution.py:1300

commit v7 on v6

--- a/solution.py
+++ b/solution.py
@@ -81,13 +81,13 @@
 
 def forward_kernel(ring, shards, parts, sizes, *refs):
     n_vec = len(sizes)
-    x_ref, w_ref, docs_ref = refs[:3]
+    x_ref, w_in, docs_ref = refs[:3]
     vec_refs, own = refs[3 : 3 + n_vec], refs[3 + n_vec : 6 + n_vec]
     outs, rest = refs[6 + n_vec : 19 + n_vec], refs[19 + n_vec :]
     att_ref, flat_ref, wg_ref, lse_ref, o_out, q_out, k_out, kt_out, vt_out, xr_out = outs[:10]
     full = outs[10:]
     (
-        xa_ref, wl_ref, low_ref, bias_ref, o_ref, q_ref, k_ref, kt_ref, vt_ref, top_ref, sum_ref,
+        w_ref, xa_ref, wl_ref, low_ref, bias_ref, o_ref, q_ref, k_ref, kt_ref, vt_ref, top_ref, sum_ref,
         send, recv, wsend, wrecv, fsend, frecv, vsend, vrecv, asend, arecv, osem,
     ) = rest
     net = Links(ring, shards)
@@ -96,6 +96,8 @@
     g, m = r // members, lax.rem(r, members)
     sib, yn, line, others = net.sib, net.yn, net.line, net.others
     above, below = z < levels - 1, z > 0
+    fetch = pltpu.make_async_copy(w_in, w_ref, osem.at[5 + GROUPS])
+    fetch.start()
     hello(net.partners())
 
     halves = 2
@@ -114,6 +116,7 @@
     xa_ref[r] = x_ref[...]
 
     width = x_ref.shape[1]
+    fetch.wait()
     for k in range(GROUPS):
 
         @pl.when(g == k)
@@ -394,16 +397,17 @@
             shape(t, BF16), shape(t, BF16), shape((GROUPS,) + x.shape, BF16),
         )
         + tuple(shape((shards,) + w.shape, w.dtype) for w in weights),
-        in_specs=[VMEM_SPEC] * (3 + len(vectors)) + [ANY_SPEC] * 3,
+        in_specs=[VMEM_SPEC, ANY_SPEC] + [VMEM_SPEC] * (1 + len(vectors)) + [ANY_SPEC] * 3,
         out_specs=(VMEM_SPEC,) * 4 + (ANY_SPEC,) * 9,
         scratch_shapes=[
+            vmem(qkv_weight.shape, BF16),
             vmem((ring,) + x.shape, BF16), vmem((shards, width // shards, 3 * SLAB), BF16),
             vmem(o, BF16), vmem((2 * SLAB, 1), F32), vmem(o, F32), vmem(q, BF16), vmem(k, BF16),
             vmem(t, BF16), vmem(t, BF16),
             vmem((GROUPS, PER, 1, BLOCK), F32), vmem((GROUPS, PER, 1, BLOCK), F32),
             dma((4, ring, 2)), dma((ring, 2)), dma((n, per)), dma((n, per)), dma((n, per, 3)),
             dma((n, per, 3)), dma((per,)), dma((per,)),
-            dma((GROUPS,)), dma((GROUPS,)), dma((5 + GROUPS,)),
+            dma((GROUPS,)), dma((GROUPS,)), dma((6 + GROUPS,)),
         ],
         compiler_params=pltpu.CompilerParams(
             collective_id=ident, has_side_effects=True, vmem_limit_bytes=VMEM_LIMIT
@@ -857,21 +861,21 @@
 
 def tail_kernel(ring, shards, specs, chunk_shapes, n0, *refs):
     (
-        go_ref, lse_ref, w_ref, mid_ref, small_ref, q_in, k_in, kt_in, vt_in, o_in, xr_in,
+        go_ref, lse_ref, w_in, mid_in, small_ref, q_in, k_in, kt_in, vt_in, o_in, xr_in,
     ) = refs[:11]
     n_terms = len(chunk_shapes)
     terms, refs = refs[11 : 11 + n_terms], refs[11 + n_terms :]
     out_ref, outs, (qkv_ref, total_small) = refs[0], refs[1 : 1 + n_terms], refs[1 + n_terms : 3 + n_terms]
     (
-        q_ref, k_ref, kt_ref, vt_ref, o_ref,
+        w_ref, mid_ref, q_ref, k_ref, kt_ref, vt_ref, o_ref,
         g_ref, x_ref, v_ref, delta_ref, acc_ref, dk_ref, dv_ref, pq_ref, stage_ref, got_ref, got2_ref,
         dw_ref, dx_ref, near_ref, far_ref, db_ref, dwl_ref, row_ref, sum_ref, all_ref,
         gsend, grecv, ksend, krecv, xsend, xrecv, lsem,
-    ) = refs[3 + n_terms : 35 + n_terms]
-    finals, rest = outs, refs[35 + n_terms :]
+    ) = refs[3 + n_terms : 37 + n_terms]
+    finals, rest = outs, refs[37 + n_terms :]
     outs, rest = rest[:n_terms], rest[n_terms:]
     copies = [
-        pltpu.make_async_copy(src, dst, lsem.at[6 + n])
+        pltpu.make_async_copy(src, dst, lsem.at[8 + n])
         for n, (src, dst) in enumerate(zip(outs, finals))
     ]
     net = Links(ring, shards)
@@ -901,7 +905,7 @@
         pltpu.make_async_copy(src, dst, lsem.at[n])
         for n, (src, dst) in enumerate(
             ((vt_in, vt_ref), (k_in, k_ref), (q_in, q_ref), (kt_in, kt_ref), (o_in, o_ref),
-             (xr_in, x_ref))
+             (xr_in, x_ref), (w_in, w_ref), (mid_in, mid_ref))
         )
     ]
     for load in loads:
@@ -922,7 +926,7 @@
     drains.append(drain)
     ticks = spread_out(jobs, offsets(levels))
 
-    width = w_ref.shape[1]
+    width = w_in.shape[1]
 
     def prepare():
         dwl_ref[...] = dw_ref[...].astype(BF16).reshape(dwl_ref.shape)
@@ -1226,9 +1230,10 @@
     result = pl.pallas_call(
         lambda *refs: tail_kernel(ring, shards, specs, chunk_shapes, n0, *refs),
         out_shape=(shape((BLOCK, width), BF16), *out_shape, shape((1, small.shape[2]), F32)),
-        in_specs=[VMEM_SPEC] * 5 + [ANY_SPEC] * (6 + len(terms)),
+        in_specs=[VMEM_SPEC] * 2 + [ANY_SPEC] * 2 + [VMEM_SPEC] + [ANY_SPEC] * (6 + len(terms)),
         out_specs=(VMEM_SPEC,) + (ANY_SPEC,) * len(terms) + (VMEM_SPEC,) * 2,
         scratch_shapes=[
+            vmem(w_group.shape, BF16), vmem(mid.shape, F32),
             vmem((GROUPS, PER, 2 * HEAD_DIM, BLOCK), BF16),
             vmem((PER, ring * BLOCK, 2 * HEAD_DIM), BF16),
             vmem(tall, BF16), vmem(tall, BF16), vmem(slab, F32),
@@ -1252,7 +1257,7 @@
             vmem(buffer, BF16),
             dma((GROUPS,)), dma((GROUPS,)),
             dma((GROUPS, members // 2)), dma((GROUPS, members // 2)),
-            dma((GROUPS, 4)), dma((GROUPS, 2, 4)), dma((9,)),
+            dma((GROUPS, 4)), dma((GROUPS, 2, 4)), dma((11,)),
             *(vmem(o.shape, BF16) for o in out_shape[: len(terms)]),
             *scratch,
         ],

time: 268 us -> 266 us (level)
  no operation moved by 1% of the time
where the time goes in v7:
time: 266 us
  Pallas kernels  265 us (100%)
    pallas_call x1, Pallas kernels, tail_all(): pl.pallas_call(lambda *refs: tail_kernel(ring, shards, specs, chunk_shape...  161 us
    pallas_call x1, Pallas kernels, forward_all(): pl.pallas_call(lambda *refs: forward_kernel(ring, shards, parts, sizes, *...  77.1 us
    pallas_call x1, Pallas kernels, mlp_all(): pl.pallas_call(lambda *refs: mlp_kernel(shards, sizes, *refs), out_shape=...  18.1 us
    pallas_call x1, Pallas kernels, widen_all(): pl.pallas_call(lambda *refs: widen_kernel(sizes, cuts, *refs), out_shape=...  8.67 us

profile of v7, /device:TPU:1, one launch (start us, length us, event | category | flops | bytes accessed | tf_op | source)
XLA Modules:
  0.0 265.6 jit_solution(7557704031131844706)
XLA Ops:
  0.6 77.1 %shard_map.254 = (bf16[4,192,256]{2,1,0:T(8,128)(2,1)}, f32[2,1,4608]{2,1,0:T(1,128)}, bf16[576,768]{1,0:T(8,128)(2,1)}, f32[4,3,1,256]{3,2,1,0:T(1,128)}, f32[4...) custom-call(bf16[256,768]{1,0:T(8,128)(2,1)} %bitcast.4, ...), custom_call_target="tpu_custom_call" | custom-call | tf_op jit(solution)/shard_map/pallas_call | solution.py:392
  77.7 18.1 %shard_map.255 = (bf16[256,768]{1,0:T(8,128)(2,1)}, bf16[4,192,256]{2,1,0:T(8,128)(2,1)}, f32[256,768]{1,0:T(8,128)}, f32[2,1,4608]{2,1,0:T(1,128)}, bf16[2,6,2,...) custom-call(bf16[4,192,256]{2,1,0:T(8,128)(2,1)} %get-tuple-element., ...), custom_call_target="tpu_custom_call" | custom-call | tf_op jit(solution)/shard_map/pallas_call | solution.py:557
  95.9 160.9 %shard_map.256 = (bf16[256,768]{1,0:T(8,128)(2,1)}, bf16[1536,768]{1,0:T(8,128)(2,1)}, bf16[384,3072]{1,0:T(8,128)(2,1)}, bf16[384,768]{1,0:T(8,128)(2,1)}, bf16...) custom-call(bf16[4,192,256]{2,1,0:T(8,128)(2,1)} %get-tuple-element.59.refs_0_, f32[4,3,1,256]{3,2,1,0:T(1,128)} %get-tuple-element.60.refs_1_, ...), custom_call_target="tpu_custom_call" | custom-call | tf_op jit(solution)/shard_map/pallas_call | solution.py:1230
  256.8 8.7 %shard_map.257 = (f32[1536,768]{1,0:T(8,128)}, f32[384,3072]{1,0:T(8,128)}, f32[384,768]{1,0:T(8,128)}, f32[384,2304]{1,0:T(8,128)}, bf16[256,768]{1,0:T(8,128)(...) custom-call(f32[1,4608]{1,0:T(1,128)} %get-tuple-element.73.refs_0_,, ...), custom_call_target="tpu_custom_call" | custom-call | tf_op jit(solution)/shard_map/pallas_call | solution.py:1305
